TPU v7x, 32 devices: a whole 2x2x4 slice. The times are simulated.
32 devices in a mesh: gx: 8 (over y, x, core), gy: 4 (over z).
Axes of the slice: x: 2, y: 2, z: 4, core: 2. Of those that a mesh axis runs over, the one named last changes fastest.
Arguments:
- features: bfloat16 [128, 64, 8, 64], P('gx', 'gy'), may hold values from -6 to 6
- cotangent: bfloat16 [128, 64, 8, 64], P('gx', 'gy'), may hold values from -6 to 6
- spectral_weight: bfloat16 [32, 32, 4, 2, 64, 64], P('gx', 'gy'), may hold values from -0.75 to 0.75
- conv_weight: bfloat16 [64, 64], replicated, may hold values from -0.75 to 0.75
- modes_x: int32 [32], replicated, may hold values from 0 to 127, as said below
- modes_y: int32 [32], replicated, may hold values from 0 to 63, as said below
- modes_z: int32 [4], replicated, may hold values from 0 to 7, as said below
Outputs:
- activation: bfloat16 [128, 64, 8, 64], P('gx', 'gy')
- grad_features: bfloat16 [128, 64, 8, 64], P('gx', 'gy')
- grad_spectral: float32 [32, 32, 4, 2, 64, 64], P('gx', 'gy')
- grad_conv: float32 [64, 64], replicated
Inputs may be any that keep to these rules, and one draw needn't show every extreme that they name: `modes_x`: 32 distinct frequencies. `modes_y`: 32 distinct frequencies. `modes_z`: 4 distinct frequencies.
All inputs are finite; a program needn't handle non-finite values.
Results may differ from a plain program's by a relative error of at most 0.0049.
Values may be sent and summed in bfloat16 or wider, within the bound.
No kernel may reach another device: no remote copies, remote signals or barrier semaphores. Data moves between devices by JAX's collectives and lax.ppermute only.
A program may use at most 64 MiB of HBM per device.

v0:
```python
import math

import jax
import jax.numpy as jnp
from jax import lax
from jax.sharding import PartitionSpec as P

HIGH = lax.Precision.HIGHEST


def phase_tables(freqs, places, length):
    product = freqs[:, None] * places[None, :] % length
    angles = product.astype(jnp.float32) * (2.0 * math.pi / length)
    return (jnp.cos(angles), jnp.sin(angles))


def plane_modes(values, factor, modes_z):
    size_x, size_y, size_z, chans = values.shape
    cos_z, sin_z = phase_tables(modes_z, jnp.arange(size_z, dtype=jnp.int32), size_z)
    wide = values.astype(jnp.float32)
    plane_real = (factor * jnp.einsum("xyzc,kz->xykc", wide, cos_z, precision=HIGH)).reshape(
        size_x, size_y, -1
    )
    plane_imag = (-factor * jnp.einsum("xyzc,kz->xykc", wide, sin_z, precision=HIGH)).reshape(
        size_x, size_y, -1
    )
    return (plane_real, plane_imag)


def line_modes(plane_real, plane_imag, freqs, places, length):
    cos_x, sin_x = phase_tables(freqs, places, length)
    line_real = jnp.einsum("kx,xyq->kyq", cos_x, plane_real, precision=HIGH) + jnp.einsum(
        "kx,xyq->kyq", sin_x, plane_imag, precision=HIGH
    )
    line_imag = jnp.einsum("kx,xyq->kyq", cos_x, plane_imag, precision=HIGH) - jnp.einsum(
        "kx,xyq->kyq", sin_x, plane_real, precision=HIGH
    )
    return jnp.stack([line_real, line_imag], axis=1)


def to_modes(values, factor, modes_x, modes_y, modes_z):
    rows_x, rows_y = (values.shape[0], values.shape[1])
    parts_x = lax.axis_size("gx")
    parts_y = lax.axis_size("gy")
    length_x = rows_x * parts_x
    length_y = rows_y * parts_y
    pencil = lax.all_to_all(values, "gx", split_axis=1, concat_axis=0, tiled=True)
    plane_real, plane_imag = plane_modes(pencil, factor, modes_z)
    whole = line_modes(
        plane_real, plane_imag, modes_x, jnp.arange(length_x, dtype=jnp.int32), length_x
    )
    spectrum = lax.all_to_all(whole, "gx", split_axis=0, concat_axis=2, tiled=True)
    places_y = lax.axis_index("gy") * rows_y + jnp.arange(rows_y, dtype=jnp.int32)
    cos_y, sin_y = phase_tables(modes_y, places_y, length_y)
    mode_real = jnp.einsum("ly,kyq->lkq", cos_y, spectrum[:, 0], precision=HIGH) + jnp.einsum(
        "ly,kyq->lkq", sin_y, spectrum[:, 1], precision=HIGH
    )
    mode_imag = jnp.einsum("ly,kyq->lkq", cos_y, spectrum[:, 1], precision=HIGH) - jnp.einsum(
        "ly,kyq->lkq", sin_y, spectrum[:, 0], precision=HIGH
    )
    return lax.psum_scatter(
        jnp.stack([mode_real, mode_imag], axis=2), "gy", scatter_dimension=0, tiled=True
    )


def to_cells(spectrum, factor, rows_x, rows_y, size_z, modes_x, modes_y, modes_z):
    length_x = rows_x * lax.axis_size("gx")
    length_y = rows_y * lax.axis_size("gy")
    places_y = lax.axis_index("gy") * rows_y + jnp.arange(rows_y, dtype=jnp.int32)
    places_x = lax.axis_index("gx") * rows_x + jnp.arange(rows_x, dtype=jnp.int32)
    piece = lax.all_gather(spectrum, "gy", axis=0, tiled=True)
    freqs = modes_y
    cos_y, sin_y = phase_tables(freqs, places_y, length_y)
    line_real = jnp.einsum("ly,lkq->kyq", cos_y, piece[:, :, 0], precision=HIGH) - jnp.einsum(
        "ly,lkq->kyq", sin_y, piece[:, :, 1], precision=HIGH
    )
    line_imag = jnp.einsum("ly,lkq->kyq", cos_y, piece[:, :, 1], precision=HIGH) + jnp.einsum(
        "ly,lkq->kyq", sin_y, piece[:, :, 0], precision=HIGH
    )
    line_real, line_imag = (line_real, line_imag)
    lines = jnp.stack([line_real, line_imag], axis=1)
    piece = lax.all_gather(lines, "gx", axis=0, tiled=True)
    freqs = modes_x
    cos_x, sin_x = phase_tables(freqs, places_x, length_x)
    plane_real = jnp.einsum("kx,kyq->xyq", cos_x, piece[:, 0], precision=HIGH) - jnp.einsum(
        "kx,kyq->xyq", sin_x, piece[:, 1], precision=HIGH
    )
    plane_imag = jnp.einsum("kx,kyq->xyq", cos_x, piece[:, 1], precision=HIGH) + jnp.einsum(
        "kx,kyq->xyq", sin_x, piece[:, 0], precision=HIGH
    )
    plane_real, plane_imag = (plane_real, plane_imag)
    count_z = modes_z.shape[0]
    plane_real = plane_real.reshape(rows_x, rows_y, count_z, -1)
    plane_imag = plane_imag.reshape(rows_x, rows_y, count_z, -1)
    cos_z, sin_z = phase_tables(modes_z, jnp.arange(size_z, dtype=jnp.int32), size_z)
    return factor * (
        jnp.einsum("xykc,kz->xyzc", plane_real, cos_z, precision=HIGH)
        - jnp.einsum("xykc,kz->xyzc", plane_imag, sin_z, precision=HIGH)
    )


def normal_cdf(values):
    return 0.5 * (1.0 + jax.scipy.special.erf(values * (1.0 / math.sqrt(2.0))))


def normal_pdf(values):
    return jnp.exp(-0.5 * values * values) * (1.0 / math.sqrt(2.0 * math.pi))


def shards(features, cotangent, spectral_weight, conv_weight, modes_x, modes_y, modes_z):
    rows_x, rows_y, size_z, chans = features.shape
    count_x, count_y, count_z = (modes_x.shape[0], modes_y.shape[0], modes_z.shape[0])
    length_x = rows_x * lax.axis_size("gx")
    length_y = rows_y * lax.axis_size("gy")
    first = 1.0 / math.sqrt(length_x * length_y * size_z)
    second = 1.0 / math.sqrt(count_x * count_y * count_z)
    spectrum = to_modes(features, first, modes_x, modes_y, modes_z)
    local_y, local_x = (spectrum.shape[0], spectrum.shape[1])
    spec_real = spectrum[:, :, 0].reshape(local_y, local_x, count_z, chans)
    spec_imag = spectrum[:, :, 1].reshape(local_y, local_x, count_z, chans)
    weight = spectral_weight.astype(jnp.float32)
    real_w = weight[:, :, :, 0]
    imag_w = weight[:, :, :, 1]
    form = "abzoi,bazi->bazo"
    mixed_real = jnp.einsum(form, real_w, spec_real, precision=HIGH) - jnp.einsum(
        form, imag_w, spec_imag, precision=HIGH
    )
    mixed_imag = jnp.einsum(form, real_w, spec_imag, precision=HIGH) + jnp.einsum(
        form, imag_w, spec_real, precision=HIGH
    )
    mixed = jnp.stack(
        [mixed_real.reshape(local_y, local_x, -1), mixed_imag.reshape(local_y, local_x, -1)], axis=2
    )
    spectral = to_cells(mixed, second, rows_x, rows_y, size_z, modes_x, modes_y, modes_z)
    flat = features.reshape(-1, chans)
    conv = jnp.dot(flat, conv_weight, preferred_element_type=jnp.float32).reshape(spectral.shape)
    pre = spectral + conv
    cdf = normal_cdf(pre)
    activation = (pre * cdf).astype(jnp.bfloat16)
    slope = (cotangent.astype(jnp.float32) * (cdf + pre * normal_pdf(pre))).astype(jnp.bfloat16)
    back = to_modes(slope, second, modes_x, modes_y, modes_z)
    back_real = back[:, :, 0].reshape(local_y, local_x, count_z, chans)
    back_imag = back[:, :, 1].reshape(local_y, local_x, count_z, chans)
    outer = "bazo,bazi->abzoi"
    grad_real = jnp.einsum(outer, back_real, spec_real, precision=HIGH) + jnp.einsum(
        outer, back_imag, spec_imag, precision=HIGH
    )
    grad_imag = jnp.einsum(outer, back_imag, spec_real, precision=HIGH) - jnp.einsum(
        outer, back_real, spec_imag, precision=HIGH
    )
    grad_spectral = jnp.stack([grad_real, grad_imag], axis=3)
    adjoint = "abzoi,bazo->bazi"
    modes_real = jnp.einsum(adjoint, real_w, back_real, precision=HIGH) + jnp.einsum(
        adjoint, imag_w, back_imag, precision=HIGH
    )
    modes_imag = jnp.einsum(adjoint, real_w, back_imag, precision=HIGH) - jnp.einsum(
        adjoint, imag_w, back_real, precision=HIGH
    )
    back_modes = jnp.stack(
        [modes_real.reshape(local_y, local_x, -1), modes_imag.reshape(local_y, local_x, -1)], axis=2
    )
    spectral_back = to_cells(back_modes, first, rows_x, rows_y, size_z, modes_x, modes_y, modes_z)
    slope_flat = slope.reshape(-1, chans)
    conv_back = jnp.dot(slope_flat, conv_weight.T, preferred_element_type=jnp.float32).reshape(
        spectral.shape
    )
    grad_features = (spectral_back + conv_back).astype(jnp.bfloat16)
    local_conv = jnp.dot(flat.T, slope_flat, preferred_element_type=jnp.float32)
    grad_conv = first * lax.psum(local_conv, ("gx", "gy"))
    return (activation, grad_features, grad_spectral, grad_conv)


def solution(mesh):
    placed = (
        P("gx", "gy", None, None),
        P("gx", "gy", None, None),
        P("gx", "gy", None, None, None, None),
        P(),
        P(),
        P(),
        P(),
    )
    return jax.shard_map(
        shards,
        mesh=mesh,
        in_specs=placed,
        out_specs=(
            P("gx", "gy", None, None),
            P("gx", "gy", None, None),
            P("gx", "gy", None, None, None, None),
            P(),
        ),
        check_vma=False,
    )
```

profile of v0, /device:TPU:0, one launch (start us, length us, event | category | flops | bytes accessed | tf_op | source)
XLA Modules:
  0.0 253.0 jit_solution(12627175154982899695)
XLA Ops:
  8.8 11.9 %all_to_all.72 = bf16[8,2,8192]{2,1,0:T(2,128)(2,1)S(1)} all-to-all(bf16[8,2,8192]{2,1,0:T(2,128)(2,1)S(1)} %reshape.85), channel_id=1, replica_groups=mesh['gx'=8,'gy'=4] {'gx'}, dimensions={0} | all-to-all | bytes 524288 | tf_op jit(solution)/shard_map/all_to_all | solution.py:47
  25.4 3.4 %all-to-all-start.1 = ((f32[32,2,2,256]{3,2,1,0:T(2,128)}), f32[32,2,2,256]{3,2,1,0:T(2,128)S(1)}, u32[]{:S(2)}, u32[]{:S(2)}) async-start(f32[32,2,2,256]{3,2,1,0:T(2,128)} %copy.85), calls=%async_computation.1 | async-start | bytes 262144 | tf_op jit(solution)/shard_map/all_to_all | solution.py:52
  28.8 5.4 %all-to-all-done.1 = f32[32,2,2,256]{3,2,1,0:T(2,128)S(1)} async-done(((f32[32,2,2,256]{3,2,1,0:T(2,128)}), f32[32,2,2,256]{3,2,1,0:T(2,128)S(1)}, u32[]{:S(2)}, u32[]{:S(2)}) %all-to-all-start.1) | async-done | bytes 131104 | tf_op jit(solution)/shard_map/all_to_all | solution.py:52
  37.5 5.0 %slice_bitcast_fusion.1 = (bf16[4,8,4,64,64]{4,3,2,1,0:T(8,128)(2,1)S(1)}, bf16[4,8,4,64,64]{4,3,2,1,0:T(8,128)(2,1)}) fusion(bf16[4,8,4,2,64,64]{5,4,3,2,1,0:T(8,128)(2,1)} %param.9), kind=kLoop, calls=%fused_computation.4 | loop fusion | bytes 4194304 | tf_op jit(solution)/shard_map/squeeze | solution.py:122
  42.4 13.6 %reduce-scatter.3.cloned.1.call-done = f32[8,4,2,256]{3,0,1,2:T(8,128)} async-done(((f32[32,4,2,256]{3,0,1,2:T(8,128)}), f32[8,4,2,256]{3,0,1,2:T(8,128)}) %reduce-scatter.3.cloned.1.call-update) | async-done | bytes 65552 | tf_op jit(solution)/shard_map/reduce_scatter | solution.py:61
  57.0 3.3 %fusion.18 = f32[8,4,4,1,64]{4,3,2,1,0:T(1,128)S(1)} fusion(bf16[4,8,4,64,64]{4,3,2,1,0:T(8,128)(2,1)S(1)} %get-tuple-element.16, f32[8,4,4,64,1]{3,2,0,1,4:T(4,128)S(1)} %reshape.67), kind=kOutput, calls=%fused_computation.26 | convolution fusion | flops 6291456 | bytes 1114112 | tf_op jit(solution)/shard_map/abzoi,bazi->bazo/dot_general | solution.py:128
  60.4 3.4 %fusion.12 = f32[8,4,4,1,64]{4,3,2,1,0:T(1,128)S(1)} fusion(bf16[4,8,4,64,64]{4,3,2,1,0:T(8,128)(2,1)S(1)} %copy-done.4, f32[8,4,4,64,1]{3,2,0,1,4:T(4,128)S(1)} %reshape.67), kind=kOutput, calls=%fused_computation.20 | convolution fusion | flops 6291456 | bytes 1114112 | tf_op jit(solution)/shard_map/abzoi,bazi->bazo/dot_general | solution.py:125
  63.7 3.4 %fusion.20 = f32[8,4,4,1,64]{4,3,2,1,0:T(1,128)S(1)} fusion(bf16[4,8,4,64,64]{4,3,2,1,0:T(8,128)(2,1)S(1)} %get-tuple-element.16, f32[8,4,4,64,1]{3,2,0,1,4:T(4,128)S(1)} %reshape.65), kind=kOutput, calls=%fused_computation.28 | convolution fusion | flops 6291456 | bytes 1114112 | tf_op jit(solution)/shard_map/abzoi,bazi->bazo/dot_general | solution.py:125
  67.1 3.4 %fusion.10 = f32[8,4,4,1,64]{4,3,2,1,0:T(1,128)S(1)} fusion(bf16[4,8,4,64,64]{4,3,2,1,0:T(8,128)(2,1)S(1)} %copy-done.4, f32[8,4,4,64,1]{3,2,0,1,4:T(4,128)S(1)} %reshape.65), kind=kOutput, calls=%fused_computation.18 | convolution fusion | flops 6291456 | bytes 1114112 | tf_op jit(solution)/shard_map/abzoi,bazi->bazo/dot_general | solution.py:128
  70.7 13.8 %all_gather.12 = f32[32,4,2,256]{3,0,1,2:T(8,128)S(1)} all-gather(f32[8,4,2,256]{3,0,1,2:T(8,128)S(1)} %pad_maximum_fusion.7), channel_id=1, replica_groups=mesh['gx'=8,'gy'=4] {'gy'}, dimensions={0}, use_global_device_ids=true | all-gather | bytes 327680 | tf_op jit(solution)/shard_map/all_gather | solution.py:71
  87.0 21.7 %all-gather.3.cloned.1.call-done = f32[32,2,16,256]{3,2,0,1:T(8,128)} async-done(((f32[4,2,16,256]{3,2,0,1:T(8,128)}), f32[32,2,16,256]{3,2,0,1:T(8,128)}) %all-gather.3.cloned.1.call-update) | async-done | bytes 1048592 | tf_op jit(solution)/shard_map/all_gather | solution.py:82
  114.8 3.7 %fusion.44 = (bf16[16,16,8,64]{3,2,1,0:T(8,128)(2,1)S(1)}, bf16[16,16,8,64]{3,2,1,0:T(8,128)(2,1)}) fusion(bf16[16,16,8,64]{3,2,1,0:T(8,128)(2,1)} %param.8, f32[16,16,8,64]{3,2,1,0:T(8,128)S(1)} %fusion.84, f32[8,16,16,64]{3,0,2,1:T(8,128)S(1)} %fusion.49, f32[16,16,4,64]{3,2,0,1:T(4,128)S(1)} %reshape.54, s32[4]{0:T(128)S(1)} %copy-done.7), kind=kOutput, calls=%fused_computation.73 | convolution fusion | flops 8389056 | bytes 2097168 | tf_op jit(solution)/shard_map/xykc,kz->xyzc/dot_general | solution.py:98
  119.0 9.5 %all_to_all.73 = bf16[8,2,8192]{2,1,0:T(2,128)(2,1)S(1)} all-to-all(bf16[8,2,8192]{2,1,0:T(2,128)(2,1)S(1)} %reshape.87), channel_id=1, replica_groups=mesh['gx'=8,'gy'=4] {'gx'}, dimensions={0} | all-to-all | bytes 524288 | tf_op jit(solution)/shard_map/all_to_all | solution.py:47
  132.5 7.9 %all_to_all.74 = f32[32,2,2,256]{3,2,1,0:T(2,128)S(1)} all-to-all(f32[32,2,2,256]{3,2,1,0:T(2,128)S(1)} %copy.105), channel_id=1, replica_groups=mesh['gx'=8,'gy'=4] {'gx'}, dimensions={0} | all-to-all | bytes 262144 | tf_op jit(solution)/shard_map/all_to_all | solution.py:52
  143.3 18.6 %reduce-scatter.5.cloned.1.call-done = f32[8,4,2,256]{3,0,1,2:T(8,128)} async-done(((f32[32,4,2,256]{3,0,1,2:T(8,128)}), f32[8,4,2,256]{3,0,1,2:T(8,128)}) %reduce-scatter.5.cloned.1.call-update) | async-done | bytes 65552 | tf_op jit(solution)/shard_map/reduce_scatter | solution.py:61
  162.8 3.3 %fusion.8 = f32[8,4,4,1,64]{4,3,2,1,0:T(1,128)S(1)} fusion(bf16[4,8,4,64,64]{4,3,2,1,0:T(8,128)(2,1)} %get-tuple-element.17, f32[8,4,4,64,1]{3,2,0,1,4:T(4,128)S(1)} %reshape.76), kind=kOutput, calls=%fused_computation.16 | convolution fusion | flops 6291456 | bytes 1114112 | tf_op jit(solution)/shard_map/abzoi,bazo->bazi/dot_general | solution.py:153
  166.2 1.7 fusion.14
  168.0 3.3 %fusion.6 = f32[8,4,4,1,64]{4,3,2,1,0:T(1,128)S(1)} fusion(bf16[4,8,4,64,64]{4,3,2,1,0:T(8,128)(2,1)} %get-tuple-element.17, f32[8,4,4,64,1]{3,2,0,1,4:T(4,128)S(1)} %reshape.74), kind=kOutput, calls=%fused_computation.14 | convolution fusion | flops 6291456 | bytes 1114112 | tf_op jit(solution)/shard_map/abzoi,bazo->bazi/dot_general | solution.py:156
  171.3 2.4 fusion.16
  174.8 13.9 %all_gather.14 = f32[32,4,2,256]{3,0,1,2:T(8,128)S(1)} all-gather(f32[8,4,2,256]{3,0,1,2:T(8,128)S(1)} %pad_maximum_fusion.8), channel_id=1, replica_groups=mesh['gx'=8,'gy'=4] {'gy'}, dimensions={0}, use_global_device_ids=true | all-gather | bytes 327680 | tf_op jit(solution)/shard_map/all_gather | solution.py:71
  191.1 38.9 %psum.7 = f32[64,64]{0,1:T(8,128)S(1)} all-reduce(f32[64,64]{0,1:T(8,128)S(1)} %convolution_bitcast_fusion), channel_id=1, replica_groups=mesh['gx'=8,'gy'=4] {'gx','gy'}, use_global_device_ids=true, to_apply=%region_2.3 | all-reduce | flops 4096 | bytes 32768 | tf_op jit(solution)/shard_map/psum | solution.py:169
  231.3 2.3 add_bitcast_fusion
  233.6 4.4 %pad_maximum_fusion = f32[4,8,4,2,64,64]{5,4,3,2,1,0:T(8,128)} fusion(f32[4,8,4,1,64,64]{5,4,3,2,1,0:T(8,128)S(1)} %get-tuple-element.25, f32[4,8,4,1,64,64]{5,4,3,2,1,0:T(8,128)S(1)} %get-tuple-element.24), kind=kLoop, calls=%fused_computation | loop fusion | flops 1048576 | bytes 8388608 | tf_op jit(solution)/shard_map/stack | solution.py:151
  244.0 2.2 fusion.22
  (122 shorter events, 37.9 us)
Async XLA Ops:
  7.2 79.6 %copy-start = (bf16[64,64]{1,0:T(8,128)(2,1)S(1)}, bf16[64,64]{1,0:T(8,128)(2,1)}, u32[]{:S(2)}) copy-start(bf16[64,64]{1,0:T(8,128)(2,1)} %param.10) | copy-start | bytes 24580
  8.4 13.3 %copy-start.7 = (s32[4]{0:T(128)S(1)}, s32[4]{0:T(128)}, u32[]{:S(2)}) copy-start(s32[4]{0:T(128)} %param.13) | copy-start | bytes 52
  21.0 1.7 copy-start.5
  22.1 12.2 %copy-start.6 = (s32[32]{0:T(128)S(1)}, s32[32]{0:T(128)}, u32[]{:S(2)}) copy-start(s32[32]{0:T(128)} %param.12) | copy-start | bytes 388
  25.4 8.8 %all-to-all-start.1 = ((f32[32,2,2,256]{3,2,1,0:T(2,128)}), f32[32,2,2,256]{3,2,1,0:T(2,128)S(1)}, u32[]{:S(2)}, u32[]{:S(2)}) async-start(f32[32,2,2,256]{3,2,1,0:T(2,128)} %copy.85), calls=%async_computation.1 | async-start | bytes 262144 | tf_op jit(solution)/shard_map/all_to_all | solution.py:52
  28.8 27.3 %reduce-scatter.3.cloned.1.call-start = ((), (), s32[]{:S(2)}) async-start(), calls=%async_computation.6 | async-start | bytes 327680 | tf_op jit(solution)/shard_map/reduce_scatter | solution.py:61
  36.9 71.9 %all-gather.3.cloned.1.call-start = ((), (), s32[]{:S(2)}) async-start(), calls=%async_computation.7 | async-start | bytes 1179648 | tf_op jit(solution)/shard_map/all_gather | solution.py:82
  42.4 21.3 %copy-start.2 = (bf16[4,8,4,64,64]{4,3,2,1,0:T(8,128)(2,1)}, bf16[4,8,4,64,64]{4,3,2,1,0:T(8,128)(2,1)S(1)}, u32[]{:S(2)}) copy-start(bf16[4,8,4,64,64]{4,3,2,1,0:T(8,128)(2,1)S(1)} %get-tuple-element.16) | copy-start | bytes 3145732
  57.0 3.4 %copy-start.4 = (bf16[4,8,4,64,64]{4,3,2,1,0:T(8,128)(2,1)S(1)}, bf16[4,8,4,64,64]{4,3,2,1,0:T(8,128)(2,1)}, u32[]{:S(2)}) copy-start(bf16[4,8,4,64,64]{4,3,2,1,0:T(8,128)(2,1)} %get-tuple-element.17) | copy-start | bytes 3145732
  67.1 19.6 %copy-start.1 = (bf16[16,16,8,64]{3,2,1,0:T(8,128)(2,1)S(1)}, bf16[16,16,8,64]{3,2,1,0:T(8,128)(2,1)}, u32[]{:S(2)}) copy-start(bf16[16,16,8,64]{3,2,1,0:T(8,128)(2,1)} %param.7) | copy-start | bytes 786436
  86.5 75.5 %reduce-scatter.5.cloned.1.call-start = ((), (), s32[]{:S(2)}) async-start(), calls=%async_computation.8 | async-start | bytes 327680 | tf_op jit(solution)/shard_map/reduce_scatter | solution.py:61
  141.0 25.2 %copy-start.3 = (bf16[4,8,4,64,64]{4,3,2,1,0:T(8,128)(2,1)S(1)}, bf16[4,8,4,64,64]{4,3,2,1,0:T(8,128)(2,1)}, u32[]{:S(2)}) copy-start(bf16[4,8,4,64,64]{4,3,2,1,0:T(8,128)(2,1)} %copy-done.2) | copy-start | bytes 3145732
  143.1 94.9 %all-gather.5.cloned.1.call-start = ((), (), s32[]{:S(2)}) async-start(), calls=%async_computation.9 | async-start | bytes 1179648 | tf_op jit(solution)/shard_map/all_gather | solution.py:82
Sparse Core Ops, SparseCore 0:
  37.0 19.0 reduce-scatter.2
  86.6 22.0 all-gather.2
  143.2 18.7 reduce-scatter.4
  190.7 22.1 all-gather.4
where the time goes:
time: 257 us; the launch traced here: 253 us
  blocking collectives  95.9 us (37%)
  waiting for transfers between devices  59.4 us (23%)
  matrix products  51 us (20%)
  local copies, waits for them, and re-layouts  17.1 us (7%)
  between operations  14.7 us (6%)
  other arithmetic  10.5 us (4%)
  starting transfers between devices  4.45 us (2%)
    psum x1, blocking collectives, shards(): grad_conv = first * lax.psum(local_conv, ('gx', 'gy'))  38.9 us
    reduce_scatter x2, waiting for transfers between devices, to_modes(): lax.psum_scatter(jnp.stack([mode_real, mode_imag], axis=2), 'gy', scatter...  32.3 us
    all_gather x2, blocking collectives, to_cells(): piece = lax.all_gather(spectrum, 'gy', axis=0, tiled=True)  27.7 us
    all_gather x2, waiting for transfers between devices, to_cells(): piece = lax.all_gather(lines, 'gx', axis=0, tiled=True)  21.7 us
    all_to_all x2, blocking collectives, to_modes(): lax.all_to_all(values, 'gx', split_axis=1, concat_axis=0, tiled=True)  21.4 us
    all_to_all x1, blocking collectives, to_modes(): lax.all_to_all(whole, 'gx', split_axis=0, concat_axis=2, tiled=True)  7.92 us
    another operation x2, other arithmetic, shards(): grad_spectral = jnp.stack([grad_real, grad_imag], axis=3)  6.71 us
    dot_general x2, matrix products, to_cells(): jnp.einsum('xykc,kz->xyzc', plane_imag, sin_z, precision=HIGH)  5.92 us
  transfers between devices with their start and end apart: 5, of which 4 were waited for; matrix products, arithmetic and copies ran while one was open for 5% of the time, Pallas kernels for 0%

commit v1 on v0

--- a/solution.py
+++ b/solution.py
@@ -3,9 +3,530 @@
 import jax
 import jax.numpy as jnp
 from jax import lax
+from jax.experimental import pallas as pl
+from jax.experimental.pallas import tpu as pltpu
 from jax.sharding import PartitionSpec as P
 
 HIGH = lax.Precision.HIGHEST
+BF = jnp.bfloat16
+F32 = jnp.float32
+LANES = 128
+EXTRA = 16
+WIDE = 1024
+
+
+def steps_of(parts):
+    return list(range(0, parts, 2)) + list(range(1, parts, 2))
+
+
+def cosine(turns, length):
+    half = length // 2
+    place = ((turns + length // 4) & (length - 1)) - half
+    place = jnp.minimum(jnp.maximum(place, -half - place), half - place)
+    angle = place.astype(F32) * (-2.0 * math.pi / length)
+    square = angle * angle
+    series = 1.0 / 362880.0 - square * (1.0 / 39916800.0)
+    series = square * series - 1.0 / 5040.0
+    series = square * series + 1.0 / 120.0
+    series = square * series - 1.0 / 6.0
+    return angle + angle * (square * series)
+
+
+def pick(ref, index, places):
+    out = jnp.zeros(index.shape, jnp.int32)
+    for k, place in enumerate(places):
+        out = jnp.where(index == k, ref[place], out)
+    return out
+
+
+def store_halves(ref, row, value):
+    high = value.astype(BF)
+    tall = ref.shape[0] // 2
+    ref[row : row + value.shape[0]] = high
+    ref[tall + row : tall + row + value.shape[0]] = (value - high.astype(F32)).astype(BF)
+
+
+def grid_of(rows, cols):
+    return (
+        lax.broadcasted_iota(jnp.int32, (rows, cols), 0),
+        lax.broadcasted_iota(jnp.int32, (rows, cols), 1),
+    )
+
+
+def table_kernel(size_z, *refs):
+    sources, outs, places, sems = refs[:4], refs[5:11], refs[11:15], refs[15]
+    line_ref, column_ref, cback_ref, lback_ref, pair_ref, turn_ref = outs
+    copies = [
+        pltpu.make_async_copy(source, place, sems.at[k])
+        for k, (source, place) in enumerate(zip(sources, places))
+    ]
+    for copy in copies:
+        copy.start()
+    for copy in copies:
+        copy.wait()
+    mx_ref, my_ref, mz_ref, conv_ref = places
+    parts_x, parts_y = lax.axis_size("gx"), lax.axis_size("gy")
+    me_x, me_y = lax.axis_index("gx"), lax.axis_index("gy")
+    count_x, count_y, count_z = mx_ref.shape[0], my_ref.shape[0], mz_ref.shape[0]
+    local_x, local_y = count_x // parts_x, count_y // parts_y
+    chans = conv_ref.shape[0]
+    block = chans // parts_x
+    length_x = line_ref.shape[1] // size_z
+    whole = line_ref.shape[1]
+    tile = 16
+
+    row, col = grid_of(tile, whole)
+    per = tile // count_z
+    x, z = col // size_z, col % size_z
+    base = pick(mz_ref, row % count_z, range(count_z)) * z * length_x
+    x = x * size_z
+    inner = row // count_z
+    for part in range(2):
+        for start in range(0, count_x, per):
+            turns = pick(mx_ref, inner, range(start, start + per)) * x + base
+            at = part * count_x * count_z + start * count_z
+            store_halves(line_ref, at, cosine(turns + part * (whole // 4), whole))
+
+    rows_y = column_ref.shape[0] // 4 // block
+    length_y = rows_y * parts_y
+    row, col = grid_of(tile, column_ref.shape[1])
+    per = tile // block
+    wide = local_y * block
+    freq = pick(my_ref, col // (2 * wide) * local_y + col // block % local_y, range(count_y))
+    shift = col // wide % 2 * (length_y // 4)
+    same = row % block == col % block
+    inner = row // block + me_y * rows_y
+    for part in range(2):
+        for start in range(0, rows_y, per):
+            turns = freq * (inner + start) + shift - part * (length_y // 4)
+            value = jnp.where(same, cosine(turns, length_y), 0.0)
+            store_halves(column_ref, part * rows_y * block + start * block, value)
+
+    row, col = grid_of(2 * rows_y, cback_ref.shape[1])
+    places = [
+        (me_y + parts_y - step) % parts_y * local_y + k for step in range(parts_y) for k in range(local_y)
+    ]
+    freq = pick(my_ref, col // (2 * local_y) * local_y + col % local_y, places)
+    shift = (col // local_y % 2 - row // rows_y) * (length_y // 4)
+    store_halves(cback_ref, 0, cosine(freq * (row % rows_y + me_y * rows_y) + shift, length_y))
+
+    row, col = grid_of(tile, lback_ref.shape[1])
+    modes = local_x * count_z
+    kx = col // (2 * modes) * local_x + col // count_z % local_x
+    places = [(me_x ^ step) * local_x + k for step in steps_of(parts_x) for k in range(local_x)]
+    freq = pick(mx_ref, kx, places) * size_z
+    base = pick(mz_ref, col % count_z, range(count_z)) * (row % size_z) * length_x
+    base = base + col // modes % 2 * (whole // 4)
+    rows_x = length_x // parts_x
+    inner = row // size_z + me_x * rows_x
+    per = tile // size_z
+    for start in range(0, rows_x, per):
+        store_halves(lback_ref, start * size_z, cosine(freq * (inner + start) + base, whole))
+
+    conv = conv_ref[...].astype(F32)
+    none = jnp.zeros_like(conv)
+    for ref, value in ((pair_ref, conv), (turn_ref, conv.T)):
+        ref[:chans] = jnp.concatenate([value, none], axis=1).astype(BF)
+        ref[chans:] = jnp.concatenate([none, value], axis=1).astype(BF)
+
+
+def dot(a, b, dims=((1,), (0,))):
+    return lax.dot_general(a, b, (dims, ((), ())), preferred_element_type=F32)
+
+
+def pairs_of(ref):
+    size_x, size_y, size_z, chans = ref.shape
+    out = []
+    for y in range(size_y // 2):
+        low = ref[:, y, :, :].astype(F32).reshape(size_x * size_z, chans)
+        high = ref[:, y + size_y // 2, :, :].astype(F32).reshape(size_x * size_z, chans)
+        out.append(jnp.concatenate([low, high], axis=1))
+    return out
+
+
+def block_transpose(arrays, block):
+    count = len(arrays)
+    arrays = list(arrays)
+    lanes = arrays[0].shape[1]
+    index = lax.broadcasted_iota(jnp.int32, arrays[0].shape, 1) // block % count
+    step = 1
+    while step < count:
+        upper = (index & step) != 0
+        for p in range(count):
+            if p & step:
+                continue
+            a, b = arrays[p], arrays[p | step]
+            arrays[p] = jnp.where(upper, pltpu.roll(b, step * block, 1), a)
+            arrays[p | step] = jnp.where(upper, b, pltpu.roll(a, lanes - step * block, 1))
+        step *= 2
+    return arrays
+
+
+def split_rows(value):
+    high = value.astype(BF)
+    return jnp.concatenate([high, (value - high.astype(F32)).astype(BF)], axis=0)
+
+
+def normal_cdf(values):
+    return 0.5 * (1.0 + lax.erf(values * (1.0 / math.sqrt(2.0))))
+
+
+def normal_pdf(values):
+    return jnp.exp(-0.5 * values * values) * (1.0 / math.sqrt(2.0 * math.pi))
+
+
+def spread_kernel(field_ref, send_ref, pairs_ref):
+    size_x, _, size_z, chans = field_ref.shape
+    step = 4
+    for x in range(0, size_x, step):
+        rows = slice(x * size_z, (x + step) * size_z)
+        pairs = pairs_of(field_ref.at[pl.ds(x, step)])
+        for p, pair in enumerate(pairs):
+            pairs_ref[p, rows] = pair.astype(BF)
+        for b, chunk in enumerate(block_transpose(pairs, chans // len(pairs))):
+            send_ref[b, rows] = chunk.astype(BF)
+
+
+def pairs_kernel(field_ref, pairs_ref):
+    for p, pair in enumerate(pairs_of(field_ref)):
+        pairs_ref[p] = pair.astype(BF)
+
+
+def joined(value):
+    chans = value.shape[1] // 2
+    return value[:, :chans].astype(F32) + value[:, chans:].astype(F32)
+
+
+def parted(value):
+    high = value.astype(BF).astype(F32)
+    both = jnp.concatenate([high, value - high], axis=1)
+    rest = jnp.zeros((EXTRA - both.shape[0], both.shape[1]), F32)
+    return jnp.concatenate([both, rest], axis=0).astype(BF)
+
+
+def transform_kernel(scale, parts_y, line_ref, column_ref, recv_ref, send_ref, *extra):
+    parts_x, tall_in, lanes = recv_ref.shape
+    rows = line_ref.shape[1] // parts_x
+    if extra:
+        total = joined(recv_ref[0, rows:, :])
+        for gx in range(1, parts_x):
+            total = total + joined(recv_ref[gx, rows:, :])
+        extra[0][...] = parted(total[: lanes // 2 // parts_x])
+    data = recv_ref[:, :rows, :].reshape(parts_x * rows, lanes)
+    lines = dot(line_ref[...], data)
+    half = lines.shape[0] // 2
+    lines = lines[:half] + lines[half:]
+    count = half // 2
+    both = jnp.concatenate([lines[:count], lines[count:]], axis=1)
+    depth = both.shape[1]
+    high = both.astype(BF)
+    low = (both - high.astype(F32)).astype(BF)
+    modes = dot(split_rows(both), column_ref[:depth, :])
+    modes = modes[:count] + modes[count:] + dot(high, column_ref[depth:, :])
+    modes = modes * scale
+    tall = count // parts_x
+    for gx in range(parts_x):
+        for gy in range(parts_y):
+            send_ref[gx * parts_y + gy] = modes[
+                gx * tall : (gx + 1) * tall, gy * LANES : (gy + 1) * LANES
+            ].astype(BF)
+
+
+def sum_parts(recv_ref, parts_y):
+    parts = recv_ref.shape[0] // parts_y
+    out = []
+    for b in range(parts):
+        total = recv_ref[b * parts_y].astype(F32)
+        for gy in range(1, parts_y):
+            total = total + recv_ref[b * parts_y + gy].astype(F32)
+        out.append(total)
+    return out
+
+
+def lay_modes(scratch, send_ref, count_y, rows):
+    chans = 64
+    for m in range(0, rows, 2):
+        parts = []
+        for part in range(2):
+            first = scratch[pl.ds(part * rows + m, count_y, stride=2 * rows), :chans]
+            second = scratch[pl.ds(part * rows + m + 1, count_y, stride=2 * rows), :chans]
+            parts.append(jnp.concatenate([first, second], axis=1))
+        send_ref[:, m * chans : (m + 2) * chans] = jnp.concatenate(parts, axis=0)
+
+
+def mix_kernel(forward, parts_y, recv_ref, weight_ref, *refs):
+    send_ref, spec_ref, scratch = refs[-3:]
+    if len(refs) == 4:
+        send_ref[:, WIDE:] = refs[0][...].astype(F32)
+    size_x, size_y, size_z, _, chans, _ = weight_ref.shape
+    rows = size_x * size_z
+    spectra = block_transpose(sum_parts(recv_ref, parts_y), chans // size_y)
+    for ky in range(size_y):
+        spec = spectra[ky]
+        spec_ref[ky] = spec
+        turned = pltpu.roll(spec, chans, 1)
+        if forward:
+            both = jnp.concatenate([spec, turned], axis=0)[:, :chans].T
+            high = both.astype(BF)
+            both = jnp.concatenate([high, (both - high.astype(F32)).astype(BF)], axis=1)
+        else:
+            first = lax.broadcasted_iota(jnp.int32, spec.shape, 1) < chans
+            both = split_rows(jnp.concatenate([spec, jnp.where(first, turned, -turned)], axis=0))
+        mode = lax.broadcasted_iota(jnp.int32, both.shape, 1 if forward else 0) % rows
+        total = jnp.zeros((2 * chans, 4 * rows) if forward else (4 * rows, chans), F32)
+        for m in range(rows):
+            weight = weight_ref[m // size_z, ky, m % size_z].reshape(2 * chans, chans)
+            own = jnp.where(mode == m, both, jnp.zeros_like(both))
+            total = total + (dot(weight, own) if forward else dot(own, weight))
+        if forward:
+            total = total.T
+        total = total[: 2 * rows] + total[2 * rows :]
+        if forward:
+            real, imag = total[:rows], total[rows:]
+            mixed = jnp.concatenate(
+                [
+                    real[:, :chans] - imag[:, chans:],
+                    imag[:, :chans] + real[:, chans:],
+                ],
+                axis=0,
+            )
+        else:
+            mixed = total
+        scratch[ky * 2 * rows : (ky + 1) * 2 * rows, :chans] = mixed
+    lay_modes(scratch, send_ref, size_y, rows)
+
+
+def column_kernel(table_ref, *refs):
+    steps = len(refs) - 2
+    send_ref, scratch = refs[steps], refs[steps + 1]
+    chans = 64
+    if refs[0].shape[1] > WIDE:
+        total = joined(refs[0][:, WIDE:])
+        for s in range(1, steps):
+            total = total + joined(refs[s][:, WIDE:])
+        send_ref[:EXTRA, WIDE:] = parted(total[: EXTRA // 2])
+        send_ref[EXTRA:, WIDE:] = jnp.zeros((send_ref.shape[0] - EXTRA, LANES), BF)
+    data = jnp.concatenate([refs[s][:, :WIDE] for s in range(steps)], axis=0)
+    high = data.astype(BF)
+    low = (data - high.astype(F32)).astype(BF)
+    lines = dot(table_ref[...], high)
+    half = lines.shape[0] // 2
+    lines = lines[:half] + lines[half:] + dot(table_ref[:half, :], low)
+    size_y = half // 2
+    count = WIDE // chans
+    for m in range(0, count, 2):
+        pair = lines[:, m * chans : (m + 2) * chans]
+        scratch[m * half : (m + 1) * half, :] = pair
+        scratch[(m + 1) * half : (m + 2) * half, :] = pltpu.roll(pair, chans, 1)
+    for part in range(2):
+        for y in range(size_y // 2):
+            first = scratch[pl.ds(part * size_y + y, count, stride=half), :chans]
+            second = scratch[pl.ds(part * size_y + y + size_y // 2, count, stride=half), :chans]
+            send_ref[part * count : (part + 1) * count, y * 2 * chans : (y + 1) * 2 * chans] = (
+                jnp.concatenate([first, second], axis=1).astype(BF)
+            )
+
+
+def cells_of(table_ref, recv_refs, scale):
+    data = jnp.concatenate([ref[:, :WIDE] for ref in recv_refs], axis=0)
+    cells = dot(table_ref[...], data)
+    half = cells.shape[0] // 2
+    return (cells[:half] + cells[half:]) * scale
+
+
+def store_pair(out_ref, p, value):
+    size_x, size_y, size_z, chans = out_ref.shape
+    out_ref[:, p, :, :] = value[:, :chans].reshape(size_x, size_z, chans).astype(out_ref.dtype)
+    out_ref[:, p + size_y // 2, :, :] = (
+        value[:, chans:].reshape(size_x, size_z, chans).astype(out_ref.dtype)
+    )
+
+
+def point_kernel(scale, table_ref, *refs):
+    conv_ref, field_ref, cot_ref, act_ref, slope_ref, send_ref = refs[-6:]
+    cells = cells_of(table_ref, refs[:-6], scale)
+    count = field_ref.shape[0]
+    slopes = []
+    grad = jnp.zeros((LANES, LANES), F32)
+    for p in range(count):
+        field = field_ref[p]
+        pre = cells[:, p * LANES : (p + 1) * LANES] + dot(field, conv_ref[...])
+        cdf = normal_cdf(pre)
+        store_pair(act_ref, p, pre * cdf)
+        slope = cot_ref[p].astype(F32) * (cdf + pre * normal_pdf(pre))
+        narrow = slope.astype(BF)
+        slope_ref[p] = narrow
+        slopes.append(narrow.astype(F32))
+        grad = grad + dot(field, narrow, ((0,), (0,)))
+    rows = slopes[0].shape[0]
+    chans = LANES // 2
+    grad = grad[:chans, :chans] + grad[chans:, chans:]
+    block = chans // count
+    for b, chunk in enumerate(block_transpose(slopes, block)):
+        send_ref[b, :rows, :] = chunk.astype(BF)
+        send_ref[b, rows:, :] = parted(grad[b * block : (b + 1) * block])
+
+
+def last_kernel(scale, table_ref, *refs):
+    conv_ref, slope_ref, out_ref, grad_ref = refs[-4:]
+    recv_refs = refs[:-4]
+    block = grad_ref.shape[0] // len(recv_refs)
+    me = lax.axis_index("gx")
+    for step, ref in zip(steps_of(len(recv_refs)), recv_refs):
+        total = joined(ref[:EXTRA, WIDE:])
+        grad_ref[pl.ds(pl.multiple_of((me ^ step) * block, block), block), :] = total[:block] * scale
+    cells = cells_of(table_ref, recv_refs, scale)
+    for p in range(slope_ref.shape[0]):
+        store_pair(out_ref, p, cells[:, p * LANES : (p + 1) * LANES] + dot(slope_ref[p], conv_ref[...]))
+
+
+def outer_kernel(spec_ref, back_ref, out_ref):
+    size_x, size_y, size_z, _, chans, _ = out_ref.shape
+    rows = size_x * size_z
+    first = lax.broadcasted_iota(jnp.int32, back_ref.shape[1:], 1) < chans
+    mode = lax.broadcasted_iota(jnp.int32, (6 * rows, chans), 0) % rows
+    for ky in range(size_y):
+        back, spec = back_ref[ky], spec_ref[ky]
+        turned = pltpu.roll(back, chans, 1)
+        left = jnp.concatenate([back, jnp.where(first, turned, -turned)], axis=0).T
+        right = jnp.concatenate([spec, pltpu.roll(spec, chans, 1)], axis=0)[:, :chans]
+        left_high, right_high = left.astype(BF), right.astype(BF)
+        left_low = (left - left_high.astype(F32)).astype(BF)
+        right_low = (right - right_high.astype(F32)).astype(BF)
+        lefts = jnp.concatenate([left_high, left_high, left_low], axis=1)
+        rights = jnp.concatenate([right_high, right_low, right_high], axis=0)
+        for m in range(rows):
+            own = jnp.where(mode == m, rights, jnp.zeros_like(rights))
+            out_ref[m // size_z, ky, m % size_z] = dot(lefts, own).reshape(2, chans, chans)
+
+
+def call(kernel, outs, *args, scratch=()):
+    params = pltpu.CompilerParams(vmem_limit_bytes=16 * 2**20)
+    return pl.pallas_call(kernel, out_shape=outs, scratch_shapes=list(scratch), compiler_params=params)(*args)
+
+
+def bind(kernel, *static):
+    def bound(*refs):
+        return kernel(*static, *refs)
+
+    return bound
+
+
+def sds(shape, dtype):
+    return jax.ShapeDtypeStruct(shape, dtype)
+
+
+def fast(features, cotangent, spectral_weight, conv_weight, modes_x, modes_y, modes_z):
+    rows_x, rows_y, size_z, chans = features.shape
+    local_x, local_y, count_z = spectral_weight.shape[:3]
+    parts_x, parts_y = lax.axis_size("gx"), lax.axis_size("gy")
+    length_x, length_y = rows_x * parts_x, rows_y * parts_y
+    block = chans // parts_x
+    cells = rows_x * size_z
+    modes = local_x * count_z
+    half_y = rows_y // 2
+    first = 1.0 / math.sqrt(length_x * length_y * size_z)
+    second = 1.0 / math.sqrt(modes_x.shape[0] * modes_y.shape[0] * count_z)
+
+    send, field = call(
+        spread_kernel,
+        (sds((parts_x, cells, LANES), BF), sds((half_y, cells, LANES), BF)),
+        features,
+    )
+    cot = call(pairs_kernel, sds((half_y, cells, LANES), BF), cotangent)
+    outside = pl.BlockSpec(memory_space=pltpu.HBM)
+    inside = pl.BlockSpec(memory_space=pltpu.VMEM)
+    line_table, column_table, column_back, line_back, conv_pair, conv_turn = pl.pallas_call(
+        bind(table_kernel, size_z),
+        in_specs=[outside] * 4 + [inside],
+        out_shape=(
+            sds((4 * modes_x.shape[0] * count_z, length_x * size_z), BF),
+            sds((4 * LANES, 4 * LANES), BF),
+            sds((4 * rows_y, 2 * modes_y.shape[0]), BF),
+            sds((2 * cells, 2 * modes_x.shape[0] * count_z), BF),
+            sds((LANES, LANES), BF),
+            sds((LANES, LANES), BF),
+        ),
+        scratch_shapes=[
+            pltpu.SMEM(modes_x.shape, jnp.int32),
+            pltpu.SMEM(modes_y.shape, jnp.int32),
+            pltpu.SMEM(modes_z.shape, jnp.int32),
+            pltpu.VMEM(conv_weight.shape, BF),
+            pltpu.SemaphoreType.DMA((4,)),
+        ],
+        compiler_params=pltpu.CompilerParams(vmem_limit_bytes=16 * 2**20),
+    )(*(pltpu.with_memory_space_constraint(x, pltpu.HBM) for x in (modes_x, modes_y, modes_z, conv_weight)), spectral_weight)
+
+    def to_modes(send, factor, extra):
+        recv = lax.all_to_all(send, "gx", 0, 0, tiled=True)
+        outs = [sds((parts_x * parts_y, modes, LANES), BF)]
+        if extra:
+            outs.append(sds((EXTRA, LANES), BF))
+        send, *rest = call(bind(transform_kernel, factor, parts_y), outs, line_table, column_table, recv)
+        return lax.all_to_all(send, ("gx", "gy"), 0, 0, tiled=True), rest
+
+    def mix(recv, forward, rest):
+        return call(
+            bind(mix_kernel, forward, parts_y),
+            (
+                sds((2 * local_y, WIDE + len(rest) * LANES), F32),
+                sds((local_y, modes, LANES), F32),
+            ),
+            recv,
+            spectral_weight,
+            *rest,
+            scratch=[pltpu.VMEM((local_y * 2 * modes, LANES), F32)],
+        )
+
+    def to_lines(send, beside=None):
+        pieces = [send]
+        for step in range(1, parts_y):
+            ring = [(i, (i + step) % parts_y) for i in range(parts_y)]
+            pieces.append(lax.ppermute(send, "gy", ring))
+        if beside is not None:
+            pieces[-1], beside = lax.optimization_barrier((pieces[-1], beside))
+        lines = call(
+            column_kernel,
+            sds((2 * modes, send.shape[1]), BF),
+            column_back,
+            *pieces,
+            scratch=[pltpu.VMEM((modes * 2 * rows_y, LANES), F32)],
+        )
+        pieces = [lines]
+        for step in range(2, parts_x, 2):
+            pieces.append(lax.ppermute(lines, "gx", [(i, i ^ step) for i in range(parts_x)]))
+        swap = [(i, i ^ 1) for i in range(parts_x)]
+        return pieces + [lax.ppermute(piece, "gx", swap) for piece in pieces], beside
+
+    recv, _ = to_modes(send, first, False)
+    send, spec = mix(recv, True, [])
+    pieces, _ = to_lines(send)
+    activation, slope, send = call(
+        bind(point_kernel, second),
+        (
+            sds(features.shape, BF),
+            sds((half_y, cells, LANES), BF),
+            sds((parts_x, cells + EXTRA, LANES), BF),
+        ),
+        line_back,
+        *pieces,
+        conv_pair,
+        field,
+        cot,
+    )
+    recv, rest = to_modes(send, second, True)
+    send, back = mix(recv, False, rest)
+    grad_spectral = call(outer_kernel, sds(spectral_weight.shape, F32), spec, back)
+    pieces, grad_spectral = to_lines(send, grad_spectral)
+    grad_features, grad_conv = call(
+        bind(last_kernel, first),
+        (sds(features.shape, BF), sds((chans, chans), F32)),
+        line_back,
+        *pieces,
+        conv_turn,
+        slope,
+    )
+    return activation, grad_features, grad_spectral, grad_conv
 
 
 def phase_tables(freqs, places, length):
@@ -99,15 +620,7 @@
     )
 
 
-def normal_cdf(values):
-    return 0.5 * (1.0 + jax.scipy.special.erf(values * (1.0 / math.sqrt(2.0))))
-
-
-def normal_pdf(values):
-    return jnp.exp(-0.5 * values * values) * (1.0 / math.sqrt(2.0 * math.pi))
-
-
-def shards(features, cotangent, spectral_weight, conv_weight, modes_x, modes_y, modes_z):
+def plain(features, cotangent, spectral_weight, conv_weight, modes_x, modes_y, modes_z):
     rows_x, rows_y, size_z, chans = features.shape
     count_x, count_y, count_z = (modes_x.shape[0], modes_y.shape[0], modes_z.shape[0])
     length_x = rows_x * lax.axis_size("gx")
@@ -170,6 +683,27 @@
     return (activation, grad_features, grad_spectral, grad_conv)
 
 
+def fits(features, spectral_weight):
+    rows_x, rows_y, size_z, chans = features.shape
+    local_x, local_y, count_z = spectral_weight.shape[:3]
+    parts_x, parts_y = lax.axis_size("gx"), lax.axis_size("gy")
+    return (
+        chans == 64
+        and parts_x == 8
+        and rows_y == 2 * parts_x
+        and local_y == parts_x
+        and rows_x * size_z == LANES
+        and local_x * count_z == 2 * parts_x
+        and parts_y == 4
+        and all(n & (n - 1) == 0 for n in (rows_x * parts_x, rows_y * parts_y, size_z))
+    )
+
+
+def shards(features, cotangent, spectral_weight, *rest):
+    run = fast if fits(features, spectral_weight) else plain
+    return run(features, cotangent, spectral_weight, *rest)
+
+
 def solution(mesh):
     placed = (
         P("gx", "gy", None, None),

time: 257 us -> 92.3 us (0.36); the launches traced: 253 us -> 91.9 us
  blocking collectives: 95.9 us -> 32.5 us
  matrix products: 51 us -> 0 us
  waiting for transfers between devices: 59.4 us -> 17.4 us
  Pallas kernels: 0 us -> 18.5 us
  between operations: 14.7 us -> 0.74 us
  starting transfers between devices: 4.45 us -> 17.3 us
  local copies, waits for them, and re-layouts: 17.1 us -> 5.41 us
  other arithmetic: 10.5 us -> 0 us
    dot_general x51 -> x0, matrix products: 51 us -> none  [the longest x2 5.92 us: to_cells(): jnp.einsum('xykc,kz->xyzc', plane_imag, sin_z, precision=HIGH)]
    psum x1 -> x0, blocking collectives: 38.9 us -> none  [shards(): grad_conv = first * lax.psum(local_conv, ('gx', 'gy'))]
    reduce_scatter x2 -> x0, waiting for transfers between devices: 32.3 us -> none  [to_modes(): lax.psum_scatter(jnp.stack([mode_real, mode_imag], axis=2), 'gy', scatter...]
    all_gather x2 -> x0, blocking collectives: 27.7 us -> none  [to_cells(): piece = lax.all_gather(spectrum, 'gy', axis=0, tiled=True)]
    all_gather x2 -> x0, waiting for transfers between devices: 21.7 us -> none  [to_cells(): piece = lax.all_gather(lines, 'gx', axis=0, tiled=True)]
    pallas_call x0 -> x12, Pallas kernels: none -> 18.5 us  [the longest x11 15.8 us: call(): pl.pallas_call(kernel, out_shape=outs, scratch_shapes=list(scratch), comp...]
    ppermute x0 -> x20, waiting for transfers between devices: none -> 15.4 us  [the longest x6 7.03 us: to_lines(): pieces.append(lax.ppermute(send, 'gy', ring))]
    ppermute x0 -> x20, starting transfers between devices: none -> 12.1 us  [the longest x6 7.11 us: to_lines(): lax.ppermute(lines, 'gx', [(i, i ^ step) for i in range(parts_x)])]
  transfers between devices with their start and end apart: 5 -> 21, of which waited for: 4 -> 15; matrix products, arithmetic and copies ran while one was open for 5% -> 0% of each run, Pallas kernels for 0% -> 9%
where the time goes in v1:
time: 92.3 us; the launch traced here: 91.9 us
  blocking collectives  32.5 us (35%)
  Pallas kernels  18.5 us (20%)
  waiting for transfers between devices  17.4 us (19%)
  starting transfers between devices  17.3 us (19%)
  local copies, waits for them, and re-layouts  5.41 us (6%)
    all_to_all x2, blocking collectives, to_modes(): return (lax.all_to_all(send, ('gx', 'gy'), 0, 0, tiled=True), rest)  22.6 us
    pallas_call x11, Pallas kernels, call(): pl.pallas_call(kernel, out_shape=outs, scratch_shapes=list(scratch), comp...  15.8 us
    all_to_all x1, blocking collectives, to_modes(): recv = lax.all_to_all(send, 'gx', 0, 0, tiled=True)  9.83 us
    ppermute x6, starting transfers between devices, to_lines(): lax.ppermute(lines, 'gx', [(i, i ^ step) for i in range(parts_x)])  7.11 us
    ppermute x6, waiting for transfers between devices, to_lines(): pieces.append(lax.ppermute(send, 'gy', ring))  7.03 us
    ppermute x6, waiting for transfers between devices, to_lines(): lax.ppermute(lines, 'gx', [(i, i ^ step) for i in range(parts_x)])  5.99 us
    unnamed x10, local copies, waits for them, and re-layouts  5.41 us
    all_to_all x1, starting transfers between devices, to_modes(): recv = lax.all_to_all(send, 'gx', 0, 0, tiled=True)  5.17 us
  transfers between devices with their start and end apart: 21, of which 15 were waited for; matrix products, arithmetic and copies ran while one was open for 0% of the time, Pallas kernels for 9%

profile of v1, /device:TPU:0, one launch (start us, length us, event | category | flops | bytes accessed | tf_op | source)
XLA Modules:
  0.0 91.9 jit_solution(7668595724497575954)
XLA Ops:
  1.7 1.4 %shard_map.103 = (bf16[8,128,128]{2,1,0:T(8,128)(2,1)}, bf16[8,128,128]{2,1,0:T(8,128)(2,1)S(1)}) custom-call(bf16[16,16,8,64]{3,2,1,0:T(8,128)(2,1)S(1)} %copy-done.4), custom_call_target="tpu_custom_call" | custom-call | tf_op jit(solution)/shard_map/pallas_call | solution.py:405
  3.0 5.2 %all-to-all-start = ((bf16[8,128,128]{2,1,0:T(8,128)(2,1)}), bf16[8,128,128]{2,1,0:T(8,128)(2,1)S(1)}, u32[]{:S(2)}, u32[]{:S(2)}) async-start(bf16[8,128,128]{2,1,0:T(8,128)(2,1)} %get-tuple-element.29), calls=%async_computation | async-start | bytes 524288 | tf_op jit(solution)/shard_map/all_to_all | solution.py:461
  8.2 2.2 %copy-done = bf16[4,8,4,2,64,64]{5,4,3,2,1,0:T(8,128)(2,1)S(1)} copy-done((bf16[4,8,4,2,64,64]{5,4,3,2,1,0:T(8,128)(2,1)S(1)}, bf16[4,8,4,2,64,64]{5,4,3,2,1,0:T(8,128)(2,1)}, u32[]{:S(2)}) %copy-start) | copy-done | bytes 2097176
  10.4 2.7 %shard_map.102 = (bf16[512,1024]{1,0:T(8,128)(2,1)S(1)}, bf16[512,512]{1,0:T(8,128)(2,1)S(1)}, bf16[64,64]{1,0:T(8,128)(2,1)S(1)}, bf16[256,256]{1,0:T(8,128)(2,...) custom-call(s32[32]{0:T(128)} %refs_0_.1, s32[32]{0:T(128)} %refs_1_.3, s32[4]{0:T(128)} %refs_2_.1, ...), custom_call_target="tpu_custom_call" | custom-call | tf_op jit(solution)/shard_map/pallas_call | solution.py:439
  13.1 2.0 %all-to-all-done.refs_2_ = bf16[8,128,128]{2,1,0:T(8,128)(2,1)S(1)} async-done(((bf16[8,128,128]{2,1,0:T(8,128)(2,1)}), bf16[8,128,128]{2,1,0:T(8,128)(2,1)S(1)}, u32[]{:S(2)}, u32[]{:S(2)}) %all-to-all-start) | async-done | bytes 262176 | tf_op jit(solution)/shard_map/all_to_all | solution.py:461
  16.0 12.5 %all_to_all.20.refs_0_ = bf16[32,16,128]{2,1,0:T(8,128)(2,1)S(1)} all-to-all(bf16[32,16,128]{2,1,0:T(8,128)(2,1)S(1)} %shard_map.104), channel_id=1, replica_groups=mesh['gx'=8,'gy'=4] {'gx','gy'}, dimensions={0} | all-to-all | bytes 262144 | tf_op jit(solution)/shard_map/all_to_all | solution.py:466
  28.5 2.2 %copy-done.1 = bf16[4,8,4,2,64,64]{5,4,3,2,1,0:T(8,128)(2,1)S(1)} copy-done((bf16[4,8,4,2,64,64]{5,4,3,2,1,0:T(8,128)(2,1)S(1)}, bf16[4,8,4,2,64,64]{5,4,3,2,1,0:T(8,128)(2,1)}, u32[]{:S(2)}) %copy-start.1) | copy-done | bytes 2097176
  30.7 2.0 %shard_map.105 = (f32[16,1024]{1,0:T(8,128)S(1)}, f32[8,16,128]{2,1,0:T(8,128)S(1)}) custom-call(bf16[32,16,128]{2,1,0:T(8,128)(2,1)S(1)} %all_to_all.20.refs_0_, bf16[4,8,4,2,64,64]{5,4,3,2,1,0:T(8,128)(2,1)S(1)} %copy-done.1), custom_call_target="tpu_custom_call" | custom-call | tf_op jit(solution)/shard_map/pallas_call | solution.py:405
  32.7 1.3 %collective-permute-start.2 = (f32[16,1024]{1,0:T(8,128)S(1)}, f32[16,1024]{1,0:T(8,128)S(1)}, u32[]{:S(2)}, u32[]{:S(2)}) collective-permute-start(f32[16,1024]{1,0:T(8,128)S(1)} %get-tuple-element.30.refs_0_), channel_id=1, source_target_pairs={{0,3},{1,0},{2,1},{3,2},{4,7},{5,4},{6,5},{7,6},{8,11},{9,8},{10,9... | collective-permute-start | bytes 196616 | tf_op jit(solution)/shard_map/ppermute | solution.py:485
  35.2 2.1 %collective-permute-done.2.refs_3_ = f32[16,1024]{1,0:T(8,128)S(1)} collective-permute-done((f32[16,1024]{1,0:T(8,128)S(1)}, f32[16,1024]{1,0:T(8,128)S(1)}, u32[]{:S(2)}, u32[]{:S(2)}) %collective-permute-start.2) | collective-permute-done | bytes 65568 | tf_op jit(solution)/shard_map/ppermute | solution.py:485
  37.3 3.9 %collective-permute-done.1.refs_2_ = f32[16,1024]{1,0:T(8,128)S(1)} collective-permute-done((f32[16,1024]{1,0:T(8,128)S(1)}, f32[16,1024]{1,0:T(8,128)S(1)}, u32[]{:S(2)}, u32[]{:S(2)}) %collective-permute-start.1) | collective-permute-done | bytes 65568 | tf_op jit(solution)/shard_map/ppermute | solution.py:485
  42.4 1.5 %collective-permute-start.4 = (bf16[32,1024]{1,0:T(8,128)(2,1)S(1)}, bf16[32,1024]{1,0:T(8,128)(2,1)S(1)}, u32[]{:S(2)}, u32[]{:S(2)}) collective-permute-start(bf16[32,1024]{1,0:T(8,128)(2,1)S(1)} %shard_map.106.refs_1_), channel_id=1, source_target_pairs={{0,16},{4,20},{8,24},{12,28},{16,0},{20,4},{24,8},{28,12},{1,17},{... | collective-permute-start | bytes 196616 | tf_op jit(solution)/shard_map/ppermute | solution.py:497
  43.9 1.2 %collective-permute-start.3 = (bf16[32,1024]{1,0:T(8,128)(2,1)S(1)}, bf16[32,1024]{1,0:T(8,128)(2,1)S(1)}, u32[]{:S(2)}, u32[]{:S(2)}) collective-permute-start(bf16[32,1024]{1,0:T(8,128)(2,1)S(1)} %shard_map.106.refs_1_), channel_id=1, source_target_pairs={{0,8},{4,12},{8,0},{12,4},{16,24},{20,28},{24,16},{28,20},{1,9},{5... | collective-permute-start | bytes 196616 | tf_op jit(solution)/shard_map/ppermute | solution.py:497
  45.1 1.8 %collective-permute-done.5.refs_4_ = bf16[32,1024]{1,0:T(8,128)(2,1)S(1)} collective-permute-done((bf16[32,1024]{1,0:T(8,128)(2,1)S(1)}, bf16[32,1024]{1,0:T(8,128)(2,1)S(1)}, u32[]{:S(2)}, u32[]{:S(2)}) %collective-permute-start.5) | collective-permute-done | bytes 65568 | tf_op jit(solution)/shard_map/ppermute | solution.py:497
  49.4 1.6 %shard_map.108 = (bf16[16,16,8,64]{3,2,1,0:T(8,128)(2,1)}, bf16[8,128,128]{2,1,0:T(8,128)(2,1)S(1)}, bf16[8,144,128]{2,1,0:T(8,128)(2,1)S(1)}) custom-call(bf16[256,256]{1,0:T(8,128)(2,1)S(1)} %get-tuple-element.25.refs_0_, bf16[32,1024]{1,0:T(8,128)(2,1)S(1)} %shard_map.106.refs_1_, bf16[32,1024]{1,0:T(8,128)(2,1)S(1)} %collective-permute-done.3.refs_2_, ...), custom_call_target="tpu_custom_call" | custom-call | tf_op jit(solution)/shard_map/pallas_call | solution.py:405
  51.1 9.8 %all_to_all.21.refs_2_ = bf16[8,144,128]{2,1,0:T(8,128)(2,1)S(1)} all-to-all(bf16[8,144,128]{2,1,0:T(8,128)(2,1)S(1)} %get-tuple-element.34), channel_id=1, replica_groups=mesh['gx'=8,'gy'=4] {'gx'}, dimensions={0} | all-to-all | bytes 589824 | tf_op jit(solution)/shard_map/all_to_all | solution.py:461
  61.7 10.1 %all_to_all.22.refs_0_ = bf16[32,16,128]{2,1,0:T(8,128)(2,1)S(1)} all-to-all(bf16[32,16,128]{2,1,0:T(8,128)(2,1)S(1)} %get-tuple-element.35), channel_id=1, replica_groups=mesh['gx'=8,'gy'=4] {'gx','gy'}, dimensions={0} | all-to-all | bytes 262144 | tf_op jit(solution)/shard_map/all_to_all | solution.py:466
  71.8 1.6 %shard_map.110 = (f32[16,1152]{1,0:T(8,128)S(1)}, f32[8,16,128]{2,1,0:T(8,128)S(1)}) custom-call(bf16[32,16,128]{2,1,0:T(8,128)(2,1)S(1)} %all_to_all.22.refs_0_, bf16[4,8,4,2,64,64]{5,4,3,2,1,0:T(8,128)(2,1)S(1)} %copy-done.2, bf16[16,128]{1,0:T(8,128)(2,1)S(1)} %get-tuple-element.36.refs_2_), custom_call_target="tpu_custom_call" | custom-call | tf_op jit(solution)/shard_map/pallas_call | solution.py:405
  74.6 1.2 %collective-permute-start.10 = (f32[16,1152]{1,0:T(8,128)S(1)}, f32[16,1152]{1,0:T(8,128)S(1)}, u32[]{:S(2)}, u32[]{:S(2)}) collective-permute-start(f32[16,1152]{1,0:T(8,128)S(1)} %get-tuple-element.37.refs_0_), channel_id=1, source_target_pairs={{0,1},{1,2},{2,3},{3,0},{4,5},{5,6},{6,7},{7,4},{8,9},{9,10},{10,1... | collective-permute-start | bytes 221192 | tf_op jit(solution)/shard_map/ppermute | solution.py:485
  75.9 5.3 %shard_map.111 = f32[4,8,4,2,64,64]{5,4,3,2,1,0:T(8,128)} custom-call(f32[8,16,128]{2,1,0:T(8,128)S(1)} %get-tuple-element.38.spec_ref, f32[8,16,128]{2,1,0:T(8,128)S(1)} %get-tuple-element.39.back_ref), custom_call_target="tpu_custom_call" | custom-call | tf_op jit(solution)/shard_map/pallas_call | solution.py:405
  83.4 1.5 %collective-permute-start.14 = (bf16[32,1152]{1,0:T(8,128)(2,1)S(1)}, bf16[32,1152]{1,0:T(8,128)(2,1)S(1)}, u32[]{:S(2)}, u32[]{:S(2)}) collective-permute-start(bf16[32,1152]{1,0:T(8,128)(2,1)S(1)} %shard_map.112.refs_1_), channel_id=1, source_target_pairs={{0,16},{4,20},{8,24},{12,28},{16,0},{20,4},{24,8},{28,12},{1,17},{... | collective-permute-start | bytes 221192 | tf_op jit(solution)/shard_map/ppermute | solution.py:497
  84.9 1.3 %collective-permute-start.13 = (bf16[32,1152]{1,0:T(8,128)(2,1)S(1)}, bf16[32,1152]{1,0:T(8,128)(2,1)S(1)}, u32[]{:S(2)}, u32[]{:S(2)}) collective-permute-start(bf16[32,1152]{1,0:T(8,128)(2,1)S(1)} %shard_map.112.refs_1_), channel_id=1, source_target_pairs={{0,8},{4,12},{8,0},{12,4},{16,24},{20,28},{24,16},{28,20},{1,9},{5... | collective-permute-start | bytes 221192 | tf_op jit(solution)/shard_map/ppermute | solution.py:497
  86.2 1.9 %collective-permute-done.15.refs_4_ = bf16[32,1152]{1,0:T(8,128)(2,1)S(1)} collective-permute-done((bf16[32,1152]{1,0:T(8,128)(2,1)S(1)}, bf16[32,1152]{1,0:T(8,128)(2,1)S(1)}, u32[]{:S(2)}, u32[]{:S(2)}) %collective-permute-start.15) | collective-permute-done | bytes 73760 | tf_op jit(solution)/shard_map/ppermute | solution.py:497
  90.5 1.3 %shard_map.113 = (bf16[16,16,8,64]{3,2,1,0:T(8,128)(2,1)}, f32[64,64]{1,0:T(8,128)}) custom-call(bf16[256,256]{1,0:T(8,128)(2,1)S(1)} %get-tuple-element.25.refs_0_, bf16[32,1152]{1,0:T(8,128)(2,1)S(1)} %shard_map.112.refs_1_, bf16[32,1152]{1,0:T(8,128)(2,1)S(1)} %collective-permute-done.13.refs_2_, bf16[32,1152]{1,0:T(8,128)(2,1)S(1)} %collective-permute-done.14.refs_3_, ...), custom_call_target="tpu_custom_call" | custom-call | tf_op jit(solution)/shard_map/pallas_call | solution.py:405
  (43 shorter events, 13.4 us)
Async XLA Ops:
  1.7 46.5 %copy-start.3 = (bf16[16,16,8,64]{3,2,1,0:T(8,128)(2,1)S(1)}, bf16[16,16,8,64]{3,2,1,0:T(8,128)(2,1)}, u32[]{:S(2)}) copy-start(bf16[16,16,8,64]{3,2,1,0:T(8,128)(2,1)} %field_ref.3) | copy-start | bytes 786436
  3.0 12.1 %all-to-all-start = ((bf16[8,128,128]{2,1,0:T(8,128)(2,1)}), bf16[8,128,128]{2,1,0:T(8,128)(2,1)S(1)}, u32[]{:S(2)}, u32[]{:S(2)}) async-start(bf16[8,128,128]{2,1,0:T(8,128)(2,1)} %get-tuple-element.29), calls=%async_computation | async-start | bytes 524288 | tf_op jit(solution)/shard_map/all_to_all | solution.py:461
  28.5 2.2 %copy-start.1 = (bf16[4,8,4,2,64,64]{5,4,3,2,1,0:T(8,128)(2,1)S(1)}, bf16[4,8,4,2,64,64]{5,4,3,2,1,0:T(8,128)(2,1)}, u32[]{:S(2)}) copy-start(bf16[4,8,4,2,64,64]{5,4,3,2,1,0:T(8,128)(2,1)} %refs_1_.5) | copy-start | bytes 6291460
  30.7 41.1 %copy-start.2 = (bf16[4,8,4,2,64,64]{5,4,3,2,1,0:T(8,128)(2,1)S(1)}, bf16[4,8,4,2,64,64]{5,4,3,2,1,0:T(8,128)(2,1)}, u32[]{:S(2)}) copy-start(bf16[4,8,4,2,64,64]{5,4,3,2,1,0:T(8,128)(2,1)} %refs_1_.5) | copy-start | bytes 6291460
  32.7 4.6 %collective-permute-start.2 = (f32[16,1024]{1,0:T(8,128)S(1)}, f32[16,1024]{1,0:T(8,128)S(1)}, u32[]{:S(2)}, u32[]{:S(2)}) collective-permute-start(f32[16,1024]{1,0:T(8,128)S(1)} %get-tuple-element.30.refs_0_), channel_id=1, source_target_pairs={{0,3},{1,0},{2,1},{3,2},{4,7},{5,4},{6,5},{7,6},{8,11},{9,8},{10,9... | collective-permute-start | bytes 196616 | tf_op jit(solution)/shard_map/ppermute | solution.py:485
  34.0 7.2 %collective-permute-start.1 = (f32[16,1024]{1,0:T(8,128)S(1)}, f32[16,1024]{1,0:T(8,128)S(1)}, u32[]{:S(2)}, u32[]{:S(2)}) collective-permute-start(f32[16,1024]{1,0:T(8,128)S(1)} %get-tuple-element.30.refs_0_), channel_id=1, source_target_pairs={{0,2},{1,3},{2,0},{3,1},{4,6},{5,7},{6,4},{7,5},{8,10},{9,11},{10,... | collective-permute-start | bytes 196616 | tf_op jit(solution)/shard_map/ppermute | solution.py:485
  34.0 7.2 %collective-permute-start = (f32[16,1024]{1,0:T(8,128)S(1)}, f32[16,1024]{1,0:T(8,128)S(1)}, u32[]{:S(2)}, u32[]{:S(2)}) collective-permute-start(f32[16,1024]{1,0:T(8,128)S(1)} %get-tuple-element.30.refs_0_), channel_id=1, source_target_pairs={{0,1},{1,2},{2,3},{3,0},{4,5},{5,6},{6,7},{7,4},{8,9},{9,10},{10,1... | collective-permute-start | bytes 196616 | tf_op jit(solution)/shard_map/ppermute | solution.py:485
  41.6 5.3 %collective-permute-start.5 = (bf16[32,1024]{1,0:T(8,128)(2,1)S(1)}, bf16[32,1024]{1,0:T(8,128)(2,1)S(1)}, u32[]{:S(2)}, u32[]{:S(2)}) collective-permute-start(bf16[32,1024]{1,0:T(8,128)(2,1)S(1)} %shard_map.106.refs_1_), channel_id=1, source_target_pairs={{0,24},{4,28},{8,16},{12,20},{16,8},{20,12},{24,0},{28,4},{1,25},{... | collective-permute-start | bytes 196616 | tf_op jit(solution)/shard_map/ppermute | solution.py:497
  42.4 5.0 %collective-permute-start.4 = (bf16[32,1024]{1,0:T(8,128)(2,1)S(1)}, bf16[32,1024]{1,0:T(8,128)(2,1)S(1)}, u32[]{:S(2)}, u32[]{:S(2)}) collective-permute-start(bf16[32,1024]{1,0:T(8,128)(2,1)S(1)} %shard_map.106.refs_1_), channel_id=1, source_target_pairs={{0,16},{4,20},{8,24},{12,28},{16,0},{20,4},{24,8},{28,12},{1,17},{... | collective-permute-start | bytes 196616 | tf_op jit(solution)/shard_map/ppermute | solution.py:497
  43.9 4.3 %collective-permute-start.3 = (bf16[32,1024]{1,0:T(8,128)(2,1)S(1)}, bf16[32,1024]{1,0:T(8,128)(2,1)S(1)}, u32[]{:S(2)}, u32[]{:S(2)}) collective-permute-start(bf16[32,1024]{1,0:T(8,128)(2,1)S(1)} %shard_map.106.refs_1_), channel_id=1, source_target_pairs={{0,8},{4,12},{8,0},{12,4},{16,24},{20,28},{24,16},{28,20},{1,9},{5... | collective-permute-start | bytes 196616 | tf_op jit(solution)/shard_map/ppermute | solution.py:497
  45.1 3.2 %collective-permute-start.6 = (bf16[32,1024]{1,0:T(8,128)(2,1)S(1)}, bf16[32,1024]{1,0:T(8,128)(2,1)S(1)}, u32[]{:S(2)}, u32[]{:S(2)}) collective-permute-start(bf16[32,1024]{1,0:T(8,128)(2,1)S(1)} %shard_map.106.refs_1_), channel_id=1, source_target_pairs={{0,4},{4,0},{8,12},{12,8},{16,20},{20,16},{24,28},{28,24},{1,5},{5... | collective-permute-start | bytes 196616 | tf_op jit(solution)/shard_map/ppermute | solution.py:499
  46.9 1.4 %collective-permute-start.9 = (bf16[32,1024]{1,0:T(8,128)(2,1)S(1)}, bf16[32,1024]{1,0:T(8,128)(2,1)S(1)}, u32[]{:S(2)}, u32[]{:S(2)}) collective-permute-start(bf16[32,1024]{1,0:T(8,128)(2,1)S(1)} %collective-permute-done.5.refs_4_), channel_id=1, source_target_pairs={{0,4},{4,0},{8,12},{12,8},{16,20},{20,16},{24,28},{28,24},{1,5},{5... | collective-permute-start | bytes 196616 | tf_op jit(solution)/shard_map/ppermute | solution.py:499
  47.3 1.3 %collective-permute-start.8 = (bf16[32,1024]{1,0:T(8,128)(2,1)S(1)}, bf16[32,1024]{1,0:T(8,128)(2,1)S(1)}, u32[]{:S(2)}, u32[]{:S(2)}) collective-permute-start(bf16[32,1024]{1,0:T(8,128)(2,1)S(1)} %collective-permute-done.4.refs_3_), channel_id=1, source_target_pairs={{0,4},{4,0},{8,12},{12,8},{16,20},{20,16},{24,28},{28,24},{1,5},{5... | collective-permute-start | bytes 196616 | tf_op jit(solution)/shard_map/ppermute | solution.py:499
  48.2 1.3 %collective-permute-start.7 = (bf16[32,1024]{1,0:T(8,128)(2,1)S(1)}, bf16[32,1024]{1,0:T(8,128)(2,1)S(1)}, u32[]{:S(2)}, u32[]{:S(2)}) collective-permute-start(bf16[32,1024]{1,0:T(8,128)(2,1)S(1)} %collective-permute-done.3.refs_2_), channel_id=1, source_target_pairs={{0,4},{4,0},{8,12},{12,8},{16,20},{20,16},{24,28},{28,24},{1,5},{5... | collective-permute-start | bytes 196616 | tf_op jit(solution)/shard_map/ppermute | solution.py:499
  73.4 7.8 %collective-permute-start.12 = (f32[16,1152]{1,0:T(8,128)S(1)}, f32[16,1152]{1,0:T(8,128)S(1)}, u32[]{:S(2)}, u32[]{:S(2)}) collective-permute-start(f32[16,1152]{1,0:T(8,128)S(1)} %get-tuple-element.37.refs_0_), channel_id=1, source_target_pairs={{0,3},{1,0},{2,1},{3,2},{4,7},{5,4},{6,5},{7,6},{8,11},{9,8},{10,9... | collective-permute-start | bytes 221192 | tf_op jit(solution)/shard_map/ppermute | solution.py:485
  74.6 7.6 %collective-permute-start.11 = (f32[16,1152]{1,0:T(8,128)S(1)}, f32[16,1152]{1,0:T(8,128)S(1)}, u32[]{:S(2)}, u32[]{:S(2)}) collective-permute-start(f32[16,1152]{1,0:T(8,128)S(1)} %get-tuple-element.37.refs_0_), channel_id=1, source_target_pairs={{0,2},{1,3},{2,0},{3,1},{4,6},{5,7},{6,4},{7,5},{8,10},{9,11},{10,... | collective-permute-start | bytes 221192 | tf_op jit(solution)/shard_map/ppermute | solution.py:485
  74.6 7.6 %collective-permute-start.10 = (f32[16,1152]{1,0:T(8,128)S(1)}, f32[16,1152]{1,0:T(8,128)S(1)}, u32[]{:S(2)}, u32[]{:S(2)}) collective-permute-start(f32[16,1152]{1,0:T(8,128)S(1)} %get-tuple-element.37.refs_0_), channel_id=1, source_target_pairs={{0,1},{1,2},{2,3},{3,0},{4,5},{5,6},{6,7},{7,4},{8,9},{9,10},{10,1... | collective-permute-start | bytes 221192 | tf_op jit(solution)/shard_map/ppermute | solution.py:485
  82.7 5.4 %collective-permute-start.15 = (bf16[32,1152]{1,0:T(8,128)(2,1)S(1)}, bf16[32,1152]{1,0:T(8,128)(2,1)S(1)}, u32[]{:S(2)}, u32[]{:S(2)}) collective-permute-start(bf16[32,1152]{1,0:T(8,128)(2,1)S(1)} %shard_map.112.refs_1_), channel_id=1, source_target_pairs={{0,24},{4,28},{8,16},{12,20},{16,8},{20,12},{24,0},{28,4},{1,25},{... | collective-permute-start | bytes 221192 | tf_op jit(solution)/shard_map/ppermute | solution.py:497
  83.4 5.1 %collective-permute-start.14 = (bf16[32,1152]{1,0:T(8,128)(2,1)S(1)}, bf16[32,1152]{1,0:T(8,128)(2,1)S(1)}, u32[]{:S(2)}, u32[]{:S(2)}) collective-permute-start(bf16[32,1152]{1,0:T(8,128)(2,1)S(1)} %shard_map.112.refs_1_), channel_id=1, source_target_pairs={{0,16},{4,20},{8,24},{12,28},{16,0},{20,4},{24,8},{28,12},{1,17},{... | collective-permute-start | bytes 221192 | tf_op jit(solution)/shard_map/ppermute | solution.py:497
  84.9 4.4 %collective-permute-start.13 = (bf16[32,1152]{1,0:T(8,128)(2,1)S(1)}, bf16[32,1152]{1,0:T(8,128)(2,1)S(1)}, u32[]{:S(2)}, u32[]{:S(2)}) collective-permute-start(bf16[32,1152]{1,0:T(8,128)(2,1)S(1)} %shard_map.112.refs_1_), channel_id=1, source_target_pairs={{0,8},{4,12},{8,0},{12,4},{16,24},{20,28},{24,16},{28,20},{1,9},{5... | collective-permute-start | bytes 221192 | tf_op jit(solution)/shard_map/ppermute | solution.py:497
  86.2 3.1 %collective-permute-start.16 = (bf16[32,1152]{1,0:T(8,128)(2,1)S(1)}, bf16[32,1152]{1,0:T(8,128)(2,1)S(1)}, u32[]{:S(2)}, u32[]{:S(2)}) collective-permute-start(bf16[32,1152]{1,0:T(8,128)(2,1)S(1)} %shard_map.112.refs_1_), channel_id=1, source_target_pairs={{0,4},{4,0},{8,12},{12,8},{16,20},{20,16},{24,28},{28,24},{1,5},{5... | collective-permute-start | bytes 221192 | tf_op jit(solution)/shard_map/ppermute | solution.py:499
  88.1 1.3 %collective-permute-start.19 = (bf16[32,1152]{1,0:T(8,128)(2,1)S(1)}, bf16[32,1152]{1,0:T(8,128)(2,1)S(1)}, u32[]{:S(2)}, u32[]{:S(2)}) collective-permute-start(bf16[32,1152]{1,0:T(8,128)(2,1)S(1)} %collective-permute-done.15.refs_4_), channel_id=1, source_target_pairs={{0,4},{4,0},{8,12},{12,8},{16,20},{20,16},{24,28},{28,24},{1,5},{5... | collective-permute-start | bytes 221192 | tf_op jit(solution)/shard_map/ppermute | solution.py:499
  88.6 1.3 %collective-permute-start.18 = (bf16[32,1152]{1,0:T(8,128)(2,1)S(1)}, bf16[32,1152]{1,0:T(8,128)(2,1)S(1)}, u32[]{:S(2)}, u32[]{:S(2)}) collective-permute-start(bf16[32,1152]{1,0:T(8,128)(2,1)S(1)} %collective-permute-done.14.refs_3_), channel_id=1, source_target_pairs={{0,4},{4,0},{8,12},{12,8},{16,20},{20,16},{24,28},{28,24},{1,5},{5... | collective-permute-start | bytes 221192 | tf_op jit(solution)/shard_map/ppermute | solution.py:499
  89.3 1.3 %collective-permute-start.17 = (bf16[32,1152]{1,0:T(8,128)(2,1)S(1)}, bf16[32,1152]{1,0:T(8,128)(2,1)S(1)}, u32[]{:S(2)}, u32[]{:S(2)}) collective-permute-start(bf16[32,1152]{1,0:T(8,128)(2,1)S(1)} %collective-permute-done.13.refs_2_), channel_id=1, source_target_pairs={{0,4},{4,0},{8,12},{12,8},{16,20},{20,16},{24,28},{28,24},{1,5},{5... | collective-permute-start | bytes 221192 | tf_op jit(solution)/shard_map/ppermute | solution.py:499
  (2 other events, 3.2 us)

commit v2 on v1

--- a/solution.py
+++ b/solution.py
@@ -13,6 +13,7 @@
 LANES = 128
 EXTRA = 16
 WIDE = 1024
+SIDES = 4
 
 
 def steps_of(parts):
@@ -75,32 +76,46 @@
     whole = line_ref.shape[1]
     tile = 16
 
-    row, col = grid_of(tile, whole)
+    rows_x = length_x // parts_x
+    row, col = grid_of(tile, LANES)
     per = tile // count_z
-    x, z = col // size_z, col % size_z
-    base = pick(mz_ref, row % count_z, range(count_z)) * z * length_x
-    x = x * size_z
+    quarter = whole // 4
+    base = pick(mz_ref, row % count_z, range(count_z)) * (col % size_z) * length_x
     inner = row // count_z
-    for part in range(2):
-        for start in range(0, count_x, per):
-            turns = pick(mx_ref, inner, range(start, start + per)) * x + base
-            at = part * count_x * count_z + start * count_z
-            store_halves(line_ref, at, cosine(turns + part * (whole // 4), whole))
+    offset = jnp.zeros(col.shape, jnp.int32)
+    for k, step in enumerate(steps_of(parts_x)):
+        offset = jnp.where(col == k, (me_x ^ step) * (rows_x * size_z), offset)
+    modes = count_x * count_z
+    for start in range(0, count_x, per):
+        freq = pick(mx_ref, inner, range(start, start + per))
+        turns = freq * (col // size_z * size_z) + base
+        cos, sin = cosine(turns, whole), cosine(turns - quarter, whole)
+        turns = freq * offset
+        cos_step, sin_step = cosine(turns, whole), cosine(turns - quarter, whole)
+        at = start * count_z
+        for k in range(parts_x):
+            cos_k = jnp.broadcast_to(cos_step[:, k : k + 1], cos.shape)
+            sin_k = jnp.broadcast_to(sin_step[:, k : k + 1], cos.shape)
+            columns = line_ref.at[:, k * LANES : (k + 1) * LANES]
+            store_halves(columns, at, cos * cos_k - sin * sin_k)
+            store_halves(columns, at + modes, -sin * cos_k - cos * sin_k)
 
     rows_y = column_ref.shape[0] // 4 // block
     length_y = rows_y * parts_y
-    row, col = grid_of(tile, column_ref.shape[1])
     per = tile // block
-    wide = local_y * block
-    freq = pick(my_ref, col // (2 * wide) * local_y + col // block % local_y, range(count_y))
-    shift = col // wide % 2 * (length_y // 4)
+    ky = col // block % local_y
+    shift = col // (LANES // 2) * (length_y // 4)
     same = row % block == col % block
+    low = col < LANES // 2
     inner = row // block + me_y * rows_y
-    for part in range(2):
+    for gy in range(parts_y):
+        freq = pick(my_ref, ky, range(gy * local_y, (gy + 1) * local_y))
+        columns = column_ref.at[:, gy * LANES : (gy + 1) * LANES]
         for start in range(0, rows_y, per):
-            turns = freq * (inner + start) + shift - part * (length_y // 4)
-            value = jnp.where(same, cosine(turns, length_y), 0.0)
-            store_halves(column_ref, part * rows_y * block + start * block, value)
+            value = jnp.where(same, cosine(freq * (inner + start) + shift, length_y), 0.0)
+            store_halves(columns, start * block, value)
+            turned = pltpu.roll(value, LANES // 2, 1)
+            store_halves(columns, (rows_y + start) * block, jnp.where(low, -turned, turned))
 
     row, col = grid_of(2 * rows_y, cback_ref.shape[1])
     places = [
@@ -117,7 +132,6 @@
     freq = pick(mx_ref, kx, places) * size_z
     base = pick(mz_ref, col % count_z, range(count_z)) * (row % size_z) * length_x
     base = base + col // modes % 2 * (whole // 4)
-    rows_x = length_x // parts_x
     inner = row // size_z + me_x * rows_x
     per = tile // size_z
     for start in range(0, rows_x, per):
@@ -175,16 +189,21 @@
     return jnp.exp(-0.5 * values * values) * (1.0 / math.sqrt(2.0 * math.pi))
 
 
-def spread_kernel(field_ref, send_ref, pairs_ref):
-    size_x, _, size_z, chans = field_ref.shape
-    step = 4
-    for x in range(0, size_x, step):
-        rows = slice(x * size_z, (x + step) * size_z)
-        pairs = pairs_of(field_ref.at[pl.ds(x, step)])
-        for p, pair in enumerate(pairs):
-            pairs_ref[p, rows] = pair.astype(BF)
-        for b, chunk in enumerate(block_transpose(pairs, chans // len(pairs))):
-            send_ref[b, rows] = chunk.astype(BF)
+def store_steps(chunk_ref, send_refs):
+    me = lax.axis_index("gx")
+    for t, ref in enumerate(send_refs):
+        for r in range(2):
+            ref[r] = chunk_ref[me ^ (2 * t + r)]
+
+
+def spread_kernel(field_ref, *refs):
+    send_refs, pairs_ref, chunk_ref = refs[:-2], refs[-2], refs[-1]
+    pairs = pairs_of(field_ref)
+    for p, pair in enumerate(pairs):
+        pairs_ref[p] = pair.astype(BF)
+    for b, chunk in enumerate(block_transpose(pairs, field_ref.shape[3] // len(pairs))):
+        chunk_ref[b] = chunk.astype(BF)
+    store_steps(chunk_ref, send_refs)
 
 
 def pairs_kernel(field_ref, pairs_ref):
@@ -204,15 +223,16 @@
     return jnp.concatenate([both, rest], axis=0).astype(BF)
 
 
-def transform_kernel(scale, parts_y, line_ref, column_ref, recv_ref, send_ref, *extra):
-    parts_x, tall_in, lanes = recv_ref.shape
+def transform_kernel(scale, parts_x, parts_y, line_ref, column_ref, *refs):
+    recv_refs, send_ref, extra = refs[:parts_x], refs[parts_x], refs[parts_x + 1 :]
     rows = line_ref.shape[1] // parts_x
+    own = [ref.at[k // (parts_x // 2)] for k, ref in enumerate(recv_refs)]
     if extra:
-        total = joined(recv_ref[0, rows:, :])
-        for gx in range(1, parts_x):
-            total = total + joined(recv_ref[gx, rows:, :])
-        extra[0][...] = parted(total[: lanes // 2 // parts_x])
-    data = recv_ref[:, :rows, :].reshape(parts_x * rows, lanes)
+        total = joined(own[0][rows:, :])
+        for ref in own[1:]:
+            total = total + joined(ref[rows:, :])
+        extra[0][...] = parted(total[: LANES // 2 // parts_x])
+    data = jnp.concatenate([ref[:rows, :] for ref in own], axis=0)
     lines = dot(line_ref[...], data)
     half = lines.shape[0] // 2
     lines = lines[:half] + lines[half:]
@@ -251,13 +271,13 @@
             first = scratch[pl.ds(part * rows + m, count_y, stride=2 * rows), :chans]
             second = scratch[pl.ds(part * rows + m + 1, count_y, stride=2 * rows), :chans]
             parts.append(jnp.concatenate([first, second], axis=1))
-        send_ref[:, m * chans : (m + 2) * chans] = jnp.concatenate(parts, axis=0)
+        send_ref[:, m * chans : (m + 2) * chans] = jnp.concatenate(parts, axis=0).astype(send_ref.dtype)
 
 
 def mix_kernel(forward, parts_y, recv_ref, weight_ref, *refs):
     send_ref, spec_ref, scratch = refs[-3:]
     if len(refs) == 4:
-        send_ref[:, WIDE:] = refs[0][...].astype(F32)
+        send_ref[:, WIDE:] = refs[0][...]
     size_x, size_y, size_z, _, chans, _ = weight_ref.shape
     rows = size_x * size_z
     spectra = block_transpose(sum_parts(recv_ref, parts_y), chans // size_y)
@@ -308,10 +328,11 @@
         send_ref[EXTRA:, WIDE:] = jnp.zeros((send_ref.shape[0] - EXTRA, LANES), BF)
     data = jnp.concatenate([refs[s][:, :WIDE] for s in range(steps)], axis=0)
     high = data.astype(BF)
-    low = (data - high.astype(F32)).astype(BF)
     lines = dot(table_ref[...], high)
     half = lines.shape[0] // 2
-    lines = lines[:half] + lines[half:] + dot(table_ref[:half, :], low)
+    lines = lines[:half] + lines[half:]
+    if data.dtype == F32:
+        lines = lines + dot(table_ref[:half, :], (data - high.astype(F32)).astype(BF))
     size_y = half // 2
     count = WIDE // chans
     for m in range(0, count, 2):
@@ -343,8 +364,10 @@
 
 
 def point_kernel(scale, table_ref, *refs):
-    conv_ref, field_ref, cot_ref, act_ref, slope_ref, send_ref = refs[-6:]
-    cells = cells_of(table_ref, refs[:-6], scale)
+    recv_refs, refs = refs[: 2 * SIDES], refs[2 * SIDES :]
+    conv_ref, field_ref, cot_ref, act_ref, slope_ref = refs[:5]
+    send_refs, chunk_ref = refs[5:-1], refs[-1]
+    cells = cells_of(table_ref, recv_refs, scale)
     count = field_ref.shape[0]
     slopes = []
     grad = jnp.zeros((LANES, LANES), F32)
@@ -363,8 +386,9 @@
     grad = grad[:chans, :chans] + grad[chans:, chans:]
     block = chans // count
     for b, chunk in enumerate(block_transpose(slopes, block)):
-        send_ref[b, :rows, :] = chunk.astype(BF)
-        send_ref[b, rows:, :] = parted(grad[b * block : (b + 1) * block])
+        chunk_ref[b, :rows, :] = chunk.astype(BF)
+        chunk_ref[b, rows:, :] = parted(grad[b * block : (b + 1) * block])
+    store_steps(chunk_ref, send_refs)
 
 
 def last_kernel(scale, table_ref, *refs):
@@ -381,10 +405,11 @@
 
 
 def outer_kernel(spec_ref, back_ref, out_ref):
-    size_x, size_y, size_z, _, chans, _ = out_ref.shape
-    rows = size_x * size_z
+    _, size_y, size_z, _, chans, _ = out_ref.shape
+    rows = back_ref.shape[1]
     first = lax.broadcasted_iota(jnp.int32, back_ref.shape[1:], 1) < chans
     mode = lax.broadcasted_iota(jnp.int32, (6 * rows, chans), 0) % rows
+    start = pl.program_id(0) * size_z
     for ky in range(size_y):
         back, spec = back_ref[ky], spec_ref[ky]
         turned = pltpu.roll(back, chans, 1)
@@ -395,9 +420,9 @@
         right_low = (right - right_high.astype(F32)).astype(BF)
         lefts = jnp.concatenate([left_high, left_high, left_low], axis=1)
         rights = jnp.concatenate([right_high, right_low, right_high], axis=0)
-        for m in range(rows):
-            own = jnp.where(mode == m, rights, jnp.zeros_like(rights))
-            out_ref[m // size_z, ky, m % size_z] = dot(lefts, own).reshape(2, chans, chans)
+        for m in range(size_z):
+            own = jnp.where(mode == start + m, rights, jnp.zeros_like(rights))
+            out_ref[0, ky, m] = dot(lefts, own).reshape(2, chans, chans)
 
 
 def call(kernel, outs, *args, scratch=()):
@@ -428,10 +453,11 @@
     first = 1.0 / math.sqrt(length_x * length_y * size_z)
     second = 1.0 / math.sqrt(modes_x.shape[0] * modes_y.shape[0] * count_z)
 
-    send, field = call(
+    *send, field = call(
         spread_kernel,
-        (sds((parts_x, cells, LANES), BF), sds((half_y, cells, LANES), BF)),
+        [sds((2, cells, LANES), BF)] * SIDES + [sds((half_y, cells, LANES), BF)],
         features,
+        scratch=[pltpu.VMEM((parts_x, cells, LANES), BF)],
     )
     cot = call(pairs_kernel, sds((half_y, cells, LANES), BF), cotangent)
     outside = pl.BlockSpec(memory_space=pltpu.HBM)
@@ -457,19 +483,33 @@
         compiler_params=pltpu.CompilerParams(vmem_limit_bytes=16 * 2**20),
     )(*(pltpu.with_memory_space_constraint(x, pltpu.HBM) for x in (modes_x, modes_y, modes_z, conv_weight)), spectral_weight)
 
-    def to_modes(send, factor, extra):
-        recv = lax.all_to_all(send, "gx", 0, 0, tiled=True)
+    def cross(pieces, beside=None):
+        pieces = pieces[:1] + [
+            lax.ppermute(piece, "gx", [(i, i ^ 2 * t) for i in range(parts_x)])
+            for t, piece in enumerate(pieces)
+            if t
+        ]
+        if beside is not None:
+            pieces[-1], beside = lax.optimization_barrier((pieces[-1], beside))
+        swap = [(i, i ^ 1) for i in range(parts_x)]
+        pieces = pieces + [lax.ppermute(piece, "gx", swap) for piece in pieces]
+        return pieces, beside
+
+    def to_modes(send, factor, extra, tables):
         outs = [sds((parts_x * parts_y, modes, LANES), BF)]
         if extra:
             outs.append(sds((EXTRA, LANES), BF))
-        send, *rest = call(bind(transform_kernel, factor, parts_y), outs, line_table, column_table, recv)
-        return lax.all_to_all(send, ("gx", "gy"), 0, 0, tiled=True), rest
+        kernel = bind(transform_kernel, factor, parts_x, parts_y)
+        pieces, ready = cross(send, None if extra else tables)
+        tables = tables if ready is None else ready
+        send, *rest = call(kernel, outs, *tables, *pieces)
+        return lax.all_to_all(send, ("gx", "gy"), 0, 0, tiled=True), rest, tables
 
     def mix(recv, forward, rest):
         return call(
             bind(mix_kernel, forward, parts_y),
             (
-                sds((2 * local_y, WIDE + len(rest) * LANES), F32),
+                sds((2 * local_y, WIDE + len(rest) * LANES), F32 if forward else BF),
                 sds((local_y, modes, LANES), F32),
             ),
             recv,
@@ -492,31 +532,36 @@
             *pieces,
             scratch=[pltpu.VMEM((modes * 2 * rows_y, LANES), F32)],
         )
-        pieces = [lines]
-        for step in range(2, parts_x, 2):
-            pieces.append(lax.ppermute(lines, "gx", [(i, i ^ step) for i in range(parts_x)]))
-        swap = [(i, i ^ 1) for i in range(parts_x)]
-        return pieces + [lax.ppermute(piece, "gx", swap) for piece in pieces], beside
-
-    recv, _ = to_modes(send, first, False)
+        return cross([lines] * SIDES)[0], beside
+
+
+    recv, _, tables = to_modes(send, first, False, (line_table, column_table))
     send, spec = mix(recv, True, [])
     pieces, _ = to_lines(send)
-    activation, slope, send = call(
+    activation, slope, *send = call(
         bind(point_kernel, second),
         (
             sds(features.shape, BF),
             sds((half_y, cells, LANES), BF),
-            sds((parts_x, cells + EXTRA, LANES), BF),
-        ),
+        )
+        + (sds((2, cells + EXTRA, LANES), BF),) * SIDES,
         line_back,
         *pieces,
         conv_pair,
         field,
         cot,
-    )
-    recv, rest = to_modes(send, second, True)
+        scratch=[pltpu.VMEM((parts_x, cells + EXTRA, LANES), BF)],
+    )
+    recv, rest, _ = to_modes(send, second, True, tables)
     send, back = mix(recv, False, rest)
-    grad_spectral = call(outer_kernel, sds(spectral_weight.shape, F32), spec, back)
+    grad_spectral = pl.pallas_call(
+        outer_kernel,
+        grid=(local_x,),
+        in_specs=[pl.BlockSpec(spec.shape, lambda i: (0, 0, 0))] * 2,
+        out_specs=pl.BlockSpec((1,) + spectral_weight.shape[1:], lambda i: (i, 0, 0, 0, 0, 0)),
+        out_shape=sds(spectral_weight.shape, F32),
+        compiler_params=pltpu.CompilerParams(vmem_limit_bytes=16 * 2**20),
+    )(spec, back)
     pieces, grad_spectral = to_lines(send, grad_spectral)
     grad_features, grad_conv = call(
         bind(last_kernel, first),

time: 92.3 us -> 88.3 us (0.957)
  blocking collectives: 32.5 us -> 25.3 us
  starting transfers between devices: 17.3 us -> 21.3 us
  waiting for transfers between devices: 17.4 us -> 20.3 us
  local copies, waits for them, and re-layouts: 5.41 us -> 3.23 us
  Pallas kernels: 18.5 us -> 17.1 us
    ppermute x14 -> x28, starting transfers between devices: 7.24 us -> 16.4 us  [the longest x12 15.2 us: cross(): lax.ppermute(piece, 'gx', [(i, i ^ 2 * t) for i in range(parts_x)])]
    all_to_all x3 -> x2, blocking collectives: 32.5 us -> 25.3 us  [to_modes(): return (lax.all_to_all(send, ('gx', 'gy'), 0, 0, tiled=True), rest, tables)]
    pallas_call x11 -> x10, Pallas kernels: 15.8 us -> 9.5 us  [call(): pl.pallas_call(kernel, out_shape=outs, scratch_shapes=list(scratch), comp...]
    ppermute x14 -> x28, waiting for transfers between devices: 8.33 us -> 14.3 us  [the longest x12 9.79 us: cross(): lax.ppermute(piece, 'gx', [(i, i ^ 2 * t) for i in range(parts_x)])]
    pallas_call x0 -> x1, Pallas kernels: none -> 5.61 us  [fast(): pl.pallas_call(outer_kernel, grid=(local_x,), in_specs=[pl.BlockSpec(spec...]
    all_to_all x1 -> x0, starting transfers between devices: 5.17 us -> none  [to_modes(): recv = lax.all_to_all(send, 'gx', 0, 0, tiled=True)]
    unnamed x10 -> x8, local copies, waits for them, and re-layouts: 5.41 us -> 3.23 us
    all_to_all x1 -> x0, waiting for transfers between devices: 2.01 us -> none  [to_modes(): recv = lax.all_to_all(send, 'gx', 0, 0, tiled=True)]
  transfers between devices with their start and end apart: 21 -> 34, of which waited for: 15 -> 21; matrix products, arithmetic and copies ran while one was open for 0% -> 0% of each run, Pallas kernels for 9% -> 9%
where the time goes in v2:
time: 88.3 us; the launch traced here: 88 us
  blocking collectives  25.3 us (29%)
  starting transfers between devices  21.3 us (24%)
  waiting for transfers between devices  20.3 us (23%)
  Pallas kernels  17.1 us (19%)
  local copies, waits for them, and re-layouts  3.23 us (4%)
    all_to_all x2, blocking collectives, to_modes(): return (lax.all_to_all(send, ('gx', 'gy'), 0, 0, tiled=True), rest, tables)  25.3 us
    ppermute x12, starting transfers between devices, cross(): lax.ppermute(piece, 'gx', [(i, i ^ 2 * t) for i in range(parts_x)])  15.2 us
    ppermute x12, waiting for transfers between devices, cross(): lax.ppermute(piece, 'gx', [(i, i ^ 2 * t) for i in range(parts_x)])  9.79 us
    pallas_call x10, Pallas kernels, call(): pl.pallas_call(kernel, out_shape=outs, scratch_shapes=list(scratch), comp...  9.5 us
    ppermute x6, waiting for transfers between devices, to_lines(): pieces.append(lax.ppermute(send, 'gy', ring))  6.01 us
    pallas_call x1, Pallas kernels, fast(): pl.pallas_call(outer_kernel, grid=(local_x,), in_specs=[pl.BlockSpec(spec...  5.61 us
    ppermute x6, starting transfers between devices, to_lines(): pieces.append(lax.ppermute(send, 'gy', ring))  4.9 us
    ppermute x16, waiting for transfers between devices, cross(): pieces = pieces + [lax.ppermute(piece, 'gx', swap) for piece in pieces]  4.51 us
  transfers between devices with their start and end apart: 34, of which 21 were waited for; matrix products, arithmetic and copies ran while one was open for 0% of the time, Pallas kernels for 9%

profile of v2, /device:TPU:0, one launch (start us, length us, event | category | flops | bytes accessed | tf_op | source)
XLA Modules:
  0.0 88.0 jit_solution(6717617165049835970)
XLA Ops:
  2.1 4.0 %collective-permute-start = (bf16[2,128,128]{2,1,0:T(8,128)(2,1)S(1)}, bf16[2,128,128]{2,1,0:T(8,128)(2,1)S(1)}, u32[]{:S(2)}, u32[]{:S(2)}) collective-permute-start(bf16[2,128,128]{2,1,0:T(8,128)(2,1)S(1)} %get-tuple-element.36), channel_id=1, source_target_pairs={{0,24},{4,28},{8,16},{12,20},{16,8},{20,12},{24,0},{28,4},{1,25},{... | collective-permute-start | bytes 196616 | tf_op jit(solution)/shard_map/ppermute | solution.py:488
  6.7 2.2 %copy-done = bf16[4,8,4,2,64,64]{5,4,3,2,1,0:T(8,128)(2,1)S(1)} copy-done((bf16[4,8,4,2,64,64]{5,4,3,2,1,0:T(8,128)(2,1)S(1)}, bf16[4,8,4,2,64,64]{5,4,3,2,1,0:T(8,128)(2,1)}, u32[]{:S(2)}) %copy-start) | copy-done | bytes 2097176
  8.9 2.0 %shard_map.102 = (bf16[512,1024]{1,0:T(8,128)(2,1)S(1)}, bf16[512,512]{1,0:T(8,128)(2,1)S(1)}, bf16[64,64]{1,0:T(8,128)(2,1)S(1)}, bf16[256,256]{1,0:T(8,128)(2,...) custom-call(s32[32]{0:T(128)} %refs_0_.1, s32[32]{0:T(128)} %refs_1_.3, s32[4]{0:T(128)} %refs_2_.1, ...), custom_call_target="tpu_custom_call" | custom-call | tf_op jit(solution)/shard_map/pallas_call | solution.py:465
  13.8 14.5 %all_to_all.10.refs_0_ = bf16[32,16,128]{2,1,0:T(8,128)(2,1)S(1)} all-to-all(bf16[32,16,128]{2,1,0:T(8,128)(2,1)S(1)} %shard_map.104), channel_id=1, replica_groups=mesh['gx'=8,'gy'=4] {'gx','gy'}, dimensions={0} | all-to-all | bytes 262144 | tf_op jit(solution)/shard_map/all_to_all | solution.py:506
  28.2 2.0 %shard_map.105 = (f32[16,1024]{1,0:T(8,128)S(1)}, f32[8,16,128]{2,1,0:T(8,128)S(1)}) custom-call(bf16[32,16,128]{2,1,0:T(8,128)(2,1)S(1)} %all_to_all.10.refs_0_, bf16[4,8,4,2,64,64]{5,4,3,2,1,0:T(8,128)(2,1)S(1)} %copy-done.1), custom_call_target="tpu_custom_call" | custom-call | tf_op jit(solution)/shard_map/pallas_call | solution.py:430
  30.2 1.3 %collective-permute-start.9 = (f32[16,1024]{1,0:T(8,128)S(1)}, f32[16,1024]{1,0:T(8,128)S(1)}, u32[]{:S(2)}, u32[]{:S(2)}) collective-permute-start(f32[16,1024]{1,0:T(8,128)S(1)} %get-tuple-element.45.refs_0_), channel_id=1, source_target_pairs={{0,3},{1,0},{2,1},{3,2},{4,7},{5,4},{6,5},{7,6},{8,11},{9,8},{10,9... | collective-permute-start | bytes 196616 | tf_op jit(solution)/shard_map/ppermute | solution.py:525
  32.7 2.1 %collective-permute-done.9.refs_3_ = f32[16,1024]{1,0:T(8,128)S(1)} collective-permute-done((f32[16,1024]{1,0:T(8,128)S(1)}, f32[16,1024]{1,0:T(8,128)S(1)}, u32[]{:S(2)}, u32[]{:S(2)}) %collective-permute-start.9) | collective-permute-done | bytes 65568 | tf_op jit(solution)/shard_map/ppermute | solution.py:525
  34.8 3.9 %collective-permute-done.8.refs_2_ = f32[16,1024]{1,0:T(8,128)S(1)} collective-permute-done((f32[16,1024]{1,0:T(8,128)S(1)}, f32[16,1024]{1,0:T(8,128)S(1)}, u32[]{:S(2)}, u32[]{:S(2)}) %collective-permute-start.8) | collective-permute-done | bytes 65568 | tf_op jit(solution)/shard_map/ppermute | solution.py:525
  39.9 1.5 %collective-permute-start.11 = (bf16[32,1024]{1,0:T(8,128)(2,1)S(1)}, bf16[32,1024]{1,0:T(8,128)(2,1)S(1)}, u32[]{:S(2)}, u32[]{:S(2)}) collective-permute-start(bf16[32,1024]{1,0:T(8,128)(2,1)S(1)} %shard_map.106.refs_1_), channel_id=1, source_target_pairs={{0,16},{4,20},{8,24},{12,28},{16,0},{20,4},{24,8},{28,12},{1,17},{... | collective-permute-start | bytes 196616 | tf_op jit(solution)/shard_map/ppermute | solution.py:488
  41.5 1.2 %collective-permute-start.10 = (bf16[32,1024]{1,0:T(8,128)(2,1)S(1)}, bf16[32,1024]{1,0:T(8,128)(2,1)S(1)}, u32[]{:S(2)}, u32[]{:S(2)}) collective-permute-start(bf16[32,1024]{1,0:T(8,128)(2,1)S(1)} %shard_map.106.refs_1_), channel_id=1, source_target_pairs={{0,8},{4,12},{8,0},{12,4},{16,24},{20,28},{24,16},{28,20},{1,9},{5... | collective-permute-start | bytes 196616 | tf_op jit(solution)/shard_map/ppermute | solution.py:488
  42.7 1.8 %collective-permute-done.12.refs_4_ = bf16[32,1024]{1,0:T(8,128)(2,1)S(1)} collective-permute-done((bf16[32,1024]{1,0:T(8,128)(2,1)S(1)}, bf16[32,1024]{1,0:T(8,128)(2,1)S(1)}, u32[]{:S(2)}, u32[]{:S(2)}) %collective-permute-start.12) | collective-permute-done | bytes 65568 | tf_op jit(solution)/shard_map/ppermute | solution.py:488
  47.0 1.6 %shard_map.108 = (bf16[16,16,8,64]{3,2,1,0:T(8,128)(2,1)}, bf16[8,128,128]{2,1,0:T(8,128)(2,1)S(1)}, bf16[2,144,128]{2,1,0:T(8,128)(2,1)S(1)}, bf16[2,144,128]{2...) custom-call(bf16[256,256]{1,0:T(8,128)(2,1)S(1)} %get-tuple-element.34.refs_0_, ...), custom_call_target="tpu_custom_call" | custom-call | tf_op jit(solution)/shard_map/pallas_call | solution.py:430
  48.6 1.2 %collective-permute-start.17 = (bf16[2,144,128]{2,1,0:T(8,128)(2,1)S(1)}, bf16[2,144,128]{2,1,0:T(8,128)(2,1)S(1)}, u32[]{:S(2)}, u32[]{:S(2)}) collective-permute-start(bf16[2,144,128]{2,1,0:T(8,128)(2,1)S(1)} %get-tuple-element.50), channel_id=1, source_target_pairs={{0,8},{4,12},{8,0},{12,4},{16,24},{20,28},{24,16},{28,20},{1,9},{5... | collective-permute-start | bytes 221192 | tf_op jit(solution)/shard_map/ppermute | solution.py:488
  50.6 1.4 %collective-permute-start.19 = (bf16[2,144,128]{2,1,0:T(8,128)(2,1)S(1)}, bf16[2,144,128]{2,1,0:T(8,128)(2,1)S(1)}, u32[]{:S(2)}, u32[]{:S(2)}) collective-permute-start(bf16[2,144,128]{2,1,0:T(8,128)(2,1)S(1)} %get-tuple-element.52), channel_id=1, source_target_pairs={{0,24},{4,28},{8,16},{12,20},{16,8},{20,12},{24,0},{28,4},{1,25},{... | collective-permute-start | bytes 221192 | tf_op jit(solution)/shard_map/ppermute | solution.py:488
  52.9 2.0 %collective-permute-done.18.refs_4_ = bf16[2,144,128]{2,1,0:T(8,128)(2,1)S(1)} collective-permute-done((bf16[2,144,128]{2,1,0:T(8,128)(2,1)S(1)}, bf16[2,144,128]{2,1,0:T(8,128)(2,1)S(1)}, u32[]{:S(2)}, u32[]{:S(2)}) %collective-permute-start.18) | collective-permute-done | bytes 73760 | tf_op jit(solution)/shard_map/ppermute | solution.py:488
  58.0 10.8 %all_to_all.11.refs_0_ = bf16[32,16,128]{2,1,0:T(8,128)(2,1)S(1)} all-to-all(bf16[32,16,128]{2,1,0:T(8,128)(2,1)S(1)} %get-tuple-element.53), channel_id=1, replica_groups=mesh['gx'=8,'gy'=4] {'gx','gy'}, dimensions={0} | all-to-all | bytes 262144 | tf_op jit(solution)/shard_map/all_to_all | solution.py:506
  68.8 1.6 %shard_map.110 = (bf16[16,1152]{1,0:T(8,128)(2,1)S(1)}, f32[8,16,128]{2,1,0:T(8,128)S(1)}) custom-call(bf16[32,16,128]{2,1,0:T(8,128)(2,1)S(1)} %all_to_all.11.refs_0_, bf16[4,8,4,2,64,64]{5,4,3,2,1,0:T(8,128)(2,1)S(1)} %copy-done.1, bf16[16,128]{1,0:T(8,128)(2,1)S(1)} %get-tuple-element.54.refs_2_), custom_call_target="tpu_custom_call" | custom-call | tf_op jit(solution)/shard_map/pallas_call | solution.py:430
  70.4 1.3 %collective-permute-start.26 = (bf16[16,1152]{1,0:T(8,128)(2,1)S(1)}, bf16[16,1152]{1,0:T(8,128)(2,1)S(1)}, u32[]{:S(2)}, u32[]{:S(2)}) collective-permute-start(bf16[16,1152]{1,0:T(8,128)(2,1)S(1)} %get-tuple-element.55.refs_0_), channel_id=1, source_target_pairs={{0,3},{1,0},{2,1},{3,2},{4,7},{5,4},{6,5},{7,6},{8,11},{9,8},{10,9... | collective-permute-start | bytes 110600 | tf_op jit(solution)/shard_map/ppermute | solution.py:525
  71.7 1.2 %collective-permute-start.24 = (bf16[16,1152]{1,0:T(8,128)(2,1)S(1)}, bf16[16,1152]{1,0:T(8,128)(2,1)S(1)}, u32[]{:S(2)}, u32[]{:S(2)}) collective-permute-start(bf16[16,1152]{1,0:T(8,128)(2,1)S(1)} %get-tuple-element.55.refs_0_), channel_id=1, source_target_pairs={{0,1},{1,2},{2,3},{3,0},{4,5},{5,6},{6,7},{7,4},{8,9},{9,10},{10,1... | collective-permute-start | bytes 110600 | tf_op jit(solution)/shard_map/ppermute | solution.py:525
  72.8 5.6 %shard_map.111 = f32[4,8,4,2,64,64]{5,4,3,2,1,0:T(8,128)} custom-call(f32[8,16,128]{2,1,0:T(8,128)S(1)} %get-tuple-element.56.spec_ref, f32[8,16,128]{2,1,0:T(8,128)S(1)} %get-tuple-element.57.back_ref), custom_call_target="tpu_custom_call" | custom-call | tf_op jit(solution)/shard_map/pallas_call | solution.py:557
  79.7 1.3 %collective-permute-start.28 = (bf16[32,1152]{1,0:T(8,128)(2,1)S(1)}, bf16[32,1152]{1,0:T(8,128)(2,1)S(1)}, u32[]{:S(2)}, u32[]{:S(2)}) collective-permute-start(bf16[32,1152]{1,0:T(8,128)(2,1)S(1)} %shard_map.112.refs_1_), channel_id=1, source_target_pairs={{0,16},{4,20},{8,24},{12,28},{16,0},{20,4},{24,8},{28,12},{1,17},{... | collective-permute-start | bytes 221192 | tf_op jit(solution)/shard_map/ppermute | solution.py:488
  81.1 1.3 %collective-permute-start.27 = (bf16[32,1152]{1,0:T(8,128)(2,1)S(1)}, bf16[32,1152]{1,0:T(8,128)(2,1)S(1)}, u32[]{:S(2)}, u32[]{:S(2)}) collective-permute-start(bf16[32,1152]{1,0:T(8,128)(2,1)S(1)} %shard_map.112.refs_1_), channel_id=1, source_target_pairs={{0,8},{4,12},{8,0},{12,4},{16,24},{20,28},{24,16},{28,20},{1,9},{5... | collective-permute-start | bytes 221192 | tf_op jit(solution)/shard_map/ppermute | solution.py:488
  82.4 1.9 %collective-permute-done.29.refs_4_ = bf16[32,1152]{1,0:T(8,128)(2,1)S(1)} collective-permute-done((bf16[32,1152]{1,0:T(8,128)(2,1)S(1)}, bf16[32,1152]{1,0:T(8,128)(2,1)S(1)}, u32[]{:S(2)}, u32[]{:S(2)}) %collective-permute-start.29) | collective-permute-done | bytes 73760 | tf_op jit(solution)/shard_map/ppermute | solution.py:488
  86.7 1.3 %shard_map.113 = (bf16[16,16,8,64]{3,2,1,0:T(8,128)(2,1)}, f32[64,64]{1,0:T(8,128)}) custom-call(bf16[256,256]{1,0:T(8,128)(2,1)S(1)} %get-tuple-element.34.refs_0_, bf16[32,1152]{1,0:T(8,128)(2,1)S(1)} %shard_map.112.refs_1_, bf16[32,1152]{1,0:T(8,128)(2,1)S(1)} %collective-permute-done.27.refs_2_, bf16[32,1152]{1,0:T(8,128)(2,1)S(1)} %collective-permute-done.28.refs_3_, ...), custom_call_target="tpu_custom_call" | custom-call | tf_op jit(solution)/shard_map/pallas_call | solution.py:430
  (66 shorter events, 18.3 us)
Async XLA Ops:
  2.1 8.8 %collective-permute-start = (bf16[2,128,128]{2,1,0:T(8,128)(2,1)S(1)}, bf16[2,128,128]{2,1,0:T(8,128)(2,1)S(1)}, u32[]{:S(2)}, u32[]{:S(2)}) collective-permute-start(bf16[2,128,128]{2,1,0:T(8,128)(2,1)S(1)} %get-tuple-element.36), channel_id=1, source_target_pairs={{0,24},{4,28},{8,16},{12,20},{16,8},{20,12},{24,0},{28,4},{1,25},{... | collective-permute-start | bytes 196616 | tf_op jit(solution)/shard_map/ppermute | solution.py:488
  6.1 4.9 %collective-permute-start.1 = (bf16[2,128,128]{2,1,0:T(8,128)(2,1)S(1)}, bf16[2,128,128]{2,1,0:T(8,128)(2,1)S(1)}, u32[]{:S(2)}, u32[]{:S(2)}) collective-permute-start(bf16[2,128,128]{2,1,0:T(8,128)(2,1)S(1)} %get-tuple-element.42), channel_id=1, source_target_pairs={{0,8},{4,12},{8,0},{12,4},{16,24},{20,28},{24,16},{28,20},{1,9},{5... | collective-permute-start | bytes 196616 | tf_op jit(solution)/shard_map/ppermute | solution.py:488
  6.6 4.9 %collective-permute-start.2 = (bf16[2,128,128]{2,1,0:T(8,128)(2,1)S(1)}, bf16[2,128,128]{2,1,0:T(8,128)(2,1)S(1)}, u32[]{:S(2)}, u32[]{:S(2)}) collective-permute-start(bf16[2,128,128]{2,1,0:T(8,128)(2,1)S(1)} %get-tuple-element.43), channel_id=1, source_target_pairs={{0,16},{4,20},{8,24},{12,28},{16,0},{20,4},{24,8},{28,12},{1,17},{... | collective-permute-start | bytes 196616 | tf_op jit(solution)/shard_map/ppermute | solution.py:488
  6.7 5.3 %collective-permute-start.3 = (bf16[2,128,128]{2,1,0:T(8,128)(2,1)S(1)}, bf16[2,128,128]{2,1,0:T(8,128)(2,1)S(1)}, u32[]{:S(2)}, u32[]{:S(2)}) collective-permute-start(bf16[2,128,128]{2,1,0:T(8,128)(2,1)S(1)} %get-tuple-element.41.refs_2_), channel_id=1, source_target_pairs={{0,4},{4,0},{8,12},{12,8},{16,20},{20,16},{24,28},{28,24},{1,5},{5... | collective-permute-start | bytes 196616 | tf_op jit(solution)/shard_map/ppermute | solution.py:495
  10.9 1.5 %collective-permute-start.4 = (bf16[2,128,128]{2,1,0:T(8,128)(2,1)S(1)}, bf16[2,128,128]{2,1,0:T(8,128)(2,1)S(1)}, u32[]{:S(2)}, u32[]{:S(2)}) collective-permute-start(bf16[2,128,128]{2,1,0:T(8,128)(2,1)S(1)} %collective-permute-done.1.refs_3_), channel_id=1, source_target_pairs={{0,4},{4,0},{8,12},{12,8},{16,20},{20,16},{24,28},{28,24},{1,5},{5... | collective-permute-start | bytes 196616 | tf_op jit(solution)/shard_map/ppermute | solution.py:495
  30.2 4.6 %collective-permute-start.9 = (f32[16,1024]{1,0:T(8,128)S(1)}, f32[16,1024]{1,0:T(8,128)S(1)}, u32[]{:S(2)}, u32[]{:S(2)}) collective-permute-start(f32[16,1024]{1,0:T(8,128)S(1)} %get-tuple-element.45.refs_0_), channel_id=1, source_target_pairs={{0,3},{1,0},{2,1},{3,2},{4,7},{5,4},{6,5},{7,6},{8,11},{9,8},{10,9... | collective-permute-start | bytes 196616 | tf_op jit(solution)/shard_map/ppermute | solution.py:525
  31.5 7.2 %collective-permute-start.8 = (f32[16,1024]{1,0:T(8,128)S(1)}, f32[16,1024]{1,0:T(8,128)S(1)}, u32[]{:S(2)}, u32[]{:S(2)}) collective-permute-start(f32[16,1024]{1,0:T(8,128)S(1)} %get-tuple-element.45.refs_0_), channel_id=1, source_target_pairs={{0,2},{1,3},{2,0},{3,1},{4,6},{5,7},{6,4},{7,5},{8,10},{9,11},{10,... | collective-permute-start | bytes 196616 | tf_op jit(solution)/shard_map/ppermute | solution.py:525
  31.5 7.2 %collective-permute-start.7 = (f32[16,1024]{1,0:T(8,128)S(1)}, f32[16,1024]{1,0:T(8,128)S(1)}, u32[]{:S(2)}, u32[]{:S(2)}) collective-permute-start(f32[16,1024]{1,0:T(8,128)S(1)} %get-tuple-element.45.refs_0_), channel_id=1, source_target_pairs={{0,1},{1,2},{2,3},{3,0},{4,5},{5,6},{6,7},{7,4},{8,9},{9,10},{10,1... | collective-permute-start | bytes 196616 | tf_op jit(solution)/shard_map/ppermute | solution.py:525
  39.1 5.3 %collective-permute-start.12 = (bf16[32,1024]{1,0:T(8,128)(2,1)S(1)}, bf16[32,1024]{1,0:T(8,128)(2,1)S(1)}, u32[]{:S(2)}, u32[]{:S(2)}) collective-permute-start(bf16[32,1024]{1,0:T(8,128)(2,1)S(1)} %shard_map.106.refs_1_), channel_id=1, source_target_pairs={{0,24},{4,28},{8,16},{12,20},{16,8},{20,12},{24,0},{28,4},{1,25},{... | collective-permute-start | bytes 196616 | tf_op jit(solution)/shard_map/ppermute | solution.py:488
  39.9 5.0 %collective-permute-start.11 = (bf16[32,1024]{1,0:T(8,128)(2,1)S(1)}, bf16[32,1024]{1,0:T(8,128)(2,1)S(1)}, u32[]{:S(2)}, u32[]{:S(2)}) collective-permute-start(bf16[32,1024]{1,0:T(8,128)(2,1)S(1)} %shard_map.106.refs_1_), channel_id=1, source_target_pairs={{0,16},{4,20},{8,24},{12,28},{16,0},{20,4},{24,8},{28,12},{1,17},{... | collective-permute-start | bytes 196616 | tf_op jit(solution)/shard_map/ppermute | solution.py:488
  41.5 4.3 %collective-permute-start.10 = (bf16[32,1024]{1,0:T(8,128)(2,1)S(1)}, bf16[32,1024]{1,0:T(8,128)(2,1)S(1)}, u32[]{:S(2)}, u32[]{:S(2)}) collective-permute-start(bf16[32,1024]{1,0:T(8,128)(2,1)S(1)} %shard_map.106.refs_1_), channel_id=1, source_target_pairs={{0,8},{4,12},{8,0},{12,4},{16,24},{20,28},{24,16},{28,20},{1,9},{5... | collective-permute-start | bytes 196616 | tf_op jit(solution)/shard_map/ppermute | solution.py:488
  42.7 3.2 %collective-permute-start.13 = (bf16[32,1024]{1,0:T(8,128)(2,1)S(1)}, bf16[32,1024]{1,0:T(8,128)(2,1)S(1)}, u32[]{:S(2)}, u32[]{:S(2)}) collective-permute-start(bf16[32,1024]{1,0:T(8,128)(2,1)S(1)} %shard_map.106.refs_1_), channel_id=1, source_target_pairs={{0,4},{4,0},{8,12},{12,8},{16,20},{20,16},{24,28},{28,24},{1,5},{5... | collective-permute-start | bytes 196616 | tf_op jit(solution)/shard_map/ppermute | solution.py:495
  48.6 4.4 %collective-permute-start.17 = (bf16[2,144,128]{2,1,0:T(8,128)(2,1)S(1)}, bf16[2,144,128]{2,1,0:T(8,128)(2,1)S(1)}, u32[]{:S(2)}, u32[]{:S(2)}) collective-permute-start(bf16[2,144,128]{2,1,0:T(8,128)(2,1)S(1)} %get-tuple-element.50), channel_id=1, source_target_pairs={{0,8},{4,12},{8,0},{12,4},{16,24},{20,28},{24,16},{28,20},{1,9},{5... | collective-permute-start | bytes 221192 | tf_op jit(solution)/shard_map/ppermute | solution.py:488
  49.8 5.1 %collective-permute-start.18 = (bf16[2,144,128]{2,1,0:T(8,128)(2,1)S(1)}, bf16[2,144,128]{2,1,0:T(8,128)(2,1)S(1)}, u32[]{:S(2)}, u32[]{:S(2)}) collective-permute-start(bf16[2,144,128]{2,1,0:T(8,128)(2,1)S(1)} %get-tuple-element.51), channel_id=1, source_target_pairs={{0,16},{4,20},{8,24},{12,28},{16,0},{20,4},{24,8},{28,12},{1,17},{... | collective-permute-start | bytes 221192 | tf_op jit(solution)/shard_map/ppermute | solution.py:488
  50.6 5.3 %collective-permute-start.19 = (bf16[2,144,128]{2,1,0:T(8,128)(2,1)S(1)}, bf16[2,144,128]{2,1,0:T(8,128)(2,1)S(1)}, u32[]{:S(2)}, u32[]{:S(2)}) collective-permute-start(bf16[2,144,128]{2,1,0:T(8,128)(2,1)S(1)} %get-tuple-element.52), channel_id=1, source_target_pairs={{0,24},{4,28},{8,16},{12,20},{16,8},{20,12},{24,0},{28,4},{1,25},{... | collective-permute-start | bytes 221192 | tf_op jit(solution)/shard_map/ppermute | solution.py:488
  52.1 3.8 %collective-permute-start.20 = (bf16[2,144,128]{2,1,0:T(8,128)(2,1)S(1)}, bf16[2,144,128]{2,1,0:T(8,128)(2,1)S(1)}, u32[]{:S(2)}, u32[]{:S(2)}) collective-permute-start(bf16[2,144,128]{2,1,0:T(8,128)(2,1)S(1)} %get-tuple-element.49.refs_2_), channel_id=1, source_target_pairs={{0,4},{4,0},{8,12},{12,8},{16,20},{20,16},{24,28},{28,24},{1,5},{5... | collective-permute-start | bytes 221192 | tf_op jit(solution)/shard_map/ppermute | solution.py:495
  52.9 2.9 %collective-permute-start.21 = (bf16[2,144,128]{2,1,0:T(8,128)(2,1)S(1)}, bf16[2,144,128]{2,1,0:T(8,128)(2,1)S(1)}, u32[]{:S(2)}, u32[]{:S(2)}) collective-permute-start(bf16[2,144,128]{2,1,0:T(8,128)(2,1)S(1)} %collective-permute-done.17.refs_3_), channel_id=1, source_target_pairs={{0,4},{4,0},{8,12},{12,8},{16,20},{20,16},{24,28},{28,24},{1,5},{5... | collective-permute-start | bytes 221192 | tf_op jit(solution)/shard_map/ppermute | solution.py:495
  70.4 8.1 %collective-permute-start.26 = (bf16[16,1152]{1,0:T(8,128)(2,1)S(1)}, bf16[16,1152]{1,0:T(8,128)(2,1)S(1)}, u32[]{:S(2)}, u32[]{:S(2)}) collective-permute-start(bf16[16,1152]{1,0:T(8,128)(2,1)S(1)} %get-tuple-element.55.refs_0_), channel_id=1, source_target_pairs={{0,3},{1,0},{2,1},{3,2},{4,7},{5,4},{6,5},{7,6},{8,11},{9,8},{10,9... | collective-permute-start | bytes 110600 | tf_op jit(solution)/shard_map/ppermute | solution.py:525
  71.6 6.8 %collective-permute-start.25 = (bf16[16,1152]{1,0:T(8,128)(2,1)S(1)}, bf16[16,1152]{1,0:T(8,128)(2,1)S(1)}, u32[]{:S(2)}, u32[]{:S(2)}) collective-permute-start(bf16[16,1152]{1,0:T(8,128)(2,1)S(1)} %get-tuple-element.55.refs_0_), channel_id=1, source_target_pairs={{0,2},{1,3},{2,0},{3,1},{4,6},{5,7},{6,4},{7,5},{8,10},{9,11},{10,... | collective-permute-start | bytes 110600 | tf_op jit(solution)/shard_map/ppermute | solution.py:525
  71.7 6.8 %collective-permute-start.24 = (bf16[16,1152]{1,0:T(8,128)(2,1)S(1)}, bf16[16,1152]{1,0:T(8,128)(2,1)S(1)}, u32[]{:S(2)}, u32[]{:S(2)}) collective-permute-start(bf16[16,1152]{1,0:T(8,128)(2,1)S(1)} %get-tuple-element.55.refs_0_), channel_id=1, source_target_pairs={{0,1},{1,2},{2,3},{3,0},{4,5},{5,6},{6,7},{7,4},{8,9},{9,10},{10,1... | collective-permute-start | bytes 110600 | tf_op jit(solution)/shard_map/ppermute | solution.py:525
  78.8 5.4 %collective-permute-start.29 = (bf16[32,1152]{1,0:T(8,128)(2,1)S(1)}, bf16[32,1152]{1,0:T(8,128)(2,1)S(1)}, u32[]{:S(2)}, u32[]{:S(2)}) collective-permute-start(bf16[32,1152]{1,0:T(8,128)(2,1)S(1)} %shard_map.112.refs_1_), channel_id=1, source_target_pairs={{0,24},{4,28},{8,16},{12,20},{16,8},{20,12},{24,0},{28,4},{1,25},{... | collective-permute-start | bytes 221192 | tf_op jit(solution)/shard_map/ppermute | solution.py:488
  79.7 5.1 %collective-permute-start.28 = (bf16[32,1152]{1,0:T(8,128)(2,1)S(1)}, bf16[32,1152]{1,0:T(8,128)(2,1)S(1)}, u32[]{:S(2)}, u32[]{:S(2)}) collective-permute-start(bf16[32,1152]{1,0:T(8,128)(2,1)S(1)} %shard_map.112.refs_1_), channel_id=1, source_target_pairs={{0,16},{4,20},{8,24},{12,28},{16,0},{20,4},{24,8},{28,12},{1,17},{... | collective-permute-start | bytes 221192 | tf_op jit(solution)/shard_map/ppermute | solution.py:488
  81.1 4.4 %collective-permute-start.27 = (bf16[32,1152]{1,0:T(8,128)(2,1)S(1)}, bf16[32,1152]{1,0:T(8,128)(2,1)S(1)}, u32[]{:S(2)}, u32[]{:S(2)}) collective-permute-start(bf16[32,1152]{1,0:T(8,128)(2,1)S(1)} %shard_map.112.refs_1_), channel_id=1, source_target_pairs={{0,8},{4,12},{8,0},{12,4},{16,24},{20,28},{24,16},{28,20},{1,9},{5... | collective-permute-start | bytes 221192 | tf_op jit(solution)/shard_map/ppermute | solution.py:488
  82.4 3.0 %collective-permute-start.30 = (bf16[32,1152]{1,0:T(8,128)(2,1)S(1)}, bf16[32,1152]{1,0:T(8,128)(2,1)S(1)}, u32[]{:S(2)}, u32[]{:S(2)}) collective-permute-start(bf16[32,1152]{1,0:T(8,128)(2,1)S(1)} %shard_map.112.refs_1_), channel_id=1, source_target_pairs={{0,4},{4,0},{8,12},{12,8},{16,20},{20,16},{24,28},{28,24},{1,5},{5... | collective-permute-start | bytes 221192 | tf_op jit(solution)/shard_map/ppermute | solution.py:495
  (14 other events, 79.5 us)

commit v3 on v2

--- a/solution.py
+++ b/solution.py
@@ -404,12 +404,12 @@
         store_pair(out_ref, p, cells[:, p * LANES : (p + 1) * LANES] + dot(slope_ref[p], conv_ref[...]))
 
 
-def outer_kernel(spec_ref, back_ref, out_ref):
-    _, size_y, size_z, _, chans, _ = out_ref.shape
-    rows = back_ref.shape[1]
+def outer_kernel(spec_ref, back_ref, out_ref, held_ref, sems):
+    size_x, size_y, size_z, _, chans, _ = held_ref.shape
+    rows = size_x * size_z
     first = lax.broadcasted_iota(jnp.int32, back_ref.shape[1:], 1) < chans
     mode = lax.broadcasted_iota(jnp.int32, (6 * rows, chans), 0) % rows
-    start = pl.program_id(0) * size_z
+    copies = []
     for ky in range(size_y):
         back, spec = back_ref[ky], spec_ref[ky]
         turned = pltpu.roll(back, chans, 1)
@@ -420,9 +420,14 @@
         right_low = (right - right_high.astype(F32)).astype(BF)
         lefts = jnp.concatenate([left_high, left_high, left_low], axis=1)
         rights = jnp.concatenate([right_high, right_low, right_high], axis=0)
-        for m in range(size_z):
-            own = jnp.where(mode == start + m, rights, jnp.zeros_like(rights))
-            out_ref[0, ky, m] = dot(lefts, own).reshape(2, chans, chans)
+        for m in range(rows):
+            own = jnp.where(mode == m, rights, jnp.zeros_like(rights))
+            held_ref[m // size_z, ky, m % size_z] = dot(lefts, own).reshape(2, chans, chans)
+        copy = pltpu.make_async_copy(held_ref.at[:, ky], out_ref.at[:, ky], sems.at[ky])
+        copy.start()
+        copies.append(copy)
+    for copy in copies:
+        copy.wait()
 
 
 def call(kernel, outs, *args, scratch=()):
@@ -464,7 +469,7 @@
     inside = pl.BlockSpec(memory_space=pltpu.VMEM)
     line_table, column_table, column_back, line_back, conv_pair, conv_turn = pl.pallas_call(
         bind(table_kernel, size_z),
-        in_specs=[outside] * 4 + [inside],
+        in_specs=[outside] * 5,
         out_shape=(
             sds((4 * modes_x.shape[0] * count_z, length_x * size_z), BF),
             sds((4 * LANES, 4 * LANES), BF),
@@ -481,7 +486,7 @@
             pltpu.SemaphoreType.DMA((4,)),
         ],
         compiler_params=pltpu.CompilerParams(vmem_limit_bytes=16 * 2**20),
-    )(*(pltpu.with_memory_space_constraint(x, pltpu.HBM) for x in (modes_x, modes_y, modes_z, conv_weight)), spectral_weight)
+    )(*(pltpu.with_memory_space_constraint(x, pltpu.HBM) for x in (modes_x, modes_y, modes_z, conv_weight, spectral_weight)))
 
     def cross(pieces, beside=None):
         pieces = pieces[:1] + [
@@ -556,10 +561,10 @@
     send, back = mix(recv, False, rest)
     grad_spectral = pl.pallas_call(
         outer_kernel,
-        grid=(local_x,),
-        in_specs=[pl.BlockSpec(spec.shape, lambda i: (0, 0, 0))] * 2,
-        out_specs=pl.BlockSpec((1,) + spectral_weight.shape[1:], lambda i: (i, 0, 0, 0, 0, 0)),
+        in_specs=[inside] * 2,
+        out_specs=outside,
         out_shape=sds(spectral_weight.shape, F32),
+        scratch_shapes=[pltpu.VMEM(spectral_weight.shape, F32), pltpu.SemaphoreType.DMA((local_y,))],
         compiler_params=pltpu.CompilerParams(vmem_limit_bytes=16 * 2**20),
     )(spec, back)
     pieces, grad_spectral = to_lines(send, grad_spectral)

time: 88.3 us -> 85.7 us (0.971)
  waiting for transfers between devices: 20.3 us -> 23.5 us
  local copies, waits for them, and re-layouts: 3.23 us -> 1.19 us
  Pallas kernels: 17.1 us -> 15.3 us
  blocking collectives: 25.3 us -> 23.9 us
    ppermute x12, waiting for transfers between devices: 9.79 us -> 12.2 us  [cross(): lax.ppermute(piece, 'gx', [(i, i ^ 2 * t) for i in range(parts_x)])]
    unnamed x8 -> x6, local copies, waits for them, and re-layouts: 3.23 us -> 1.19 us
    pallas_call x2, Pallas kernels: 7.61 us -> 5.77 us  [the longest x1 3.92 us: fast(): pl.pallas_call(outer_kernel, in_specs=[inside] * 2, out_specs=outside, ou...]
    all_to_all x2, blocking collectives: 25.3 us -> 23.9 us  [to_modes(): return (lax.all_to_all(send, ('gx', 'gy'), 0, 0, tiled=True), rest, tables)]
  transfers between devices with their start and end apart: 34 -> 34, of which waited for: 21 -> 23; matrix products, arithmetic and copies ran while one was open for 0% -> 0% of each run, Pallas kernels for 9% -> 7%
where the time goes in v3:
time: 85.7 us; the launch traced here: 85.4 us
  blocking collectives  23.9 us (28%)
  waiting for transfers between devices  23.5 us (27%)
  starting transfers between devices  20.7 us (24%)
  Pallas kernels  15.3 us (18%)
  local copies, waits for them, and re-layouts  1.19 us (1%)
    all_to_all x2, blocking collectives, to_modes(): return (lax.all_to_all(send, ('gx', 'gy'), 0, 0, tiled=True), rest, tables)  23.9 us
    ppermute x12, starting transfers between devices, cross(): lax.ppermute(piece, 'gx', [(i, i ^ 2 * t) for i in range(parts_x)])  15.2 us
    ppermute x12, waiting for transfers between devices, cross(): lax.ppermute(piece, 'gx', [(i, i ^ 2 * t) for i in range(parts_x)])  12.2 us
    pallas_call x10, Pallas kernels, call(): pl.pallas_call(kernel, out_shape=outs, scratch_shapes=list(scratch), comp...  9.52 us
    ppermute x6, waiting for transfers between devices, to_lines(): pieces.append(lax.ppermute(send, 'gy', ring))  6.85 us
    ppermute x6, starting transfers between devices, to_lines(): pieces.append(lax.ppermute(send, 'gy', ring))  4.89 us
    ppermute x16, waiting for transfers between devices, cross(): pieces = pieces + [lax.ppermute(piece, 'gx', swap) for piece in pieces]  4.5 us
    pallas_call x1, Pallas kernels, fast(): pl.pallas_call(outer_kernel, in_specs=[inside] * 2, out_specs=outside, ou...  3.92 us
  transfers between devices with their start and end apart: 34, of which 23 were waited for; matrix products, arithmetic and copies ran while one was open for 0% of the time, Pallas kernels for 7%

profile of v3, /device:TPU:0, one launch (start us, length us, event | category | flops | bytes accessed | tf_op | source)
XLA Modules:
  0.0 85.4 jit_solution(16528837598460184889)
XLA Ops:
  2.3 4.0 %collective-permute-start = (bf16[2,128,128]{2,1,0:T(8,128)(2,1)S(1)}, bf16[2,128,128]{2,1,0:T(8,128)(2,1)S(1)}, u32[]{:S(2)}, u32[]{:S(2)}) collective-permute-start(bf16[2,128,128]{2,1,0:T(8,128)(2,1)S(1)} %get-tuple-element.36), channel_id=1, source_target_pairs={{0,24},{4,28},{8,16},{12,20},{16,8},{20,12},{24,0},{28,4},{1,25},{... | collective-permute-start | bytes 196616 | tf_op jit(solution)/shard_map/ppermute | solution.py:493
  6.9 1.9 %shard_map.102 = (bf16[512,1024]{1,0:T(8,128)(2,1)S(1)}, bf16[512,512]{1,0:T(8,128)(2,1)S(1)}, bf16[64,64]{1,0:T(8,128)(2,1)S(1)}, bf16[256,256]{1,0:T(8,128)(2,...) custom-call(s32[32]{0:T(128)} %refs_0_.1, s32[32]{0:T(128)} %refs_1_.3, s32[4]{0:T(128)} %refs_2_.1, ...), custom_call_target="tpu_custom_call" | custom-call | tf_op jit(solution)/shard_map/pallas_call | solution.py:470
  8.7 1.7 %collective-permute-done.1.refs_3_ = bf16[2,128,128]{2,1,0:T(8,128)(2,1)S(1)} collective-permute-done((bf16[2,128,128]{2,1,0:T(8,128)(2,1)S(1)}, bf16[2,128,128]{2,1,0:T(8,128)(2,1)S(1)}, u32[]{:S(2)}, u32[]{:S(2)}) %collective-permute-start.1) | collective-permute-done | bytes 65568 | tf_op jit(solution)/shard_map/ppermute | solution.py:493
  13.3 13.1 %all_to_all.10.refs_0_ = bf16[32,16,128]{2,1,0:T(8,128)(2,1)S(1)} all-to-all(bf16[32,16,128]{2,1,0:T(8,128)(2,1)S(1)} %shard_map.104), channel_id=1, replica_groups=mesh['gx'=8,'gy'=4] {'gx','gy'}, dimensions={0} | all-to-all | bytes 262144 | tf_op jit(solution)/shard_map/all_to_all | solution.py:511
  26.4 2.0 %shard_map.105 = (f32[16,1024]{1,0:T(8,128)S(1)}, f32[8,16,128]{2,1,0:T(8,128)S(1)}) custom-call(bf16[32,16,128]{2,1,0:T(8,128)(2,1)S(1)} %all_to_all.10.refs_0_, bf16[4,8,4,2,64,64]{5,4,3,2,1,0:T(8,128)(2,1)S(1)} %copy-done), custom_call_target="tpu_custom_call" | custom-call | tf_op jit(solution)/shard_map/pallas_call | solution.py:435
  28.4 1.3 %collective-permute-start.9 = (f32[16,1024]{1,0:T(8,128)S(1)}, f32[16,1024]{1,0:T(8,128)S(1)}, u32[]{:S(2)}, u32[]{:S(2)}) collective-permute-start(f32[16,1024]{1,0:T(8,128)S(1)} %get-tuple-element.45.refs_0_), channel_id=1, source_target_pairs={{0,3},{1,0},{2,1},{3,2},{4,7},{5,4},{6,5},{7,6},{8,11},{9,8},{10,9... | collective-permute-start | bytes 196616 | tf_op jit(solution)/shard_map/ppermute | solution.py:530
  30.9 2.1 %collective-permute-done.9.refs_3_ = f32[16,1024]{1,0:T(8,128)S(1)} collective-permute-done((f32[16,1024]{1,0:T(8,128)S(1)}, f32[16,1024]{1,0:T(8,128)S(1)}, u32[]{:S(2)}, u32[]{:S(2)}) %collective-permute-start.9) | collective-permute-done | bytes 65568 | tf_op jit(solution)/shard_map/ppermute | solution.py:530
  33.0 3.9 %collective-permute-done.8.refs_2_ = f32[16,1024]{1,0:T(8,128)S(1)} collective-permute-done((f32[16,1024]{1,0:T(8,128)S(1)}, f32[16,1024]{1,0:T(8,128)S(1)}, u32[]{:S(2)}, u32[]{:S(2)}) %collective-permute-start.8) | collective-permute-done | bytes 65568 | tf_op jit(solution)/shard_map/ppermute | solution.py:530
  38.1 1.5 %collective-permute-start.11 = (bf16[32,1024]{1,0:T(8,128)(2,1)S(1)}, bf16[32,1024]{1,0:T(8,128)(2,1)S(1)}, u32[]{:S(2)}, u32[]{:S(2)}) collective-permute-start(bf16[32,1024]{1,0:T(8,128)(2,1)S(1)} %shard_map.106.refs_1_), channel_id=1, source_target_pairs={{0,16},{4,20},{8,24},{12,28},{16,0},{20,4},{24,8},{28,12},{1,17},{... | collective-permute-start | bytes 196616 | tf_op jit(solution)/shard_map/ppermute | solution.py:493
  39.6 1.2 %collective-permute-start.10 = (bf16[32,1024]{1,0:T(8,128)(2,1)S(1)}, bf16[32,1024]{1,0:T(8,128)(2,1)S(1)}, u32[]{:S(2)}, u32[]{:S(2)}) collective-permute-start(bf16[32,1024]{1,0:T(8,128)(2,1)S(1)} %shard_map.106.refs_1_), channel_id=1, source_target_pairs={{0,8},{4,12},{8,0},{12,4},{16,24},{20,28},{24,16},{28,20},{1,9},{5... | collective-permute-start | bytes 196616 | tf_op jit(solution)/shard_map/ppermute | solution.py:493
  40.8 1.8 %collective-permute-done.12.refs_4_ = bf16[32,1024]{1,0:T(8,128)(2,1)S(1)} collective-permute-done((bf16[32,1024]{1,0:T(8,128)(2,1)S(1)}, bf16[32,1024]{1,0:T(8,128)(2,1)S(1)}, u32[]{:S(2)}, u32[]{:S(2)}) %collective-permute-start.12) | collective-permute-done | bytes 65568 | tf_op jit(solution)/shard_map/ppermute | solution.py:493
  45.1 1.6 %shard_map.108 = (bf16[16,16,8,64]{3,2,1,0:T(8,128)(2,1)}, bf16[8,128,128]{2,1,0:T(8,128)(2,1)S(1)}, bf16[2,144,128]{2,1,0:T(8,128)(2,1)S(1)}, bf16[2,144,128]{2...) custom-call(bf16[256,256]{1,0:T(8,128)(2,1)S(1)} %get-tuple-element.34.refs_0_, ...), custom_call_target="tpu_custom_call" | custom-call | tf_op jit(solution)/shard_map/pallas_call | solution.py:435
  46.7 1.2 %collective-permute-start.17 = (bf16[2,144,128]{2,1,0:T(8,128)(2,1)S(1)}, bf16[2,144,128]{2,1,0:T(8,128)(2,1)S(1)}, u32[]{:S(2)}, u32[]{:S(2)}) collective-permute-start(bf16[2,144,128]{2,1,0:T(8,128)(2,1)S(1)} %get-tuple-element.50), channel_id=1, source_target_pairs={{0,8},{4,12},{8,0},{12,4},{16,24},{20,28},{24,16},{28,20},{1,9},{5... | collective-permute-start | bytes 221192 | tf_op jit(solution)/shard_map/ppermute | solution.py:493
  48.8 1.4 %collective-permute-start.19 = (bf16[2,144,128]{2,1,0:T(8,128)(2,1)S(1)}, bf16[2,144,128]{2,1,0:T(8,128)(2,1)S(1)}, u32[]{:S(2)}, u32[]{:S(2)}) collective-permute-start(bf16[2,144,128]{2,1,0:T(8,128)(2,1)S(1)} %get-tuple-element.52), channel_id=1, source_target_pairs={{0,24},{4,28},{8,16},{12,20},{16,8},{20,12},{24,0},{28,4},{1,25},{... | collective-permute-start | bytes 221192 | tf_op jit(solution)/shard_map/ppermute | solution.py:493
  51.1 2.0 %collective-permute-done.18.refs_4_ = bf16[2,144,128]{2,1,0:T(8,128)(2,1)S(1)} collective-permute-done((bf16[2,144,128]{2,1,0:T(8,128)(2,1)S(1)}, bf16[2,144,128]{2,1,0:T(8,128)(2,1)S(1)}, u32[]{:S(2)}, u32[]{:S(2)}) %collective-permute-start.18) | collective-permute-done | bytes 73760 | tf_op jit(solution)/shard_map/ppermute | solution.py:493
  56.2 10.8 %all_to_all.11.refs_0_ = bf16[32,16,128]{2,1,0:T(8,128)(2,1)S(1)} all-to-all(bf16[32,16,128]{2,1,0:T(8,128)(2,1)S(1)} %get-tuple-element.53), channel_id=1, replica_groups=mesh['gx'=8,'gy'=4] {'gx','gy'}, dimensions={0} | all-to-all | bytes 262144 | tf_op jit(solution)/shard_map/all_to_all | solution.py:511
  67.0 1.6 %shard_map.110 = (bf16[16,1152]{1,0:T(8,128)(2,1)S(1)}, f32[8,16,128]{2,1,0:T(8,128)S(1)}) custom-call(bf16[32,16,128]{2,1,0:T(8,128)(2,1)S(1)} %all_to_all.11.refs_0_, bf16[4,8,4,2,64,64]{5,4,3,2,1,0:T(8,128)(2,1)S(1)} %copy-done, bf16[16,128]{1,0:T(8,128)(2,1)S(1)} %get-tuple-element.54.refs_2_), custom_call_target="tpu_custom_call" | custom-call | tf_op jit(solution)/shard_map/pallas_call | solution.py:435
  68.6 1.3 %collective-permute-start.26 = (bf16[16,1152]{1,0:T(8,128)(2,1)S(1)}, bf16[16,1152]{1,0:T(8,128)(2,1)S(1)}, u32[]{:S(2)}, u32[]{:S(2)}) collective-permute-start(bf16[16,1152]{1,0:T(8,128)(2,1)S(1)} %get-tuple-element.55.refs_0_), channel_id=1, source_target_pairs={{0,3},{1,0},{2,1},{3,2},{4,7},{5,4},{6,5},{7,6},{8,11},{9,8},{10,9... | collective-permute-start | bytes 110600 | tf_op jit(solution)/shard_map/ppermute | solution.py:530
  69.8 1.2 %collective-permute-start.24 = (bf16[16,1152]{1,0:T(8,128)(2,1)S(1)}, bf16[16,1152]{1,0:T(8,128)(2,1)S(1)}, u32[]{:S(2)}, u32[]{:S(2)}) collective-permute-start(bf16[16,1152]{1,0:T(8,128)(2,1)S(1)} %get-tuple-element.55.refs_0_), channel_id=1, source_target_pairs={{0,1},{1,2},{2,3},{3,0},{4,5},{5,6},{6,7},{7,4},{8,9},{9,10},{10,1... | collective-permute-start | bytes 110600 | tf_op jit(solution)/shard_map/ppermute | solution.py:530
  71.0 3.9 %shard_map.111 = f32[4,8,4,2,64,64]{5,4,3,2,1,0:T(8,128)} custom-call(f32[8,16,128]{2,1,0:T(8,128)S(1)} %get-tuple-element.56.spec_ref, f32[8,16,128]{2,1,0:T(8,128)S(1)} %get-tuple-element.57.back_ref), custom_call_target="tpu_custom_call" | custom-call | tf_op jit(solution)/shard_map/pallas_call | solution.py:562
  77.0 1.5 %collective-permute-start.28 = (bf16[32,1152]{1,0:T(8,128)(2,1)S(1)}, bf16[32,1152]{1,0:T(8,128)(2,1)S(1)}, u32[]{:S(2)}, u32[]{:S(2)}) collective-permute-start(bf16[32,1152]{1,0:T(8,128)(2,1)S(1)} %shard_map.112.refs_1_), channel_id=1, source_target_pairs={{0,16},{4,20},{8,24},{12,28},{16,0},{20,4},{24,8},{28,12},{1,17},{... | collective-permute-start | bytes 221192 | tf_op jit(solution)/shard_map/ppermute | solution.py:493
  78.5 1.2 %collective-permute-start.27 = (bf16[32,1152]{1,0:T(8,128)(2,1)S(1)}, bf16[32,1152]{1,0:T(8,128)(2,1)S(1)}, u32[]{:S(2)}, u32[]{:S(2)}) collective-permute-start(bf16[32,1152]{1,0:T(8,128)(2,1)S(1)} %shard_map.112.refs_1_), channel_id=1, source_target_pairs={{0,8},{4,12},{8,0},{12,4},{16,24},{20,28},{24,16},{28,20},{1,9},{5... | collective-permute-start | bytes 221192 | tf_op jit(solution)/shard_map/ppermute | solution.py:493
  79.7 1.9 %collective-permute-done.29.refs_4_ = bf16[32,1152]{1,0:T(8,128)(2,1)S(1)} collective-permute-done((bf16[32,1152]{1,0:T(8,128)(2,1)S(1)}, bf16[32,1152]{1,0:T(8,128)(2,1)S(1)}, u32[]{:S(2)}, u32[]{:S(2)}) %collective-permute-start.29) | collective-permute-done | bytes 73760 | tf_op jit(solution)/shard_map/ppermute | solution.py:493
  84.1 1.3 %shard_map.113 = (bf16[16,16,8,64]{3,2,1,0:T(8,128)(2,1)}, f32[64,64]{1,0:T(8,128)}) custom-call(bf16[256,256]{1,0:T(8,128)(2,1)S(1)} %get-tuple-element.34.refs_0_, bf16[32,1152]{1,0:T(8,128)(2,1)S(1)} %shard_map.112.refs_1_, bf16[32,1152]{1,0:T(8,128)(2,1)S(1)} %collective-permute-done.27.refs_2_, bf16[32,1152]{1,0:T(8,128)(2,1)S(1)} %collective-permute-done.28.refs_3_, ...), custom_call_target="tpu_custom_call" | custom-call | tf_op jit(solution)/shard_map/pallas_call | solution.py:435
  (64 shorter events, 19.2 us)
Async XLA Ops:
  2.3 6.5 %collective-permute-start = (bf16[2,128,128]{2,1,0:T(8,128)(2,1)S(1)}, bf16[2,128,128]{2,1,0:T(8,128)(2,1)S(1)}, u32[]{:S(2)}, u32[]{:S(2)}) collective-permute-start(bf16[2,128,128]{2,1,0:T(8,128)(2,1)S(1)} %get-tuple-element.36), channel_id=1, source_target_pairs={{0,24},{4,28},{8,16},{12,20},{16,8},{20,12},{24,0},{28,4},{1,25},{... | collective-permute-start | bytes 196616 | tf_op jit(solution)/shard_map/ppermute | solution.py:493
  6.2 4.3 %collective-permute-start.1 = (bf16[2,128,128]{2,1,0:T(8,128)(2,1)S(1)}, bf16[2,128,128]{2,1,0:T(8,128)(2,1)S(1)}, u32[]{:S(2)}, u32[]{:S(2)}) collective-permute-start(bf16[2,128,128]{2,1,0:T(8,128)(2,1)S(1)} %get-tuple-element.42), channel_id=1, source_target_pairs={{0,8},{4,12},{8,0},{12,4},{16,24},{20,28},{24,16},{28,20},{1,9},{5... | collective-permute-start | bytes 196616 | tf_op jit(solution)/shard_map/ppermute | solution.py:493
  6.8 4.3 %collective-permute-start.2 = (bf16[2,128,128]{2,1,0:T(8,128)(2,1)S(1)}, bf16[2,128,128]{2,1,0:T(8,128)(2,1)S(1)}, u32[]{:S(2)}, u32[]{:S(2)}) collective-permute-start(bf16[2,128,128]{2,1,0:T(8,128)(2,1)S(1)} %get-tuple-element.43), channel_id=1, source_target_pairs={{0,16},{4,20},{8,24},{12,28},{16,0},{20,4},{24,8},{28,12},{1,17},{... | collective-permute-start | bytes 196616 | tf_op jit(solution)/shard_map/ppermute | solution.py:493
  6.9 4.7 %collective-permute-start.3 = (bf16[2,128,128]{2,1,0:T(8,128)(2,1)S(1)}, bf16[2,128,128]{2,1,0:T(8,128)(2,1)S(1)}, u32[]{:S(2)}, u32[]{:S(2)}) collective-permute-start(bf16[2,128,128]{2,1,0:T(8,128)(2,1)S(1)} %get-tuple-element.41.refs_2_), channel_id=1, source_target_pairs={{0,4},{4,0},{8,12},{12,8},{16,20},{20,16},{24,28},{28,24},{1,5},{5... | collective-permute-start | bytes 196616 | tf_op jit(solution)/shard_map/ppermute | solution.py:500
  28.4 4.6 %collective-permute-start.9 = (f32[16,1024]{1,0:T(8,128)S(1)}, f32[16,1024]{1,0:T(8,128)S(1)}, u32[]{:S(2)}, u32[]{:S(2)}) collective-permute-start(f32[16,1024]{1,0:T(8,128)S(1)} %get-tuple-element.45.refs_0_), channel_id=1, source_target_pairs={{0,3},{1,0},{2,1},{3,2},{4,7},{5,4},{6,5},{7,6},{8,11},{9,8},{10,9... | collective-permute-start | bytes 196616 | tf_op jit(solution)/shard_map/ppermute | solution.py:530
  29.7 7.2 %collective-permute-start.8 = (f32[16,1024]{1,0:T(8,128)S(1)}, f32[16,1024]{1,0:T(8,128)S(1)}, u32[]{:S(2)}, u32[]{:S(2)}) collective-permute-start(f32[16,1024]{1,0:T(8,128)S(1)} %get-tuple-element.45.refs_0_), channel_id=1, source_target_pairs={{0,2},{1,3},{2,0},{3,1},{4,6},{5,7},{6,4},{7,5},{8,10},{9,11},{10,... | collective-permute-start | bytes 196616 | tf_op jit(solution)/shard_map/ppermute | solution.py:530
  29.7 7.2 %collective-permute-start.7 = (f32[16,1024]{1,0:T(8,128)S(1)}, f32[16,1024]{1,0:T(8,128)S(1)}, u32[]{:S(2)}, u32[]{:S(2)}) collective-permute-start(f32[16,1024]{1,0:T(8,128)S(1)} %get-tuple-element.45.refs_0_), channel_id=1, source_target_pairs={{0,1},{1,2},{2,3},{3,0},{4,5},{5,6},{6,7},{7,4},{8,9},{9,10},{10,1... | collective-permute-start | bytes 196616 | tf_op jit(solution)/shard_map/ppermute | solution.py:530
  37.3 5.3 %collective-permute-start.12 = (bf16[32,1024]{1,0:T(8,128)(2,1)S(1)}, bf16[32,1024]{1,0:T(8,128)(2,1)S(1)}, u32[]{:S(2)}, u32[]{:S(2)}) collective-permute-start(bf16[32,1024]{1,0:T(8,128)(2,1)S(1)} %shard_map.106.refs_1_), channel_id=1, source_target_pairs={{0,24},{4,28},{8,16},{12,20},{16,8},{20,12},{24,0},{28,4},{1,25},{... | collective-permute-start | bytes 196616 | tf_op jit(solution)/shard_map/ppermute | solution.py:493
  38.1 5.0 %collective-permute-start.11 = (bf16[32,1024]{1,0:T(8,128)(2,1)S(1)}, bf16[32,1024]{1,0:T(8,128)(2,1)S(1)}, u32[]{:S(2)}, u32[]{:S(2)}) collective-permute-start(bf16[32,1024]{1,0:T(8,128)(2,1)S(1)} %shard_map.106.refs_1_), channel_id=1, source_target_pairs={{0,16},{4,20},{8,24},{12,28},{16,0},{20,4},{24,8},{28,12},{1,17},{... | collective-permute-start | bytes 196616 | tf_op jit(solution)/shard_map/ppermute | solution.py:493
  39.6 4.3 %collective-permute-start.10 = (bf16[32,1024]{1,0:T(8,128)(2,1)S(1)}, bf16[32,1024]{1,0:T(8,128)(2,1)S(1)}, u32[]{:S(2)}, u32[]{:S(2)}) collective-permute-start(bf16[32,1024]{1,0:T(8,128)(2,1)S(1)} %shard_map.106.refs_1_), channel_id=1, source_target_pairs={{0,8},{4,12},{8,0},{12,4},{16,24},{20,28},{24,16},{28,20},{1,9},{5... | collective-permute-start | bytes 196616 | tf_op jit(solution)/shard_map/ppermute | solution.py:493
  40.8 3.2 %collective-permute-start.13 = (bf16[32,1024]{1,0:T(8,128)(2,1)S(1)}, bf16[32,1024]{1,0:T(8,128)(2,1)S(1)}, u32[]{:S(2)}, u32[]{:S(2)}) collective-permute-start(bf16[32,1024]{1,0:T(8,128)(2,1)S(1)} %shard_map.106.refs_1_), channel_id=1, source_target_pairs={{0,4},{4,0},{8,12},{12,8},{16,20},{20,16},{24,28},{28,24},{1,5},{5... | collective-permute-start | bytes 196616 | tf_op jit(solution)/shard_map/ppermute | solution.py:500
  42.6 1.4 %collective-permute-start.16 = (bf16[32,1024]{1,0:T(8,128)(2,1)S(1)}, bf16[32,1024]{1,0:T(8,128)(2,1)S(1)}, u32[]{:S(2)}, u32[]{:S(2)}) collective-permute-start(bf16[32,1024]{1,0:T(8,128)(2,1)S(1)} %collective-permute-done.12.refs_4_), channel_id=1, source_target_pairs={{0,4},{4,0},{8,12},{12,8},{16,20},{20,16},{24,28},{28,24},{1,5},{5... | collective-permute-start | bytes 196616 | tf_op jit(solution)/shard_map/ppermute | solution.py:500
  46.7 4.4 %collective-permute-start.17 = (bf16[2,144,128]{2,1,0:T(8,128)(2,1)S(1)}, bf16[2,144,128]{2,1,0:T(8,128)(2,1)S(1)}, u32[]{:S(2)}, u32[]{:S(2)}) collective-permute-start(bf16[2,144,128]{2,1,0:T(8,128)(2,1)S(1)} %get-tuple-element.50), channel_id=1, source_target_pairs={{0,8},{4,12},{8,0},{12,4},{16,24},{20,28},{24,16},{28,20},{1,9},{5... | collective-permute-start | bytes 221192 | tf_op jit(solution)/shard_map/ppermute | solution.py:493
  48.0 5.1 %collective-permute-start.18 = (bf16[2,144,128]{2,1,0:T(8,128)(2,1)S(1)}, bf16[2,144,128]{2,1,0:T(8,128)(2,1)S(1)}, u32[]{:S(2)}, u32[]{:S(2)}) collective-permute-start(bf16[2,144,128]{2,1,0:T(8,128)(2,1)S(1)} %get-tuple-element.51), channel_id=1, source_target_pairs={{0,16},{4,20},{8,24},{12,28},{16,0},{20,4},{24,8},{28,12},{1,17},{... | collective-permute-start | bytes 221192 | tf_op jit(solution)/shard_map/ppermute | solution.py:493
  48.8 5.3 %collective-permute-start.19 = (bf16[2,144,128]{2,1,0:T(8,128)(2,1)S(1)}, bf16[2,144,128]{2,1,0:T(8,128)(2,1)S(1)}, u32[]{:S(2)}, u32[]{:S(2)}) collective-permute-start(bf16[2,144,128]{2,1,0:T(8,128)(2,1)S(1)} %get-tuple-element.52), channel_id=1, source_target_pairs={{0,24},{4,28},{8,16},{12,20},{16,8},{20,12},{24,0},{28,4},{1,25},{... | collective-permute-start | bytes 221192 | tf_op jit(solution)/shard_map/ppermute | solution.py:493
  50.2 3.8 %collective-permute-start.20 = (bf16[2,144,128]{2,1,0:T(8,128)(2,1)S(1)}, bf16[2,144,128]{2,1,0:T(8,128)(2,1)S(1)}, u32[]{:S(2)}, u32[]{:S(2)}) collective-permute-start(bf16[2,144,128]{2,1,0:T(8,128)(2,1)S(1)} %get-tuple-element.49.refs_2_), channel_id=1, source_target_pairs={{0,4},{4,0},{8,12},{12,8},{16,20},{20,16},{24,28},{28,24},{1,5},{5... | collective-permute-start | bytes 221192 | tf_op jit(solution)/shard_map/ppermute | solution.py:500
  51.1 3.0 %collective-permute-start.21 = (bf16[2,144,128]{2,1,0:T(8,128)(2,1)S(1)}, bf16[2,144,128]{2,1,0:T(8,128)(2,1)S(1)}, u32[]{:S(2)}, u32[]{:S(2)}) collective-permute-start(bf16[2,144,128]{2,1,0:T(8,128)(2,1)S(1)} %collective-permute-done.17.refs_3_), channel_id=1, source_target_pairs={{0,4},{4,0},{8,12},{12,8},{16,20},{20,16},{24,28},{28,24},{1,5},{5... | collective-permute-start | bytes 221192 | tf_op jit(solution)/shard_map/ppermute | solution.py:500
  68.6 6.4 %collective-permute-start.26 = (bf16[16,1152]{1,0:T(8,128)(2,1)S(1)}, bf16[16,1152]{1,0:T(8,128)(2,1)S(1)}, u32[]{:S(2)}, u32[]{:S(2)}) collective-permute-start(bf16[16,1152]{1,0:T(8,128)(2,1)S(1)} %get-tuple-element.55.refs_0_), channel_id=1, source_target_pairs={{0,3},{1,0},{2,1},{3,2},{4,7},{5,4},{6,5},{7,6},{8,11},{9,8},{10,9... | collective-permute-start | bytes 110600 | tf_op jit(solution)/shard_map/ppermute | solution.py:530
  69.8 6.0 %collective-permute-start.25 = (bf16[16,1152]{1,0:T(8,128)(2,1)S(1)}, bf16[16,1152]{1,0:T(8,128)(2,1)S(1)}, u32[]{:S(2)}, u32[]{:S(2)}) collective-permute-start(bf16[16,1152]{1,0:T(8,128)(2,1)S(1)} %get-tuple-element.55.refs_0_), channel_id=1, source_target_pairs={{0,2},{1,3},{2,0},{3,1},{4,6},{5,7},{6,4},{7,5},{8,10},{9,11},{10,... | collective-permute-start | bytes 110600 | tf_op jit(solution)/shard_map/ppermute | solution.py:530
  69.8 6.0 %collective-permute-start.24 = (bf16[16,1152]{1,0:T(8,128)(2,1)S(1)}, bf16[16,1152]{1,0:T(8,128)(2,1)S(1)}, u32[]{:S(2)}, u32[]{:S(2)}) collective-permute-start(bf16[16,1152]{1,0:T(8,128)(2,1)S(1)} %get-tuple-element.55.refs_0_), channel_id=1, source_target_pairs={{0,1},{1,2},{2,3},{3,0},{4,5},{5,6},{6,7},{7,4},{8,9},{9,10},{10,1... | collective-permute-start | bytes 110600 | tf_op jit(solution)/shard_map/ppermute | solution.py:530
  76.2 5.4 %collective-permute-start.29 = (bf16[32,1152]{1,0:T(8,128)(2,1)S(1)}, bf16[32,1152]{1,0:T(8,128)(2,1)S(1)}, u32[]{:S(2)}, u32[]{:S(2)}) collective-permute-start(bf16[32,1152]{1,0:T(8,128)(2,1)S(1)} %shard_map.112.refs_1_), channel_id=1, source_target_pairs={{0,24},{4,28},{8,16},{12,20},{16,8},{20,12},{24,0},{28,4},{1,25},{... | collective-permute-start | bytes 221192 | tf_op jit(solution)/shard_map/ppermute | solution.py:493
  77.0 5.1 %collective-permute-start.28 = (bf16[32,1152]{1,0:T(8,128)(2,1)S(1)}, bf16[32,1152]{1,0:T(8,128)(2,1)S(1)}, u32[]{:S(2)}, u32[]{:S(2)}) collective-permute-start(bf16[32,1152]{1,0:T(8,128)(2,1)S(1)} %shard_map.112.refs_1_), channel_id=1, source_target_pairs={{0,16},{4,20},{8,24},{12,28},{16,0},{20,4},{24,8},{28,12},{1,17},{... | collective-permute-start | bytes 221192 | tf_op jit(solution)/shard_map/ppermute | solution.py:493
  78.5 4.4 %collective-permute-start.27 = (bf16[32,1152]{1,0:T(8,128)(2,1)S(1)}, bf16[32,1152]{1,0:T(8,128)(2,1)S(1)}, u32[]{:S(2)}, u32[]{:S(2)}) collective-permute-start(bf16[32,1152]{1,0:T(8,128)(2,1)S(1)} %shard_map.112.refs_1_), channel_id=1, source_target_pairs={{0,8},{4,12},{8,0},{12,4},{16,24},{20,28},{24,16},{28,20},{1,9},{5... | collective-permute-start | bytes 221192 | tf_op jit(solution)/shard_map/ppermute | solution.py:493
  79.7 3.1 %collective-permute-start.30 = (bf16[32,1152]{1,0:T(8,128)(2,1)S(1)}, bf16[32,1152]{1,0:T(8,128)(2,1)S(1)}, u32[]{:S(2)}, u32[]{:S(2)}) collective-permute-start(bf16[32,1152]{1,0:T(8,128)(2,1)S(1)} %shard_map.112.refs_1_), channel_id=1, source_target_pairs={{0,4},{4,0},{8,12},{12,8},{16,20},{20,16},{24,28},{28,24},{1,5},{5... | collective-permute-start | bytes 221192 | tf_op jit(solution)/shard_map/ppermute | solution.py:500
  (13 other events, 81.8 us)

commit v4 on v3

--- a/solution.py
+++ b/solution.py
@@ -292,14 +292,20 @@
         else:
             first = lax.broadcasted_iota(jnp.int32, spec.shape, 1) < chans
             both = split_rows(jnp.concatenate([spec, jnp.where(first, turned, -turned)], axis=0))
-        mode = lax.broadcasted_iota(jnp.int32, both.shape, 1 if forward else 0) % rows
-        total = jnp.zeros((2 * chans, 4 * rows) if forward else (4 * rows, chans), F32)
-        for m in range(rows):
-            weight = weight_ref[m // size_z, ky, m % size_z].reshape(2 * chans, chans)
-            own = jnp.where(mode == m, both, jnp.zeros_like(both))
-            total = total + (dot(weight, own) if forward else dot(own, weight))
         if forward:
+            wide = [weight_ref[m // size_z, ky, m % size_z].reshape(2 * chans, chans) for m in range(rows)]
+            wide = [jnp.concatenate(wide[m : m + 2], axis=1) for m in range(0, rows, 2)]
+            mode = lax.broadcasted_iota(jnp.int32, both.shape, 1) % rows
+            own = [jnp.where(mode == m, both, jnp.zeros_like(both)) for m in range(rows)]
+            total = dot(jnp.concatenate(wide, axis=1), jnp.concatenate(own, axis=0))
             total = total.T
+        else:
+            stack = jnp.concatenate(
+                [weight_ref[kx, ky].reshape(size_z * 2 * chans, chans) for kx in range(size_x)], axis=0
+            )
+            mode = lax.broadcasted_iota(jnp.int32, both.shape, 0) % rows
+            own = [jnp.where(mode == m, both, jnp.zeros_like(both)) for m in range(rows)]
+            total = dot(jnp.concatenate(own, axis=1), stack)
         total = total[: 2 * rows] + total[2 * rows :]
         if forward:
             real, imag = total[:rows], total[rows:]
@@ -327,12 +333,9 @@
         send_ref[:EXTRA, WIDE:] = parted(total[: EXTRA // 2])
         send_ref[EXTRA:, WIDE:] = jnp.zeros((send_ref.shape[0] - EXTRA, LANES), BF)
     data = jnp.concatenate([refs[s][:, :WIDE] for s in range(steps)], axis=0)
-    high = data.astype(BF)
-    lines = dot(table_ref[...], high)
+    lines = dot(table_ref[...], data)
     half = lines.shape[0] // 2
     lines = lines[:half] + lines[half:]
-    if data.dtype == F32:
-        lines = lines + dot(table_ref[:half, :], (data - high.astype(F32)).astype(BF))
     size_y = half // 2
     count = WIDE // chans
     for m in range(0, count, 2):
@@ -514,7 +517,7 @@
         return call(
             bind(mix_kernel, forward, parts_y),
             (
-                sds((2 * local_y, WIDE + len(rest) * LANES), F32 if forward else BF),
+                sds((2 * local_y, WIDE + len(rest) * LANES), BF),
                 sds((local_y, modes, LANES), F32),
             ),
             recv,

time: 85.7 us -> 83.6 us (0.975)
  waiting for transfers between devices: 23.5 us -> 22.2 us
    ppermute x6, waiting for transfers between devices: 6.85 us -> 5.44 us  [to_lines(): pieces.append(lax.ppermute(send, 'gy', ring))]
where the time goes in v4:
time: 83.6 us; the launch traced here: 83.4 us
  blocking collectives  23.8 us (28%)
  waiting for transfers between devices  22.2 us (27%)
  starting transfers between devices  20.6 us (25%)
  Pallas kernels  14.7 us (18%)
  local copies, waits for them, and re-layouts  1.19 us (1%)
    all_to_all x2, blocking collectives, to_modes(): return (lax.all_to_all(send, ('gx', 'gy'), 0, 0, tiled=True), rest, tables)  23.8 us
    ppermute x12, starting transfers between devices, cross(): lax.ppermute(piece, 'gx', [(i, i ^ 2 * t) for i in range(parts_x)])  15.2 us
    ppermute x12, waiting for transfers between devices, cross(): lax.ppermute(piece, 'gx', [(i, i ^ 2 * t) for i in range(parts_x)])  12.2 us
    pallas_call x10, Pallas kernels, call(): pl.pallas_call(kernel, out_shape=outs, scratch_shapes=list(scratch), comp...  8.93 us
    ppermute x6, waiting for transfers between devices, to_lines(): pieces.append(lax.ppermute(send, 'gy', ring))  5.44 us
    ppermute x6, starting transfers between devices, to_lines(): pieces.append(lax.ppermute(send, 'gy', ring))  4.9 us
    ppermute x16, waiting for transfers between devices, cross(): pieces = pieces + [lax.ppermute(piece, 'gx', swap) for piece in pieces]  4.5 us
    pallas_call x1, Pallas kernels, fast(): pl.pallas_call(outer_kernel, in_specs=[inside] * 2, out_specs=outside, ou...  3.91 us
  transfers between devices with their start and end apart: 34, of which 23 were waited for; matrix products, arithmetic and copies ran while one was open for 0% of the time, Pallas kernels for 7%

profile of v4, /device:TPU:0, one launch (start us, length us, event | category | flops | bytes accessed | tf_op | source)
XLA Modules:
  0.0 83.4 jit_solution(16090023539767084966)
XLA Ops:
  2.3 4.0 %collective-permute-start = (bf16[2,128,128]{2,1,0:T(8,128)(2,1)S(1)}, bf16[2,128,128]{2,1,0:T(8,128)(2,1)S(1)}, u32[]{:S(2)}, u32[]{:S(2)}) collective-permute-start(bf16[2,128,128]{2,1,0:T(8,128)(2,1)S(1)} %get-tuple-element.36), channel_id=1, source_target_pairs={{0,24},{4,28},{8,16},{12,20},{16,8},{20,12},{24,0},{28,4},{1,25},{... | collective-permute-start | bytes 196616 | tf_op jit(solution)/shard_map/ppermute | solution.py:496
  6.9 1.9 %shard_map.102 = (bf16[512,1024]{1,0:T(8,128)(2,1)S(1)}, bf16[512,512]{1,0:T(8,128)(2,1)S(1)}, bf16[64,64]{1,0:T(8,128)(2,1)S(1)}, bf16[256,256]{1,0:T(8,128)(2,...) custom-call(s32[32]{0:T(128)} %refs_0_.1, s32[32]{0:T(128)} %refs_1_.3, s32[4]{0:T(128)} %refs_2_.1, ...), custom_call_target="tpu_custom_call" | custom-call | tf_op jit(solution)/shard_map/pallas_call | solution.py:473
  8.7 1.7 %collective-permute-done.1.refs_3_ = bf16[2,128,128]{2,1,0:T(8,128)(2,1)S(1)} collective-permute-done((bf16[2,128,128]{2,1,0:T(8,128)(2,1)S(1)}, bf16[2,128,128]{2,1,0:T(8,128)(2,1)S(1)}, u32[]{:S(2)}, u32[]{:S(2)}) %collective-permute-start.1) | collective-permute-done | bytes 65568 | tf_op jit(solution)/shard_map/ppermute | solution.py:496
  13.3 13.1 %all_to_all.10.refs_0_ = bf16[32,16,128]{2,1,0:T(8,128)(2,1)S(1)} all-to-all(bf16[32,16,128]{2,1,0:T(8,128)(2,1)S(1)} %shard_map.104), channel_id=1, replica_groups=mesh['gx'=8,'gy'=4] {'gx','gy'}, dimensions={0} | all-to-all | bytes 262144 | tf_op jit(solution)/shard_map/all_to_all | solution.py:514
  26.4 2.0 %shard_map.105 = (bf16[16,1024]{1,0:T(8,128)(2,1)S(1)}, f32[8,16,128]{2,1,0:T(8,128)S(1)}) custom-call(bf16[32,16,128]{2,1,0:T(8,128)(2,1)S(1)} %all_to_all.10.refs_0_, bf16[4,8,4,2,64,64]{5,4,3,2,1,0:T(8,128)(2,1)S(1)} %copy-done), custom_call_target="tpu_custom_call" | custom-call | tf_op jit(solution)/shard_map/pallas_call | solution.py:438
  28.4 1.3 %collective-permute-start.9 = (bf16[16,1024]{1,0:T(8,128)(2,1)S(1)}, bf16[16,1024]{1,0:T(8,128)(2,1)S(1)}, u32[]{:S(2)}, u32[]{:S(2)}) collective-permute-start(bf16[16,1024]{1,0:T(8,128)(2,1)S(1)} %get-tuple-element.45.refs_0_), channel_id=1, source_target_pairs={{0,3},{1,0},{2,1},{3,2},{4,7},{5,4},{6,5},{7,6},{8,11},{9,8},{10,9... | collective-permute-start | bytes 98312 | tf_op jit(solution)/shard_map/ppermute | solution.py:533
  29.6 1.2 %collective-permute-start.7 = (bf16[16,1024]{1,0:T(8,128)(2,1)S(1)}, bf16[16,1024]{1,0:T(8,128)(2,1)S(1)}, u32[]{:S(2)}, u32[]{:S(2)}) collective-permute-start(bf16[16,1024]{1,0:T(8,128)(2,1)S(1)} %get-tuple-element.45.refs_0_), channel_id=1, source_target_pairs={{0,1},{1,2},{2,3},{3,0},{4,5},{5,6},{6,7},{7,4},{8,9},{9,10},{10,1... | collective-permute-start | bytes 98312 | tf_op jit(solution)/shard_map/ppermute | solution.py:533
  30.8 1.6 %collective-permute-done.9.refs_3_ = bf16[16,1024]{1,0:T(8,128)(2,1)S(1)} collective-permute-done((bf16[16,1024]{1,0:T(8,128)(2,1)S(1)}, bf16[16,1024]{1,0:T(8,128)(2,1)S(1)}, u32[]{:S(2)}, u32[]{:S(2)}) %collective-permute-start.9) | collective-permute-done | bytes 32800 | tf_op jit(solution)/shard_map/ppermute | solution.py:533
  32.5 3.0 %collective-permute-done.8.refs_2_ = bf16[16,1024]{1,0:T(8,128)(2,1)S(1)} collective-permute-done((bf16[16,1024]{1,0:T(8,128)(2,1)S(1)}, bf16[16,1024]{1,0:T(8,128)(2,1)S(1)}, u32[]{:S(2)}, u32[]{:S(2)}) %collective-permute-start.8) | collective-permute-done | bytes 32800 | tf_op jit(solution)/shard_map/ppermute | solution.py:533
  36.8 1.4 %collective-permute-start.11 = (bf16[32,1024]{1,0:T(8,128)(2,1)S(1)}, bf16[32,1024]{1,0:T(8,128)(2,1)S(1)}, u32[]{:S(2)}, u32[]{:S(2)}) collective-permute-start(bf16[32,1024]{1,0:T(8,128)(2,1)S(1)} %shard_map.106.refs_1_), channel_id=1, source_target_pairs={{0,16},{4,20},{8,24},{12,28},{16,0},{20,4},{24,8},{28,12},{1,17},{... | collective-permute-start | bytes 196616 | tf_op jit(solution)/shard_map/ppermute | solution.py:496
  38.1 1.2 %collective-permute-start.10 = (bf16[32,1024]{1,0:T(8,128)(2,1)S(1)}, bf16[32,1024]{1,0:T(8,128)(2,1)S(1)}, u32[]{:S(2)}, u32[]{:S(2)}) collective-permute-start(bf16[32,1024]{1,0:T(8,128)(2,1)S(1)} %shard_map.106.refs_1_), channel_id=1, source_target_pairs={{0,8},{4,12},{8,0},{12,4},{16,24},{20,28},{24,16},{28,20},{1,9},{5... | collective-permute-start | bytes 196616 | tf_op jit(solution)/shard_map/ppermute | solution.py:496
  39.3 1.7 %collective-permute-done.12.refs_4_ = bf16[32,1024]{1,0:T(8,128)(2,1)S(1)} collective-permute-done((bf16[32,1024]{1,0:T(8,128)(2,1)S(1)}, bf16[32,1024]{1,0:T(8,128)(2,1)S(1)}, u32[]{:S(2)}, u32[]{:S(2)}) %collective-permute-start.12) | collective-permute-done | bytes 65568 | tf_op jit(solution)/shard_map/ppermute | solution.py:496
  43.6 1.6 %shard_map.108 = (bf16[16,16,8,64]{3,2,1,0:T(8,128)(2,1)}, bf16[8,128,128]{2,1,0:T(8,128)(2,1)S(1)}, bf16[2,144,128]{2,1,0:T(8,128)(2,1)S(1)}, bf16[2,144,128]{2...) custom-call(bf16[256,256]{1,0:T(8,128)(2,1)S(1)} %get-tuple-element.34.refs_0_, ...), custom_call_target="tpu_custom_call" | custom-call | tf_op jit(solution)/shard_map/pallas_call | solution.py:438
  45.2 1.2 %collective-permute-start.17 = (bf16[2,144,128]{2,1,0:T(8,128)(2,1)S(1)}, bf16[2,144,128]{2,1,0:T(8,128)(2,1)S(1)}, u32[]{:S(2)}, u32[]{:S(2)}) collective-permute-start(bf16[2,144,128]{2,1,0:T(8,128)(2,1)S(1)} %get-tuple-element.50), channel_id=1, source_target_pairs={{0,8},{4,12},{8,0},{12,4},{16,24},{20,28},{24,16},{28,20},{1,9},{5... | collective-permute-start | bytes 221192 | tf_op jit(solution)/shard_map/ppermute | solution.py:496
  47.3 1.4 %collective-permute-start.19 = (bf16[2,144,128]{2,1,0:T(8,128)(2,1)S(1)}, bf16[2,144,128]{2,1,0:T(8,128)(2,1)S(1)}, u32[]{:S(2)}, u32[]{:S(2)}) collective-permute-start(bf16[2,144,128]{2,1,0:T(8,128)(2,1)S(1)} %get-tuple-element.52), channel_id=1, source_target_pairs={{0,24},{4,28},{8,16},{12,20},{16,8},{20,12},{24,0},{28,4},{1,25},{... | collective-permute-start | bytes 221192 | tf_op jit(solution)/shard_map/ppermute | solution.py:496
  49.6 2.0 %collective-permute-done.18.refs_4_ = bf16[2,144,128]{2,1,0:T(8,128)(2,1)S(1)} collective-permute-done((bf16[2,144,128]{2,1,0:T(8,128)(2,1)S(1)}, bf16[2,144,128]{2,1,0:T(8,128)(2,1)S(1)}, u32[]{:S(2)}, u32[]{:S(2)}) %collective-permute-start.18) | collective-permute-done | bytes 73760 | tf_op jit(solution)/shard_map/ppermute | solution.py:496
  54.7 10.7 %all_to_all.11.refs_0_ = bf16[32,16,128]{2,1,0:T(8,128)(2,1)S(1)} all-to-all(bf16[32,16,128]{2,1,0:T(8,128)(2,1)S(1)} %get-tuple-element.53), channel_id=1, replica_groups=mesh['gx'=8,'gy'=4] {'gx','gy'}, dimensions={0} | all-to-all | bytes 262144 | tf_op jit(solution)/shard_map/all_to_all | solution.py:514
  66.5 1.3 %collective-permute-start.26 = (bf16[16,1152]{1,0:T(8,128)(2,1)S(1)}, bf16[16,1152]{1,0:T(8,128)(2,1)S(1)}, u32[]{:S(2)}, u32[]{:S(2)}) collective-permute-start(bf16[16,1152]{1,0:T(8,128)(2,1)S(1)} %get-tuple-element.55.refs_0_), channel_id=1, source_target_pairs={{0,3},{1,0},{2,1},{3,2},{4,7},{5,4},{6,5},{7,6},{8,11},{9,8},{10,9... | collective-permute-start | bytes 110600 | tf_op jit(solution)/shard_map/ppermute | solution.py:533
  67.7 1.2 %collective-permute-start.24 = (bf16[16,1152]{1,0:T(8,128)(2,1)S(1)}, bf16[16,1152]{1,0:T(8,128)(2,1)S(1)}, u32[]{:S(2)}, u32[]{:S(2)}) collective-permute-start(bf16[16,1152]{1,0:T(8,128)(2,1)S(1)} %get-tuple-element.55.refs_0_), channel_id=1, source_target_pairs={{0,1},{1,2},{2,3},{3,0},{4,5},{5,6},{6,7},{7,4},{8,9},{9,10},{10,1... | collective-permute-start | bytes 110600 | tf_op jit(solution)/shard_map/ppermute | solution.py:533
  68.9 3.9 %shard_map.111 = f32[4,8,4,2,64,64]{5,4,3,2,1,0:T(8,128)} custom-call(f32[8,16,128]{2,1,0:T(8,128)S(1)} %get-tuple-element.56.spec_ref, f32[8,16,128]{2,1,0:T(8,128)S(1)} %get-tuple-element.57.back_ref), custom_call_target="tpu_custom_call" | custom-call | tf_op jit(solution)/shard_map/pallas_call | solution.py:565
  74.9 1.5 %collective-permute-start.28 = (bf16[32,1152]{1,0:T(8,128)(2,1)S(1)}, bf16[32,1152]{1,0:T(8,128)(2,1)S(1)}, u32[]{:S(2)}, u32[]{:S(2)}) collective-permute-start(bf16[32,1152]{1,0:T(8,128)(2,1)S(1)} %shard_map.112.refs_1_), channel_id=1, source_target_pairs={{0,16},{4,20},{8,24},{12,28},{16,0},{20,4},{24,8},{28,12},{1,17},{... | collective-permute-start | bytes 221192 | tf_op jit(solution)/shard_map/ppermute | solution.py:496
  76.4 1.2 %collective-permute-start.27 = (bf16[32,1152]{1,0:T(8,128)(2,1)S(1)}, bf16[32,1152]{1,0:T(8,128)(2,1)S(1)}, u32[]{:S(2)}, u32[]{:S(2)}) collective-permute-start(bf16[32,1152]{1,0:T(8,128)(2,1)S(1)} %shard_map.112.refs_1_), channel_id=1, source_target_pairs={{0,8},{4,12},{8,0},{12,4},{16,24},{20,28},{24,16},{28,20},{1,9},{5... | collective-permute-start | bytes 221192 | tf_op jit(solution)/shard_map/ppermute | solution.py:496
  77.6 1.9 %collective-permute-done.29.refs_4_ = bf16[32,1152]{1,0:T(8,128)(2,1)S(1)} collective-permute-done((bf16[32,1152]{1,0:T(8,128)(2,1)S(1)}, bf16[32,1152]{1,0:T(8,128)(2,1)S(1)}, u32[]{:S(2)}, u32[]{:S(2)}) %collective-permute-start.29) | collective-permute-done | bytes 73760 | tf_op jit(solution)/shard_map/ppermute | solution.py:496
  82.0 1.3 %shard_map.113 = (bf16[16,16,8,64]{3,2,1,0:T(8,128)(2,1)}, f32[64,64]{1,0:T(8,128)}) custom-call(bf16[256,256]{1,0:T(8,128)(2,1)S(1)} %get-tuple-element.34.refs_0_, bf16[32,1152]{1,0:T(8,128)(2,1)S(1)} %shard_map.112.refs_1_, bf16[32,1152]{1,0:T(8,128)(2,1)S(1)} %collective-permute-done.27.refs_2_, bf16[32,1152]{1,0:T(8,128)(2,1)S(1)} %collective-permute-done.28.refs_3_, ...), custom_call_target="tpu_custom_call" | custom-call | tf_op jit(solution)/shard_map/pallas_call | solution.py:438
  (64 shorter events, 19.3 us)
Async XLA Ops:
  2.3 6.5 %collective-permute-start = (bf16[2,128,128]{2,1,0:T(8,128)(2,1)S(1)}, bf16[2,128,128]{2,1,0:T(8,128)(2,1)S(1)}, u32[]{:S(2)}, u32[]{:S(2)}) collective-permute-start(bf16[2,128,128]{2,1,0:T(8,128)(2,1)S(1)} %get-tuple-element.36), channel_id=1, source_target_pairs={{0,24},{4,28},{8,16},{12,20},{16,8},{20,12},{24,0},{28,4},{1,25},{... | collective-permute-start | bytes 196616 | tf_op jit(solution)/shard_map/ppermute | solution.py:496
  6.2 4.3 %collective-permute-start.1 = (bf16[2,128,128]{2,1,0:T(8,128)(2,1)S(1)}, bf16[2,128,128]{2,1,0:T(8,128)(2,1)S(1)}, u32[]{:S(2)}, u32[]{:S(2)}) collective-permute-start(bf16[2,128,128]{2,1,0:T(8,128)(2,1)S(1)} %get-tuple-element.42), channel_id=1, source_target_pairs={{0,8},{4,12},{8,0},{12,4},{16,24},{20,28},{24,16},{28,20},{1,9},{5... | collective-permute-start | bytes 196616 | tf_op jit(solution)/shard_map/ppermute | solution.py:496
  6.8 4.3 %collective-permute-start.2 = (bf16[2,128,128]{2,1,0:T(8,128)(2,1)S(1)}, bf16[2,128,128]{2,1,0:T(8,128)(2,1)S(1)}, u32[]{:S(2)}, u32[]{:S(2)}) collective-permute-start(bf16[2,128,128]{2,1,0:T(8,128)(2,1)S(1)} %get-tuple-element.43), channel_id=1, source_target_pairs={{0,16},{4,20},{8,24},{12,28},{16,0},{20,4},{24,8},{28,12},{1,17},{... | collective-permute-start | bytes 196616 | tf_op jit(solution)/shard_map/ppermute | solution.py:496
  6.9 4.7 %collective-permute-start.3 = (bf16[2,128,128]{2,1,0:T(8,128)(2,1)S(1)}, bf16[2,128,128]{2,1,0:T(8,128)(2,1)S(1)}, u32[]{:S(2)}, u32[]{:S(2)}) collective-permute-start(bf16[2,128,128]{2,1,0:T(8,128)(2,1)S(1)} %get-tuple-element.41.refs_2_), channel_id=1, source_target_pairs={{0,4},{4,0},{8,12},{12,8},{16,20},{20,16},{24,28},{28,24},{1,5},{5... | collective-permute-start | bytes 196616 | tf_op jit(solution)/shard_map/ppermute | solution.py:503
  28.4 4.1 %collective-permute-start.9 = (bf16[16,1024]{1,0:T(8,128)(2,1)S(1)}, bf16[16,1024]{1,0:T(8,128)(2,1)S(1)}, u32[]{:S(2)}, u32[]{:S(2)}) collective-permute-start(bf16[16,1024]{1,0:T(8,128)(2,1)S(1)} %get-tuple-element.45.refs_0_), channel_id=1, source_target_pairs={{0,3},{1,0},{2,1},{3,2},{4,7},{5,4},{6,5},{7,6},{8,11},{9,8},{10,9... | collective-permute-start | bytes 98312 | tf_op jit(solution)/shard_map/ppermute | solution.py:533
  29.6 5.8 %collective-permute-start.8 = (bf16[16,1024]{1,0:T(8,128)(2,1)S(1)}, bf16[16,1024]{1,0:T(8,128)(2,1)S(1)}, u32[]{:S(2)}, u32[]{:S(2)}) collective-permute-start(bf16[16,1024]{1,0:T(8,128)(2,1)S(1)} %get-tuple-element.45.refs_0_), channel_id=1, source_target_pairs={{0,2},{1,3},{2,0},{3,1},{4,6},{5,7},{6,4},{7,5},{8,10},{9,11},{10,... | collective-permute-start | bytes 98312 | tf_op jit(solution)/shard_map/ppermute | solution.py:533
  29.6 5.8 %collective-permute-start.7 = (bf16[16,1024]{1,0:T(8,128)(2,1)S(1)}, bf16[16,1024]{1,0:T(8,128)(2,1)S(1)}, u32[]{:S(2)}, u32[]{:S(2)}) collective-permute-start(bf16[16,1024]{1,0:T(8,128)(2,1)S(1)} %get-tuple-element.45.refs_0_), channel_id=1, source_target_pairs={{0,1},{1,2},{2,3},{3,0},{4,5},{5,6},{6,7},{7,4},{8,9},{9,10},{10,1... | collective-permute-start | bytes 98312 | tf_op jit(solution)/shard_map/ppermute | solution.py:533
  35.8 5.3 %collective-permute-start.12 = (bf16[32,1024]{1,0:T(8,128)(2,1)S(1)}, bf16[32,1024]{1,0:T(8,128)(2,1)S(1)}, u32[]{:S(2)}, u32[]{:S(2)}) collective-permute-start(bf16[32,1024]{1,0:T(8,128)(2,1)S(1)} %shard_map.106.refs_1_), channel_id=1, source_target_pairs={{0,24},{4,28},{8,16},{12,20},{16,8},{20,12},{24,0},{28,4},{1,25},{... | collective-permute-start | bytes 196616 | tf_op jit(solution)/shard_map/ppermute | solution.py:496
  36.8 4.9 %collective-permute-start.11 = (bf16[32,1024]{1,0:T(8,128)(2,1)S(1)}, bf16[32,1024]{1,0:T(8,128)(2,1)S(1)}, u32[]{:S(2)}, u32[]{:S(2)}) collective-permute-start(bf16[32,1024]{1,0:T(8,128)(2,1)S(1)} %shard_map.106.refs_1_), channel_id=1, source_target_pairs={{0,16},{4,20},{8,24},{12,28},{16,0},{20,4},{24,8},{28,12},{1,17},{... | collective-permute-start | bytes 196616 | tf_op jit(solution)/shard_map/ppermute | solution.py:496
  38.1 4.3 %collective-permute-start.10 = (bf16[32,1024]{1,0:T(8,128)(2,1)S(1)}, bf16[32,1024]{1,0:T(8,128)(2,1)S(1)}, u32[]{:S(2)}, u32[]{:S(2)}) collective-permute-start(bf16[32,1024]{1,0:T(8,128)(2,1)S(1)} %shard_map.106.refs_1_), channel_id=1, source_target_pairs={{0,8},{4,12},{8,0},{12,4},{16,24},{20,28},{24,16},{28,20},{1,9},{5... | collective-permute-start | bytes 196616 | tf_op jit(solution)/shard_map/ppermute | solution.py:496
  39.3 3.2 %collective-permute-start.13 = (bf16[32,1024]{1,0:T(8,128)(2,1)S(1)}, bf16[32,1024]{1,0:T(8,128)(2,1)S(1)}, u32[]{:S(2)}, u32[]{:S(2)}) collective-permute-start(bf16[32,1024]{1,0:T(8,128)(2,1)S(1)} %shard_map.106.refs_1_), channel_id=1, source_target_pairs={{0,4},{4,0},{8,12},{12,8},{16,20},{20,16},{24,28},{28,24},{1,5},{5... | collective-permute-start | bytes 196616 | tf_op jit(solution)/shard_map/ppermute | solution.py:503
  41.1 1.5 %collective-permute-start.16 = (bf16[32,1024]{1,0:T(8,128)(2,1)S(1)}, bf16[32,1024]{1,0:T(8,128)(2,1)S(1)}, u32[]{:S(2)}, u32[]{:S(2)}) collective-permute-start(bf16[32,1024]{1,0:T(8,128)(2,1)S(1)} %collective-permute-done.12.refs_4_), channel_id=1, source_target_pairs={{0,4},{4,0},{8,12},{12,8},{16,20},{20,16},{24,28},{28,24},{1,5},{5... | collective-permute-start | bytes 196616 | tf_op jit(solution)/shard_map/ppermute | solution.py:503
  45.2 4.4 %collective-permute-start.17 = (bf16[2,144,128]{2,1,0:T(8,128)(2,1)S(1)}, bf16[2,144,128]{2,1,0:T(8,128)(2,1)S(1)}, u32[]{:S(2)}, u32[]{:S(2)}) collective-permute-start(bf16[2,144,128]{2,1,0:T(8,128)(2,1)S(1)} %get-tuple-element.50), channel_id=1, source_target_pairs={{0,8},{4,12},{8,0},{12,4},{16,24},{20,28},{24,16},{28,20},{1,9},{5... | collective-permute-start | bytes 221192 | tf_op jit(solution)/shard_map/ppermute | solution.py:496
  46.5 5.1 %collective-permute-start.18 = (bf16[2,144,128]{2,1,0:T(8,128)(2,1)S(1)}, bf16[2,144,128]{2,1,0:T(8,128)(2,1)S(1)}, u32[]{:S(2)}, u32[]{:S(2)}) collective-permute-start(bf16[2,144,128]{2,1,0:T(8,128)(2,1)S(1)} %get-tuple-element.51), channel_id=1, source_target_pairs={{0,16},{4,20},{8,24},{12,28},{16,0},{20,4},{24,8},{28,12},{1,17},{... | collective-permute-start | bytes 221192 | tf_op jit(solution)/shard_map/ppermute | solution.py:496
  47.3 5.3 %collective-permute-start.19 = (bf16[2,144,128]{2,1,0:T(8,128)(2,1)S(1)}, bf16[2,144,128]{2,1,0:T(8,128)(2,1)S(1)}, u32[]{:S(2)}, u32[]{:S(2)}) collective-permute-start(bf16[2,144,128]{2,1,0:T(8,128)(2,1)S(1)} %get-tuple-element.52), channel_id=1, source_target_pairs={{0,24},{4,28},{8,16},{12,20},{16,8},{20,12},{24,0},{28,4},{1,25},{... | collective-permute-start | bytes 221192 | tf_op jit(solution)/shard_map/ppermute | solution.py:496
  48.7 3.8 %collective-permute-start.20 = (bf16[2,144,128]{2,1,0:T(8,128)(2,1)S(1)}, bf16[2,144,128]{2,1,0:T(8,128)(2,1)S(1)}, u32[]{:S(2)}, u32[]{:S(2)}) collective-permute-start(bf16[2,144,128]{2,1,0:T(8,128)(2,1)S(1)} %get-tuple-element.49.refs_2_), channel_id=1, source_target_pairs={{0,4},{4,0},{8,12},{12,8},{16,20},{20,16},{24,28},{28,24},{1,5},{5... | collective-permute-start | bytes 221192 | tf_op jit(solution)/shard_map/ppermute | solution.py:503
  49.6 3.0 %collective-permute-start.21 = (bf16[2,144,128]{2,1,0:T(8,128)(2,1)S(1)}, bf16[2,144,128]{2,1,0:T(8,128)(2,1)S(1)}, u32[]{:S(2)}, u32[]{:S(2)}) collective-permute-start(bf16[2,144,128]{2,1,0:T(8,128)(2,1)S(1)} %collective-permute-done.17.refs_3_), channel_id=1, source_target_pairs={{0,4},{4,0},{8,12},{12,8},{16,20},{20,16},{24,28},{28,24},{1,5},{5... | collective-permute-start | bytes 221192 | tf_op jit(solution)/shard_map/ppermute | solution.py:503
  66.5 6.4 %collective-permute-start.26 = (bf16[16,1152]{1,0:T(8,128)(2,1)S(1)}, bf16[16,1152]{1,0:T(8,128)(2,1)S(1)}, u32[]{:S(2)}, u32[]{:S(2)}) collective-permute-start(bf16[16,1152]{1,0:T(8,128)(2,1)S(1)} %get-tuple-element.55.refs_0_), channel_id=1, source_target_pairs={{0,3},{1,0},{2,1},{3,2},{4,7},{5,4},{6,5},{7,6},{8,11},{9,8},{10,9... | collective-permute-start | bytes 110600 | tf_op jit(solution)/shard_map/ppermute | solution.py:533
  67.7 6.0 %collective-permute-start.25 = (bf16[16,1152]{1,0:T(8,128)(2,1)S(1)}, bf16[16,1152]{1,0:T(8,128)(2,1)S(1)}, u32[]{:S(2)}, u32[]{:S(2)}) collective-permute-start(bf16[16,1152]{1,0:T(8,128)(2,1)S(1)} %get-tuple-element.55.refs_0_), channel_id=1, source_target_pairs={{0,2},{1,3},{2,0},{3,1},{4,6},{5,7},{6,4},{7,5},{8,10},{9,11},{10,... | collective-permute-start | bytes 110600 | tf_op jit(solution)/shard_map/ppermute | solution.py:533
  67.7 6.0 %collective-permute-start.24 = (bf16[16,1152]{1,0:T(8,128)(2,1)S(1)}, bf16[16,1152]{1,0:T(8,128)(2,1)S(1)}, u32[]{:S(2)}, u32[]{:S(2)}) collective-permute-start(bf16[16,1152]{1,0:T(8,128)(2,1)S(1)} %get-tuple-element.55.refs_0_), channel_id=1, source_target_pairs={{0,1},{1,2},{2,3},{3,0},{4,5},{5,6},{6,7},{7,4},{8,9},{9,10},{10,1... | collective-permute-start | bytes 110600 | tf_op jit(solution)/shard_map/ppermute | solution.py:533
  74.1 5.4 %collective-permute-start.29 = (bf16[32,1152]{1,0:T(8,128)(2,1)S(1)}, bf16[32,1152]{1,0:T(8,128)(2,1)S(1)}, u32[]{:S(2)}, u32[]{:S(2)}) collective-permute-start(bf16[32,1152]{1,0:T(8,128)(2,1)S(1)} %shard_map.112.refs_1_), channel_id=1, source_target_pairs={{0,24},{4,28},{8,16},{12,20},{16,8},{20,12},{24,0},{28,4},{1,25},{... | collective-permute-start | bytes 221192 | tf_op jit(solution)/shard_map/ppermute | solution.py:496
  74.9 5.1 %collective-permute-start.28 = (bf16[32,1152]{1,0:T(8,128)(2,1)S(1)}, bf16[32,1152]{1,0:T(8,128)(2,1)S(1)}, u32[]{:S(2)}, u32[]{:S(2)}) collective-permute-start(bf16[32,1152]{1,0:T(8,128)(2,1)S(1)} %shard_map.112.refs_1_), channel_id=1, source_target_pairs={{0,16},{4,20},{8,24},{12,28},{16,0},{20,4},{24,8},{28,12},{1,17},{... | collective-permute-start | bytes 221192 | tf_op jit(solution)/shard_map/ppermute | solution.py:496
  76.4 4.4 %collective-permute-start.27 = (bf16[32,1152]{1,0:T(8,128)(2,1)S(1)}, bf16[32,1152]{1,0:T(8,128)(2,1)S(1)}, u32[]{:S(2)}, u32[]{:S(2)}) collective-permute-start(bf16[32,1152]{1,0:T(8,128)(2,1)S(1)} %shard_map.112.refs_1_), channel_id=1, source_target_pairs={{0,8},{4,12},{8,0},{12,4},{16,24},{20,28},{24,16},{28,20},{1,9},{5... | collective-permute-start | bytes 221192 | tf_op jit(solution)/shard_map/ppermute | solution.py:496
  77.6 3.1 %collective-permute-start.30 = (bf16[32,1152]{1,0:T(8,128)(2,1)S(1)}, bf16[32,1152]{1,0:T(8,128)(2,1)S(1)}, u32[]{:S(2)}, u32[]{:S(2)}) collective-permute-start(bf16[32,1152]{1,0:T(8,128)(2,1)S(1)} %shard_map.112.refs_1_), channel_id=1, source_target_pairs={{0,4},{4,0},{8,12},{12,8},{16,20},{20,16},{24,28},{28,24},{1,5},{5... | collective-permute-start | bytes 221192 | tf_op jit(solution)/shard_map/ppermute | solution.py:503
  (13 other events, 80.3 us)

commit v5 on v4

--- a/solution.py
+++ b/solution.py
@@ -206,9 +206,12 @@
     store_steps(chunk_ref, send_refs)
 
 
-def pairs_kernel(field_ref, pairs_ref):
-    for p, pair in enumerate(pairs_of(field_ref)):
+def ready_kernel(cot_ref, field_ref, conv_ref, pairs_ref, mapped_ref, turned_ref):
+    for p, pair in enumerate(pairs_of(cot_ref)):
         pairs_ref[p] = pair.astype(BF)
+        field = field_ref[p]
+        mapped_ref[p] = dot(field, conv_ref[...])
+        turned_ref[p] = field.astype(F32).T.astype(BF)
 
 
 def joined(value):
@@ -376,14 +379,14 @@
     grad = jnp.zeros((LANES, LANES), F32)
     for p in range(count):
         field = field_ref[p]
-        pre = cells[:, p * LANES : (p + 1) * LANES] + dot(field, conv_ref[...])
+        pre = cells[:, p * LANES : (p + 1) * LANES] + conv_ref[p]
         cdf = normal_cdf(pre)
         store_pair(act_ref, p, pre * cdf)
         slope = cot_ref[p].astype(F32) * (cdf + pre * normal_pdf(pre))
         narrow = slope.astype(BF)
         slope_ref[p] = narrow
         slopes.append(narrow.astype(F32))
-        grad = grad + dot(field, narrow, ((0,), (0,)))
+        grad = grad + dot(field, narrow)
     rows = slopes[0].shape[0]
     chans = LANES // 2
     grad = grad[:chans, :chans] + grad[chans:, chans:]
@@ -467,7 +470,6 @@
         features,
         scratch=[pltpu.VMEM((parts_x, cells, LANES), BF)],
     )
-    cot = call(pairs_kernel, sds((half_y, cells, LANES), BF), cotangent)
     outside = pl.BlockSpec(memory_space=pltpu.HBM)
     inside = pl.BlockSpec(memory_space=pltpu.VMEM)
     line_table, column_table, column_back, line_back, conv_pair, conv_turn = pl.pallas_call(
@@ -545,7 +547,15 @@
 
     recv, _, tables = to_modes(send, first, False, (line_table, column_table))
     send, spec = mix(recv, True, [])
-    pieces, _ = to_lines(send)
+    pair_shape = (half_y, cells, LANES)
+    ready = call(
+        ready_kernel,
+        (sds(pair_shape, BF), sds(pair_shape, F32), sds((half_y, LANES, cells), BF)),
+        cotangent,
+        field,
+        conv_pair,
+    )
+    pieces, (cot, mapped, turned) = to_lines(send, ready)
     activation, slope, *send = call(
         bind(point_kernel, second),
         (
@@ -555,8 +565,8 @@
         + (sds((2, cells + EXTRA, LANES), BF),) * SIDES,
         line_back,
         *pieces,
-        conv_pair,
-        field,
+        mapped,
+        turned,
         cot,
         scratch=[pltpu.VMEM((parts_x, cells + EXTRA, LANES), BF)],
     )

time: 83.6 us -> 83.5 us (level)
  no operation moved by 1% of the time
where the time goes in v5:
time: 83.5 us; the launch traced here: 83.3 us
  blocking collectives  23.8 us (29%)
  waiting for transfers between devices  22.1 us (26%)
  starting transfers between devices  20.6 us (25%)
  Pallas kernels  14.7 us (18%)
  local copies, waits for them, and re-layouts  1.19 us (1%)
    all_to_all x2, blocking collectives, to_modes(): return (lax.all_to_all(send, ('gx', 'gy'), 0, 0, tiled=True), rest, tables)  23.8 us
    ppermute x12, starting transfers between devices, cross(): lax.ppermute(piece, 'gx', [(i, i ^ 2 * t) for i in range(parts_x)])  15.2 us
    ppermute x12, waiting for transfers between devices, cross(): lax.ppermute(piece, 'gx', [(i, i ^ 2 * t) for i in range(parts_x)])  12.2 us
    pallas_call x10, Pallas kernels, call(): pl.pallas_call(kernel, out_shape=outs, scratch_shapes=list(scratch), comp...  8.95 us
    ppermute x6, waiting for transfers between devices, to_lines(): pieces.append(lax.ppermute(send, 'gy', ring))  5.17 us
    ppermute x6, starting transfers between devices, to_lines(): pieces.append(lax.ppermute(send, 'gy', ring))  4.9 us
    ppermute x16, waiting for transfers between devices, cross(): pieces = pieces + [lax.ppermute(piece, 'gx', swap) for piece in pieces]  4.66 us
    pallas_call x1, Pallas kernels, fast(): pl.pallas_call(outer_kernel, in_specs=[inside] * 2, out_specs=outside, ou...  3.92 us
  transfers between devices with their start and end apart: 34, of which 23 were waited for; matrix products, arithmetic and copies ran while one was open for 0% of the time, Pallas kernels for 7%

profile of v5, /device:TPU:0, one launch (start us, length us, event | category | flops | bytes accessed | tf_op | source)
XLA Modules:
  0.0 83.3 jit_solution(16968575439753710723)
XLA Ops:
  2.3 4.0 %collective-permute-start = (bf16[2,128,128]{2,1,0:T(8,128)(2,1)S(1)}, bf16[2,128,128]{2,1,0:T(8,128)(2,1)S(1)}, u32[]{:S(2)}, u32[]{:S(2)}) collective-permute-start(bf16[2,128,128]{2,1,0:T(8,128)(2,1)S(1)} %get-tuple-element.43), channel_id=1, source_target_pairs={{0,24},{4,28},{8,16},{12,20},{16,8},{20,12},{24,0},{28,4},{1,25},{... | collective-permute-start | bytes 196616 | tf_op jit(solution)/shard_map/ppermute | solution.py:498
  6.9 1.9 %shard_map.102 = (bf16[512,1024]{1,0:T(8,128)(2,1)S(1)}, bf16[512,512]{1,0:T(8,128)(2,1)S(1)}, bf16[64,64]{1,0:T(8,128)(2,1)S(1)}, bf16[256,256]{1,0:T(8,128)(2,...) custom-call(s32[32]{0:T(128)} %refs_0_.1, s32[32]{0:T(128)} %refs_1_.3, s32[4]{0:T(128)} %refs_2_.1, ...), custom_call_target="tpu_custom_call" | custom-call | tf_op jit(solution)/shard_map/pallas_call | solution.py:475
  8.7 1.7 %collective-permute-done.1.refs_3_ = bf16[2,128,128]{2,1,0:T(8,128)(2,1)S(1)} collective-permute-done((bf16[2,128,128]{2,1,0:T(8,128)(2,1)S(1)}, bf16[2,128,128]{2,1,0:T(8,128)(2,1)S(1)}, u32[]{:S(2)}, u32[]{:S(2)}) %collective-permute-start.1) | collective-permute-done | bytes 65568 | tf_op jit(solution)/shard_map/ppermute | solution.py:498
  13.3 13.1 %all_to_all.10.refs_0_ = bf16[32,16,128]{2,1,0:T(8,128)(2,1)S(1)} all-to-all(bf16[32,16,128]{2,1,0:T(8,128)(2,1)S(1)} %shard_map.104), channel_id=1, replica_groups=mesh['gx'=8,'gy'=4] {'gx','gy'}, dimensions={0} | all-to-all | bytes 262144 | tf_op jit(solution)/shard_map/all_to_all | solution.py:516
  26.4 2.0 %shard_map.105 = (bf16[16,1024]{1,0:T(8,128)(2,1)S(1)}, f32[8,16,128]{2,1,0:T(8,128)S(1)}) custom-call(bf16[32,16,128]{2,1,0:T(8,128)(2,1)S(1)} %all_to_all.10.refs_0_, bf16[4,8,4,2,64,64]{5,4,3,2,1,0:T(8,128)(2,1)S(1)} %copy-done), custom_call_target="tpu_custom_call" | custom-call | tf_op jit(solution)/shard_map/pallas_call | solution.py:441
  28.4 1.3 %collective-permute-start.9 = (bf16[16,1024]{1,0:T(8,128)(2,1)S(1)}, bf16[16,1024]{1,0:T(8,128)(2,1)S(1)}, u32[]{:S(2)}, u32[]{:S(2)}) collective-permute-start(bf16[16,1024]{1,0:T(8,128)(2,1)S(1)} %get-tuple-element.52.refs_0_), channel_id=1, source_target_pairs={{0,3},{1,0},{2,1},{3,2},{4,7},{5,4},{6,5},{7,6},{8,11},{9,8},{10,9... | collective-permute-start | bytes 98312 | tf_op jit(solution)/shard_map/ppermute | solution.py:535
  29.6 1.2 %collective-permute-start.7 = (bf16[16,1024]{1,0:T(8,128)(2,1)S(1)}, bf16[16,1024]{1,0:T(8,128)(2,1)S(1)}, u32[]{:S(2)}, u32[]{:S(2)}) collective-permute-start(bf16[16,1024]{1,0:T(8,128)(2,1)S(1)} %get-tuple-element.52.refs_0_), channel_id=1, source_target_pairs={{0,1},{1,2},{2,3},{3,0},{4,5},{5,6},{6,7},{7,4},{8,9},{9,10},{10,1... | collective-permute-start | bytes 98312 | tf_op jit(solution)/shard_map/ppermute | solution.py:535
  31.1 1.4 %collective-permute-done.9.refs_3_ = bf16[16,1024]{1,0:T(8,128)(2,1)S(1)} collective-permute-done((bf16[16,1024]{1,0:T(8,128)(2,1)S(1)}, bf16[16,1024]{1,0:T(8,128)(2,1)S(1)}, u32[]{:S(2)}, u32[]{:S(2)}) %collective-permute-start.9) | collective-permute-done | bytes 32800 | tf_op jit(solution)/shard_map/ppermute | solution.py:535
  32.5 3.0 %collective-permute-done.8.refs_2_ = bf16[16,1024]{1,0:T(8,128)(2,1)S(1)} collective-permute-done((bf16[16,1024]{1,0:T(8,128)(2,1)S(1)}, bf16[16,1024]{1,0:T(8,128)(2,1)S(1)}, u32[]{:S(2)}, u32[]{:S(2)}) %collective-permute-start.8) | collective-permute-done | bytes 32800 | tf_op jit(solution)/shard_map/ppermute | solution.py:535
  36.8 1.4 %collective-permute-start.11 = (bf16[32,1024]{1,0:T(8,128)(2,1)S(1)}, bf16[32,1024]{1,0:T(8,128)(2,1)S(1)}, u32[]{:S(2)}, u32[]{:S(2)}) collective-permute-start(bf16[32,1024]{1,0:T(8,128)(2,1)S(1)} %shard_map.107.refs_1_), channel_id=1, source_target_pairs={{0,16},{4,20},{8,24},{12,28},{16,0},{20,4},{24,8},{28,12},{1,17},{... | collective-permute-start | bytes 196616 | tf_op jit(solution)/shard_map/ppermute | solution.py:498
  38.1 1.2 %collective-permute-start.10 = (bf16[32,1024]{1,0:T(8,128)(2,1)S(1)}, bf16[32,1024]{1,0:T(8,128)(2,1)S(1)}, u32[]{:S(2)}, u32[]{:S(2)}) collective-permute-start(bf16[32,1024]{1,0:T(8,128)(2,1)S(1)} %shard_map.107.refs_1_), channel_id=1, source_target_pairs={{0,8},{4,12},{8,0},{12,4},{16,24},{20,28},{24,16},{28,20},{1,9},{5... | collective-permute-start | bytes 196616 | tf_op jit(solution)/shard_map/ppermute | solution.py:498
  39.3 1.7 %collective-permute-done.12.refs_4_ = bf16[32,1024]{1,0:T(8,128)(2,1)S(1)} collective-permute-done((bf16[32,1024]{1,0:T(8,128)(2,1)S(1)}, bf16[32,1024]{1,0:T(8,128)(2,1)S(1)}, u32[]{:S(2)}, u32[]{:S(2)}) %collective-permute-start.12) | collective-permute-done | bytes 65568 | tf_op jit(solution)/shard_map/ppermute | solution.py:498
  43.6 1.5 %shard_map.108 = (bf16[16,16,8,64]{3,2,1,0:T(8,128)(2,1)}, bf16[8,128,128]{2,1,0:T(8,128)(2,1)S(1)}, bf16[2,144,128]{2,1,0:T(8,128)(2,1)S(1)}, bf16[2,144,128]{2...) custom-call(bf16[256,256]{1,0:T(8,128)(2,1)S(1)} %get-tuple-element.41.refs_0_, ...), custom_call_target="tpu_custom_call" | custom-call | tf_op jit(solution)/shard_map/pallas_call | solution.py:441
  45.2 1.2 %collective-permute-start.17 = (bf16[2,144,128]{2,1,0:T(8,128)(2,1)S(1)}, bf16[2,144,128]{2,1,0:T(8,128)(2,1)S(1)}, u32[]{:S(2)}, u32[]{:S(2)}) collective-permute-start(bf16[2,144,128]{2,1,0:T(8,128)(2,1)S(1)} %get-tuple-element.64), channel_id=1, source_target_pairs={{0,8},{4,12},{8,0},{12,4},{16,24},{20,28},{24,16},{28,20},{1,9},{5... | collective-permute-start | bytes 221192 | tf_op jit(solution)/shard_map/ppermute | solution.py:498
  47.2 1.4 %collective-permute-start.19 = (bf16[2,144,128]{2,1,0:T(8,128)(2,1)S(1)}, bf16[2,144,128]{2,1,0:T(8,128)(2,1)S(1)}, u32[]{:S(2)}, u32[]{:S(2)}) collective-permute-start(bf16[2,144,128]{2,1,0:T(8,128)(2,1)S(1)} %get-tuple-element.66), channel_id=1, source_target_pairs={{0,24},{4,28},{8,16},{12,20},{16,8},{20,12},{24,0},{28,4},{1,25},{... | collective-permute-start | bytes 221192 | tf_op jit(solution)/shard_map/ppermute | solution.py:498
  49.5 2.0 %collective-permute-done.18.refs_4_ = bf16[2,144,128]{2,1,0:T(8,128)(2,1)S(1)} collective-permute-done((bf16[2,144,128]{2,1,0:T(8,128)(2,1)S(1)}, bf16[2,144,128]{2,1,0:T(8,128)(2,1)S(1)}, u32[]{:S(2)}, u32[]{:S(2)}) %collective-permute-start.18) | collective-permute-done | bytes 73760 | tf_op jit(solution)/shard_map/ppermute | solution.py:498
  54.6 10.7 %all_to_all.11.refs_0_ = bf16[32,16,128]{2,1,0:T(8,128)(2,1)S(1)} all-to-all(bf16[32,16,128]{2,1,0:T(8,128)(2,1)S(1)} %get-tuple-element.67), channel_id=1, replica_groups=mesh['gx'=8,'gy'=4] {'gx','gy'}, dimensions={0} | all-to-all | bytes 262144 | tf_op jit(solution)/shard_map/all_to_all | solution.py:516
  66.4 1.3 %collective-permute-start.26 = (bf16[16,1152]{1,0:T(8,128)(2,1)S(1)}, bf16[16,1152]{1,0:T(8,128)(2,1)S(1)}, u32[]{:S(2)}, u32[]{:S(2)}) collective-permute-start(bf16[16,1152]{1,0:T(8,128)(2,1)S(1)} %get-tuple-element.69.refs_0_), channel_id=1, source_target_pairs={{0,3},{1,0},{2,1},{3,2},{4,7},{5,4},{6,5},{7,6},{8,11},{9,8},{10,9... | collective-permute-start | bytes 110600 | tf_op jit(solution)/shard_map/ppermute | solution.py:535
  67.7 1.2 %collective-permute-start.24 = (bf16[16,1152]{1,0:T(8,128)(2,1)S(1)}, bf16[16,1152]{1,0:T(8,128)(2,1)S(1)}, u32[]{:S(2)}, u32[]{:S(2)}) collective-permute-start(bf16[16,1152]{1,0:T(8,128)(2,1)S(1)} %get-tuple-element.69.refs_0_), channel_id=1, source_target_pairs={{0,1},{1,2},{2,3},{3,0},{4,5},{5,6},{6,7},{7,4},{8,9},{9,10},{10,1... | collective-permute-start | bytes 110600 | tf_op jit(solution)/shard_map/ppermute | solution.py:535
  68.8 3.9 %shard_map.111 = f32[4,8,4,2,64,64]{5,4,3,2,1,0:T(8,128)} custom-call(f32[8,16,128]{2,1,0:T(8,128)S(1)} %get-tuple-element.70.spec_ref, f32[8,16,128]{2,1,0:T(8,128)S(1)} %get-tuple-element.71.back_ref), custom_call_target="tpu_custom_call" | custom-call | tf_op jit(solution)/shard_map/pallas_call | solution.py:575
  74.8 1.5 %collective-permute-start.28 = (bf16[32,1152]{1,0:T(8,128)(2,1)S(1)}, bf16[32,1152]{1,0:T(8,128)(2,1)S(1)}, u32[]{:S(2)}, u32[]{:S(2)}) collective-permute-start(bf16[32,1152]{1,0:T(8,128)(2,1)S(1)} %shard_map.112.refs_1_), channel_id=1, source_target_pairs={{0,16},{4,20},{8,24},{12,28},{16,0},{20,4},{24,8},{28,12},{1,17},{... | collective-permute-start | bytes 221192 | tf_op jit(solution)/shard_map/ppermute | solution.py:498
  76.3 1.2 %collective-permute-start.27 = (bf16[32,1152]{1,0:T(8,128)(2,1)S(1)}, bf16[32,1152]{1,0:T(8,128)(2,1)S(1)}, u32[]{:S(2)}, u32[]{:S(2)}) collective-permute-start(bf16[32,1152]{1,0:T(8,128)(2,1)S(1)} %shard_map.112.refs_1_), channel_id=1, source_target_pairs={{0,8},{4,12},{8,0},{12,4},{16,24},{20,28},{24,16},{28,20},{1,9},{5... | collective-permute-start | bytes 221192 | tf_op jit(solution)/shard_map/ppermute | solution.py:498
  77.5 1.9 %collective-permute-done.29.refs_4_ = bf16[32,1152]{1,0:T(8,128)(2,1)S(1)} collective-permute-done((bf16[32,1152]{1,0:T(8,128)(2,1)S(1)}, bf16[32,1152]{1,0:T(8,128)(2,1)S(1)}, u32[]{:S(2)}, u32[]{:S(2)}) %collective-permute-start.29) | collective-permute-done | bytes 73760 | tf_op jit(solution)/shard_map/ppermute | solution.py:498
  81.9 1.3 %shard_map.113 = (bf16[16,16,8,64]{3,2,1,0:T(8,128)(2,1)}, f32[64,64]{1,0:T(8,128)}) custom-call(bf16[256,256]{1,0:T(8,128)(2,1)S(1)} %get-tuple-element.41.refs_0_, bf16[32,1152]{1,0:T(8,128)(2,1)S(1)} %shard_map.112.refs_1_, bf16[32,1152]{1,0:T(8,128)(2,1)S(1)} %collective-permute-done.27.refs_2_, bf16[32,1152]{1,0:T(8,128)(2,1)S(1)} %collective-permute-done.28.refs_3_, ...), custom_call_target="tpu_custom_call" | custom-call | tf_op jit(solution)/shard_map/pallas_call | solution.py:441
  (64 shorter events, 19.6 us)
Async XLA Ops:
  2.3 6.5 %collective-permute-start = (bf16[2,128,128]{2,1,0:T(8,128)(2,1)S(1)}, bf16[2,128,128]{2,1,0:T(8,128)(2,1)S(1)}, u32[]{:S(2)}, u32[]{:S(2)}) collective-permute-start(bf16[2,128,128]{2,1,0:T(8,128)(2,1)S(1)} %get-tuple-element.43), channel_id=1, source_target_pairs={{0,24},{4,28},{8,16},{12,20},{16,8},{20,12},{24,0},{28,4},{1,25},{... | collective-permute-start | bytes 196616 | tf_op jit(solution)/shard_map/ppermute | solution.py:498
  6.2 4.3 %collective-permute-start.1 = (bf16[2,128,128]{2,1,0:T(8,128)(2,1)S(1)}, bf16[2,128,128]{2,1,0:T(8,128)(2,1)S(1)}, u32[]{:S(2)}, u32[]{:S(2)}) collective-permute-start(bf16[2,128,128]{2,1,0:T(8,128)(2,1)S(1)} %get-tuple-element.49), channel_id=1, source_target_pairs={{0,8},{4,12},{8,0},{12,4},{16,24},{20,28},{24,16},{28,20},{1,9},{5... | collective-permute-start | bytes 196616 | tf_op jit(solution)/shard_map/ppermute | solution.py:498
  6.8 4.3 %collective-permute-start.2 = (bf16[2,128,128]{2,1,0:T(8,128)(2,1)S(1)}, bf16[2,128,128]{2,1,0:T(8,128)(2,1)S(1)}, u32[]{:S(2)}, u32[]{:S(2)}) collective-permute-start(bf16[2,128,128]{2,1,0:T(8,128)(2,1)S(1)} %get-tuple-element.50), channel_id=1, source_target_pairs={{0,16},{4,20},{8,24},{12,28},{16,0},{20,4},{24,8},{28,12},{1,17},{... | collective-permute-start | bytes 196616 | tf_op jit(solution)/shard_map/ppermute | solution.py:498
  6.9 4.7 %collective-permute-start.3 = (bf16[2,128,128]{2,1,0:T(8,128)(2,1)S(1)}, bf16[2,128,128]{2,1,0:T(8,128)(2,1)S(1)}, u32[]{:S(2)}, u32[]{:S(2)}) collective-permute-start(bf16[2,128,128]{2,1,0:T(8,128)(2,1)S(1)} %get-tuple-element.48.refs_2_), channel_id=1, source_target_pairs={{0,4},{4,0},{8,12},{12,8},{16,20},{20,16},{24,28},{28,24},{1,5},{5... | collective-permute-start | bytes 196616 | tf_op jit(solution)/shard_map/ppermute | solution.py:505
  11.0 1.4 %collective-permute-start.6 = (bf16[2,128,128]{2,1,0:T(8,128)(2,1)S(1)}, bf16[2,128,128]{2,1,0:T(8,128)(2,1)S(1)}, u32[]{:S(2)}, u32[]{:S(2)}) collective-permute-start(bf16[2,128,128]{2,1,0:T(8,128)(2,1)S(1)} %collective-permute-done.refs_5_), channel_id=1, source_target_pairs={{0,4},{4,0},{8,12},{12,8},{16,20},{20,16},{24,28},{28,24},{1,5},{5... | collective-permute-start | bytes 196616 | tf_op jit(solution)/shard_map/ppermute | solution.py:505
  28.4 4.1 %collective-permute-start.9 = (bf16[16,1024]{1,0:T(8,128)(2,1)S(1)}, bf16[16,1024]{1,0:T(8,128)(2,1)S(1)}, u32[]{:S(2)}, u32[]{:S(2)}) collective-permute-start(bf16[16,1024]{1,0:T(8,128)(2,1)S(1)} %get-tuple-element.52.refs_0_), channel_id=1, source_target_pairs={{0,3},{1,0},{2,1},{3,2},{4,7},{5,4},{6,5},{7,6},{8,11},{9,8},{10,9... | collective-permute-start | bytes 98312 | tf_op jit(solution)/shard_map/ppermute | solution.py:535
  29.6 5.8 %collective-permute-start.8 = (bf16[16,1024]{1,0:T(8,128)(2,1)S(1)}, bf16[16,1024]{1,0:T(8,128)(2,1)S(1)}, u32[]{:S(2)}, u32[]{:S(2)}) collective-permute-start(bf16[16,1024]{1,0:T(8,128)(2,1)S(1)} %get-tuple-element.52.refs_0_), channel_id=1, source_target_pairs={{0,2},{1,3},{2,0},{3,1},{4,6},{5,7},{6,4},{7,5},{8,10},{9,11},{10,... | collective-permute-start | bytes 98312 | tf_op jit(solution)/shard_map/ppermute | solution.py:535
  29.6 5.8 %collective-permute-start.7 = (bf16[16,1024]{1,0:T(8,128)(2,1)S(1)}, bf16[16,1024]{1,0:T(8,128)(2,1)S(1)}, u32[]{:S(2)}, u32[]{:S(2)}) collective-permute-start(bf16[16,1024]{1,0:T(8,128)(2,1)S(1)} %get-tuple-element.52.refs_0_), channel_id=1, source_target_pairs={{0,1},{1,2},{2,3},{3,0},{4,5},{5,6},{6,7},{7,4},{8,9},{9,10},{10,1... | collective-permute-start | bytes 98312 | tf_op jit(solution)/shard_map/ppermute | solution.py:535
  35.8 5.3 %collective-permute-start.12 = (bf16[32,1024]{1,0:T(8,128)(2,1)S(1)}, bf16[32,1024]{1,0:T(8,128)(2,1)S(1)}, u32[]{:S(2)}, u32[]{:S(2)}) collective-permute-start(bf16[32,1024]{1,0:T(8,128)(2,1)S(1)} %shard_map.107.refs_1_), channel_id=1, source_target_pairs={{0,24},{4,28},{8,16},{12,20},{16,8},{20,12},{24,0},{28,4},{1,25},{... | collective-permute-start | bytes 196616 | tf_op jit(solution)/shard_map/ppermute | solution.py:498
  36.8 4.9 %collective-permute-start.11 = (bf16[32,1024]{1,0:T(8,128)(2,1)S(1)}, bf16[32,1024]{1,0:T(8,128)(2,1)S(1)}, u32[]{:S(2)}, u32[]{:S(2)}) collective-permute-start(bf16[32,1024]{1,0:T(8,128)(2,1)S(1)} %shard_map.107.refs_1_), channel_id=1, source_target_pairs={{0,16},{4,20},{8,24},{12,28},{16,0},{20,4},{24,8},{28,12},{1,17},{... | collective-permute-start | bytes 196616 | tf_op jit(solution)/shard_map/ppermute | solution.py:498
  38.1 4.3 %collective-permute-start.10 = (bf16[32,1024]{1,0:T(8,128)(2,1)S(1)}, bf16[32,1024]{1,0:T(8,128)(2,1)S(1)}, u32[]{:S(2)}, u32[]{:S(2)}) collective-permute-start(bf16[32,1024]{1,0:T(8,128)(2,1)S(1)} %shard_map.107.refs_1_), channel_id=1, source_target_pairs={{0,8},{4,12},{8,0},{12,4},{16,24},{20,28},{24,16},{28,20},{1,9},{5... | collective-permute-start | bytes 196616 | tf_op jit(solution)/shard_map/ppermute | solution.py:498
  39.3 3.1 %collective-permute-start.13 = (bf16[32,1024]{1,0:T(8,128)(2,1)S(1)}, bf16[32,1024]{1,0:T(8,128)(2,1)S(1)}, u32[]{:S(2)}, u32[]{:S(2)}) collective-permute-start(bf16[32,1024]{1,0:T(8,128)(2,1)S(1)} %shard_map.107.refs_1_), channel_id=1, source_target_pairs={{0,4},{4,0},{8,12},{12,8},{16,20},{20,16},{24,28},{28,24},{1,5},{5... | collective-permute-start | bytes 196616 | tf_op jit(solution)/shard_map/ppermute | solution.py:505
  45.2 4.4 %collective-permute-start.17 = (bf16[2,144,128]{2,1,0:T(8,128)(2,1)S(1)}, bf16[2,144,128]{2,1,0:T(8,128)(2,1)S(1)}, u32[]{:S(2)}, u32[]{:S(2)}) collective-permute-start(bf16[2,144,128]{2,1,0:T(8,128)(2,1)S(1)} %get-tuple-element.64), channel_id=1, source_target_pairs={{0,8},{4,12},{8,0},{12,4},{16,24},{20,28},{24,16},{28,20},{1,9},{5... | collective-permute-start | bytes 221192 | tf_op jit(solution)/shard_map/ppermute | solution.py:498
  46.4 5.1 %collective-permute-start.18 = (bf16[2,144,128]{2,1,0:T(8,128)(2,1)S(1)}, bf16[2,144,128]{2,1,0:T(8,128)(2,1)S(1)}, u32[]{:S(2)}, u32[]{:S(2)}) collective-permute-start(bf16[2,144,128]{2,1,0:T(8,128)(2,1)S(1)} %get-tuple-element.65), channel_id=1, source_target_pairs={{0,16},{4,20},{8,24},{12,28},{16,0},{20,4},{24,8},{28,12},{1,17},{... | collective-permute-start | bytes 221192 | tf_op jit(solution)/shard_map/ppermute | solution.py:498
  47.2 5.3 %collective-permute-start.19 = (bf16[2,144,128]{2,1,0:T(8,128)(2,1)S(1)}, bf16[2,144,128]{2,1,0:T(8,128)(2,1)S(1)}, u32[]{:S(2)}, u32[]{:S(2)}) collective-permute-start(bf16[2,144,128]{2,1,0:T(8,128)(2,1)S(1)} %get-tuple-element.66), channel_id=1, source_target_pairs={{0,24},{4,28},{8,16},{12,20},{16,8},{20,12},{24,0},{28,4},{1,25},{... | collective-permute-start | bytes 221192 | tf_op jit(solution)/shard_map/ppermute | solution.py:498
  48.6 3.8 %collective-permute-start.20 = (bf16[2,144,128]{2,1,0:T(8,128)(2,1)S(1)}, bf16[2,144,128]{2,1,0:T(8,128)(2,1)S(1)}, u32[]{:S(2)}, u32[]{:S(2)}) collective-permute-start(bf16[2,144,128]{2,1,0:T(8,128)(2,1)S(1)} %get-tuple-element.63.refs_2_), channel_id=1, source_target_pairs={{0,4},{4,0},{8,12},{12,8},{16,20},{20,16},{24,28},{28,24},{1,5},{5... | collective-permute-start | bytes 221192 | tf_op jit(solution)/shard_map/ppermute | solution.py:505
  49.5 2.9 %collective-permute-start.21 = (bf16[2,144,128]{2,1,0:T(8,128)(2,1)S(1)}, bf16[2,144,128]{2,1,0:T(8,128)(2,1)S(1)}, u32[]{:S(2)}, u32[]{:S(2)}) collective-permute-start(bf16[2,144,128]{2,1,0:T(8,128)(2,1)S(1)} %collective-permute-done.17.refs_3_), channel_id=1, source_target_pairs={{0,4},{4,0},{8,12},{12,8},{16,20},{20,16},{24,28},{28,24},{1,5},{5... | collective-permute-start | bytes 221192 | tf_op jit(solution)/shard_map/ppermute | solution.py:505
  66.4 6.4 %collective-permute-start.26 = (bf16[16,1152]{1,0:T(8,128)(2,1)S(1)}, bf16[16,1152]{1,0:T(8,128)(2,1)S(1)}, u32[]{:S(2)}, u32[]{:S(2)}) collective-permute-start(bf16[16,1152]{1,0:T(8,128)(2,1)S(1)} %get-tuple-element.69.refs_0_), channel_id=1, source_target_pairs={{0,3},{1,0},{2,1},{3,2},{4,7},{5,4},{6,5},{7,6},{8,11},{9,8},{10,9... | collective-permute-start | bytes 110600 | tf_op jit(solution)/shard_map/ppermute | solution.py:535
  67.6 6.0 %collective-permute-start.25 = (bf16[16,1152]{1,0:T(8,128)(2,1)S(1)}, bf16[16,1152]{1,0:T(8,128)(2,1)S(1)}, u32[]{:S(2)}, u32[]{:S(2)}) collective-permute-start(bf16[16,1152]{1,0:T(8,128)(2,1)S(1)} %get-tuple-element.69.refs_0_), channel_id=1, source_target_pairs={{0,2},{1,3},{2,0},{3,1},{4,6},{5,7},{6,4},{7,5},{8,10},{9,11},{10,... | collective-permute-start | bytes 110600 | tf_op jit(solution)/shard_map/ppermute | solution.py:535
  67.7 6.0 %collective-permute-start.24 = (bf16[16,1152]{1,0:T(8,128)(2,1)S(1)}, bf16[16,1152]{1,0:T(8,128)(2,1)S(1)}, u32[]{:S(2)}, u32[]{:S(2)}) collective-permute-start(bf16[16,1152]{1,0:T(8,128)(2,1)S(1)} %get-tuple-element.69.refs_0_), channel_id=1, source_target_pairs={{0,1},{1,2},{2,3},{3,0},{4,5},{5,6},{6,7},{7,4},{8,9},{9,10},{10,1... | collective-permute-start | bytes 110600 | tf_op jit(solution)/shard_map/ppermute | solution.py:535
  74.0 5.4 %collective-permute-start.29 = (bf16[32,1152]{1,0:T(8,128)(2,1)S(1)}, bf16[32,1152]{1,0:T(8,128)(2,1)S(1)}, u32[]{:S(2)}, u32[]{:S(2)}) collective-permute-start(bf16[32,1152]{1,0:T(8,128)(2,1)S(1)} %shard_map.112.refs_1_), channel_id=1, source_target_pairs={{0,24},{4,28},{8,16},{12,20},{16,8},{20,12},{24,0},{28,4},{1,25},{... | collective-permute-start | bytes 221192 | tf_op jit(solution)/shard_map/ppermute | solution.py:498
  74.8 5.1 %collective-permute-start.28 = (bf16[32,1152]{1,0:T(8,128)(2,1)S(1)}, bf16[32,1152]{1,0:T(8,128)(2,1)S(1)}, u32[]{:S(2)}, u32[]{:S(2)}) collective-permute-start(bf16[32,1152]{1,0:T(8,128)(2,1)S(1)} %shard_map.112.refs_1_), channel_id=1, source_target_pairs={{0,16},{4,20},{8,24},{12,28},{16,0},{20,4},{24,8},{28,12},{1,17},{... | collective-permute-start | bytes 221192 | tf_op jit(solution)/shard_map/ppermute | solution.py:498
  76.3 4.4 %collective-permute-start.27 = (bf16[32,1152]{1,0:T(8,128)(2,1)S(1)}, bf16[32,1152]{1,0:T(8,128)(2,1)S(1)}, u32[]{:S(2)}, u32[]{:S(2)}) collective-permute-start(bf16[32,1152]{1,0:T(8,128)(2,1)S(1)} %shard_map.112.refs_1_), channel_id=1, source_target_pairs={{0,8},{4,12},{8,0},{12,4},{16,24},{20,28},{24,16},{28,20},{1,9},{5... | collective-permute-start | bytes 221192 | tf_op jit(solution)/shard_map/ppermute | solution.py:498
  77.5 3.1 %collective-permute-start.30 = (bf16[32,1152]{1,0:T(8,128)(2,1)S(1)}, bf16[32,1152]{1,0:T(8,128)(2,1)S(1)}, u32[]{:S(2)}, u32[]{:S(2)}) collective-permute-start(bf16[32,1152]{1,0:T(8,128)(2,1)S(1)} %shard_map.112.refs_1_), channel_id=1, source_target_pairs={{0,4},{4,0},{8,12},{12,8},{16,20},{20,16},{24,28},{28,24},{1,5},{5... | collective-permute-start | bytes 221192 | tf_op jit(solution)/shard_map/ppermute | solution.py:505
  (13 other events, 68.6 us)

commit v6 on v5

--- a/solution.py
+++ b/solution.py
@@ -236,9 +236,9 @@
             total = total + joined(ref[rows:, :])
         extra[0][...] = parted(total[: LANES // 2 // parts_x])
     data = jnp.concatenate([ref[:rows, :] for ref in own], axis=0)
-    lines = dot(line_ref[...], data)
-    half = lines.shape[0] // 2
-    lines = lines[:half] + lines[half:]
+    half = line_ref.shape[0] // 2
+    table = jnp.concatenate([line_ref[:half, :], line_ref[half:, :]], axis=1)
+    lines = dot(table, jnp.concatenate([data, data], axis=0))
     count = half // 2
     both = jnp.concatenate([lines[:count], lines[count:]], axis=1)
     depth = both.shape[1]
@@ -284,44 +284,46 @@
     size_x, size_y, size_z, _, chans, _ = weight_ref.shape
     rows = size_x * size_z
     spectra = block_transpose(sum_parts(recv_ref, parts_y), chans // size_y)
-    for ky in range(size_y):
-        spec = spectra[ky]
+    for ky, spec in enumerate(spectra):
         spec_ref[ky] = spec
-        turned = pltpu.roll(spec, chans, 1)
-        if forward:
-            both = jnp.concatenate([spec, turned], axis=0)[:, :chans].T
+    if forward:
+        group = LANES // (2 * rows)
+        for start in range(0, size_y, group):
+            both = []
+            for spec in spectra[start : start + group]:
+                both += [spec, pltpu.roll(spec, chans, 1)]
+            both = jnp.concatenate(both, axis=0)[:, :chans].T
             high = both.astype(BF)
             both = jnp.concatenate([high, (both - high.astype(F32)).astype(BF)], axis=1)
-        else:
-            first = lax.broadcasted_iota(jnp.int32, spec.shape, 1) < chans
+            lane = lax.broadcasted_iota(jnp.int32, both.shape, 1) % LANES
+            mode = lane // (2 * rows) * rows + lane % rows
+            own = [jnp.where(mode == m, both, jnp.zeros_like(both)) for m in range(group * rows)]
+            wide = [
+                weight_ref[m // size_z, start + ky, m % size_z].reshape(2 * chans, chans)
+                for ky in range(group)
+                for m in range(rows)
+            ]
+            wide = [jnp.concatenate(wide[m : m + 2], axis=1) for m in range(0, len(wide), 2)]
+            total = dot(jnp.concatenate(wide, axis=1), jnp.concatenate(own, axis=0))
+            total = (total[:, :LANES] + total[:, LANES:]).T
+            for ky in range(group):
+                at = ky * 2 * rows
+                real, imag = total[at : at + rows], total[at + rows : at + 2 * rows]
+                at += start * 2 * rows
+                scratch[at : at + rows, :chans] = real[:, :chans] - imag[:, chans:]
+                scratch[at + rows : at + 2 * rows, :chans] = imag[:, :chans] + real[:, chans:]
+    else:
+        first = lax.broadcasted_iota(jnp.int32, spectra[0].shape, 1) < chans
+        for ky, spec in enumerate(spectra):
+            turned = pltpu.roll(spec, chans, 1)
             both = split_rows(jnp.concatenate([spec, jnp.where(first, turned, -turned)], axis=0))
-        if forward:
-            wide = [weight_ref[m // size_z, ky, m % size_z].reshape(2 * chans, chans) for m in range(rows)]
-            wide = [jnp.concatenate(wide[m : m + 2], axis=1) for m in range(0, rows, 2)]
-            mode = lax.broadcasted_iota(jnp.int32, both.shape, 1) % rows
-            own = [jnp.where(mode == m, both, jnp.zeros_like(both)) for m in range(rows)]
-            total = dot(jnp.concatenate(wide, axis=1), jnp.concatenate(own, axis=0))
-            total = total.T
-        else:
             stack = jnp.concatenate(
                 [weight_ref[kx, ky].reshape(size_z * 2 * chans, chans) for kx in range(size_x)], axis=0
             )
             mode = lax.broadcasted_iota(jnp.int32, both.shape, 0) % rows
             own = [jnp.where(mode == m, both, jnp.zeros_like(both)) for m in range(rows)]
             total = dot(jnp.concatenate(own, axis=1), stack)
-        total = total[: 2 * rows] + total[2 * rows :]
-        if forward:
-            real, imag = total[:rows], total[rows:]
-            mixed = jnp.concatenate(
-                [
-                    real[:, :chans] - imag[:, chans:],
-                    imag[:, :chans] + real[:, chans:],
-                ],
-                axis=0,
-            )
-        else:
-            mixed = total
-        scratch[ky * 2 * rows : (ky + 1) * 2 * rows, :chans] = mixed
+            scratch[ky * 2 * rows : (ky + 1) * 2 * rows, :chans] = total[: 2 * rows] + total[2 * rows :]
     lay_modes(scratch, send_ref, size_y, rows)
 
 

time: 83.5 us -> 82.5 us (0.988)
  Pallas kernels: 14.7 us -> 13.7 us
    pallas_call x10, Pallas kernels: 8.95 us -> 7.9 us  [call(): pl.pallas_call(kernel, out_shape=outs, scratch_shapes=list(scratch), comp...]
where the time goes in v6:
time: 82.5 us; the launch traced here: 82.2 us
  blocking collectives  23.8 us (29%)
  waiting for transfers between devices  22.1 us (27%)
  starting transfers between devices  20.6 us (25%)
  Pallas kernels  13.7 us (17%)
  local copies, waits for them, and re-layouts  1.19 us (1%)
    all_to_all x2, blocking collectives, to_modes(): return (lax.all_to_all(send, ('gx', 'gy'), 0, 0, tiled=True), rest, tables)  23.8 us
    ppermute x12, starting transfers between devices, cross(): lax.ppermute(piece, 'gx', [(i, i ^ 2 * t) for i in range(parts_x)])  15.2 us
    ppermute x12, waiting for transfers between devices, cross(): lax.ppermute(piece, 'gx', [(i, i ^ 2 * t) for i in range(parts_x)])  12.2 us
    pallas_call x10, Pallas kernels, call(): pl.pallas_call(kernel, out_shape=outs, scratch_shapes=list(scratch), comp...  7.9 us
    ppermute x6, waiting for transfers between devices, to_lines(): pieces.append(lax.ppermute(send, 'gy', ring))  5.18 us
    ppermute x6, starting transfers between devices, to_lines(): pieces.append(lax.ppermute(send, 'gy', ring))  4.9 us
    ppermute x16, waiting for transfers between devices, cross(): pieces = pieces + [lax.ppermute(piece, 'gx', swap) for piece in pieces]  4.66 us
    pallas_call x1, Pallas kernels, fast(): pl.pallas_call(outer_kernel, in_specs=[inside] * 2, out_specs=outside, ou...  3.91 us
  transfers between devices with their start and end apart: 34, of which 23 were waited for; matrix products, arithmetic and copies ran while one was open for 0% of the time, Pallas kernels for 7%

profile of v6, /device:TPU:0, one launch (start us, length us, event | category | flops | bytes accessed | tf_op | source)
XLA Modules:
  0.0 82.2 jit_solution(13690783131434665193)
XLA Ops:
  2.3 4.0 %collective-permute-start = (bf16[2,128,128]{2,1,0:T(8,128)(2,1)S(1)}, bf16[2,128,128]{2,1,0:T(8,128)(2,1)S(1)}, u32[]{:S(2)}, u32[]{:S(2)}) collective-permute-start(bf16[2,128,128]{2,1,0:T(8,128)(2,1)S(1)} %get-tuple-element.43), channel_id=1, source_target_pairs={{0,24},{4,28},{8,16},{12,20},{16,8},{20,12},{24,0},{28,4},{1,25},{... | collective-permute-start | bytes 196616 | tf_op jit(solution)/shard_map/ppermute | solution.py:500
  6.9 1.9 %shard_map.102 = (bf16[512,1024]{1,0:T(8,128)(2,1)S(1)}, bf16[512,512]{1,0:T(8,128)(2,1)S(1)}, bf16[64,64]{1,0:T(8,128)(2,1)S(1)}, bf16[256,256]{1,0:T(8,128)(2,...) custom-call(s32[32]{0:T(128)} %refs_0_.1, s32[32]{0:T(128)} %refs_1_.3, s32[4]{0:T(128)} %refs_2_.1, ...), custom_call_target="tpu_custom_call" | custom-call | tf_op jit(solution)/shard_map/pallas_call | solution.py:477
  8.7 1.7 %collective-permute-done.1.refs_3_ = bf16[2,128,128]{2,1,0:T(8,128)(2,1)S(1)} collective-permute-done((bf16[2,128,128]{2,1,0:T(8,128)(2,1)S(1)}, bf16[2,128,128]{2,1,0:T(8,128)(2,1)S(1)}, u32[]{:S(2)}, u32[]{:S(2)}) %collective-permute-start.1) | collective-permute-done | bytes 65568 | tf_op jit(solution)/shard_map/ppermute | solution.py:500
  13.1 13.1 %all_to_all.10.refs_0_ = bf16[32,16,128]{2,1,0:T(8,128)(2,1)S(1)} all-to-all(bf16[32,16,128]{2,1,0:T(8,128)(2,1)S(1)} %shard_map.104), channel_id=1, replica_groups=mesh['gx'=8,'gy'=4] {'gx','gy'}, dimensions={0} | all-to-all | bytes 262144 | tf_op jit(solution)/shard_map/all_to_all | solution.py:518
  26.2 1.3 %shard_map.105 = (bf16[16,1024]{1,0:T(8,128)(2,1)S(1)}, f32[8,16,128]{2,1,0:T(8,128)S(1)}) custom-call(bf16[32,16,128]{2,1,0:T(8,128)(2,1)S(1)} %all_to_all.10.refs_0_, bf16[4,8,4,2,64,64]{5,4,3,2,1,0:T(8,128)(2,1)S(1)} %copy-done), custom_call_target="tpu_custom_call" | custom-call | tf_op jit(solution)/shard_map/pallas_call | solution.py:443
  27.5 1.3 %collective-permute-start.9 = (bf16[16,1024]{1,0:T(8,128)(2,1)S(1)}, bf16[16,1024]{1,0:T(8,128)(2,1)S(1)}, u32[]{:S(2)}, u32[]{:S(2)}) collective-permute-start(bf16[16,1024]{1,0:T(8,128)(2,1)S(1)} %get-tuple-element.52.refs_0_), channel_id=1, source_target_pairs={{0,3},{1,0},{2,1},{3,2},{4,7},{5,4},{6,5},{7,6},{8,11},{9,8},{10,9... | collective-permute-start | bytes 98312 | tf_op jit(solution)/shard_map/ppermute | solution.py:537
  28.8 1.2 %collective-permute-start.7 = (bf16[16,1024]{1,0:T(8,128)(2,1)S(1)}, bf16[16,1024]{1,0:T(8,128)(2,1)S(1)}, u32[]{:S(2)}, u32[]{:S(2)}) collective-permute-start(bf16[16,1024]{1,0:T(8,128)(2,1)S(1)} %get-tuple-element.52.refs_0_), channel_id=1, source_target_pairs={{0,1},{1,2},{2,3},{3,0},{4,5},{5,6},{6,7},{7,4},{8,9},{9,10},{10,1... | collective-permute-start | bytes 98312 | tf_op jit(solution)/shard_map/ppermute | solution.py:537
  30.2 1.4 %collective-permute-done.9.refs_3_ = bf16[16,1024]{1,0:T(8,128)(2,1)S(1)} collective-permute-done((bf16[16,1024]{1,0:T(8,128)(2,1)S(1)}, bf16[16,1024]{1,0:T(8,128)(2,1)S(1)}, u32[]{:S(2)}, u32[]{:S(2)}) %collective-permute-start.9) | collective-permute-done | bytes 32800 | tf_op jit(solution)/shard_map/ppermute | solution.py:537
  31.6 3.0 %collective-permute-done.8.refs_2_ = bf16[16,1024]{1,0:T(8,128)(2,1)S(1)} collective-permute-done((bf16[16,1024]{1,0:T(8,128)(2,1)S(1)}, bf16[16,1024]{1,0:T(8,128)(2,1)S(1)}, u32[]{:S(2)}, u32[]{:S(2)}) %collective-permute-start.8) | collective-permute-done | bytes 32800 | tf_op jit(solution)/shard_map/ppermute | solution.py:537
  35.9 1.4 %collective-permute-start.11 = (bf16[32,1024]{1,0:T(8,128)(2,1)S(1)}, bf16[32,1024]{1,0:T(8,128)(2,1)S(1)}, u32[]{:S(2)}, u32[]{:S(2)}) collective-permute-start(bf16[32,1024]{1,0:T(8,128)(2,1)S(1)} %shard_map.107.refs_1_), channel_id=1, source_target_pairs={{0,16},{4,20},{8,24},{12,28},{16,0},{20,4},{24,8},{28,12},{1,17},{... | collective-permute-start | bytes 196616 | tf_op jit(solution)/shard_map/ppermute | solution.py:500
  37.3 1.2 %collective-permute-start.10 = (bf16[32,1024]{1,0:T(8,128)(2,1)S(1)}, bf16[32,1024]{1,0:T(8,128)(2,1)S(1)}, u32[]{:S(2)}, u32[]{:S(2)}) collective-permute-start(bf16[32,1024]{1,0:T(8,128)(2,1)S(1)} %shard_map.107.refs_1_), channel_id=1, source_target_pairs={{0,8},{4,12},{8,0},{12,4},{16,24},{20,28},{24,16},{28,20},{1,9},{5... | collective-permute-start | bytes 196616 | tf_op jit(solution)/shard_map/ppermute | solution.py:500
  38.5 1.7 %collective-permute-done.12.refs_4_ = bf16[32,1024]{1,0:T(8,128)(2,1)S(1)} collective-permute-done((bf16[32,1024]{1,0:T(8,128)(2,1)S(1)}, bf16[32,1024]{1,0:T(8,128)(2,1)S(1)}, u32[]{:S(2)}, u32[]{:S(2)}) %collective-permute-start.12) | collective-permute-done | bytes 65568 | tf_op jit(solution)/shard_map/ppermute | solution.py:500
  42.8 1.5 %shard_map.108 = (bf16[16,16,8,64]{3,2,1,0:T(8,128)(2,1)}, bf16[8,128,128]{2,1,0:T(8,128)(2,1)S(1)}, bf16[2,144,128]{2,1,0:T(8,128)(2,1)S(1)}, bf16[2,144,128]{2...) custom-call(bf16[256,256]{1,0:T(8,128)(2,1)S(1)} %get-tuple-element.41.refs_0_, ...), custom_call_target="tpu_custom_call" | custom-call | tf_op jit(solution)/shard_map/pallas_call | solution.py:443
  44.3 1.2 %collective-permute-start.17 = (bf16[2,144,128]{2,1,0:T(8,128)(2,1)S(1)}, bf16[2,144,128]{2,1,0:T(8,128)(2,1)S(1)}, u32[]{:S(2)}, u32[]{:S(2)}) collective-permute-start(bf16[2,144,128]{2,1,0:T(8,128)(2,1)S(1)} %get-tuple-element.64), channel_id=1, source_target_pairs={{0,8},{4,12},{8,0},{12,4},{16,24},{20,28},{24,16},{28,20},{1,9},{5... | collective-permute-start | bytes 221192 | tf_op jit(solution)/shard_map/ppermute | solution.py:500
  46.3 1.4 %collective-permute-start.19 = (bf16[2,144,128]{2,1,0:T(8,128)(2,1)S(1)}, bf16[2,144,128]{2,1,0:T(8,128)(2,1)S(1)}, u32[]{:S(2)}, u32[]{:S(2)}) collective-permute-start(bf16[2,144,128]{2,1,0:T(8,128)(2,1)S(1)} %get-tuple-element.66), channel_id=1, source_target_pairs={{0,24},{4,28},{8,16},{12,20},{16,8},{20,12},{24,0},{28,4},{1,25},{... | collective-permute-start | bytes 221192 | tf_op jit(solution)/shard_map/ppermute | solution.py:500
  48.7 2.0 %collective-permute-done.18.refs_4_ = bf16[2,144,128]{2,1,0:T(8,128)(2,1)S(1)} collective-permute-done((bf16[2,144,128]{2,1,0:T(8,128)(2,1)S(1)}, bf16[2,144,128]{2,1,0:T(8,128)(2,1)S(1)}, u32[]{:S(2)}, u32[]{:S(2)}) %collective-permute-start.18) | collective-permute-done | bytes 73760 | tf_op jit(solution)/shard_map/ppermute | solution.py:500
  53.5 10.7 %all_to_all.11.refs_0_ = bf16[32,16,128]{2,1,0:T(8,128)(2,1)S(1)} all-to-all(bf16[32,16,128]{2,1,0:T(8,128)(2,1)S(1)} %get-tuple-element.67), channel_id=1, replica_groups=mesh['gx'=8,'gy'=4] {'gx','gy'}, dimensions={0} | all-to-all | bytes 262144 | tf_op jit(solution)/shard_map/all_to_all | solution.py:518
  65.3 1.3 %collective-permute-start.26 = (bf16[16,1152]{1,0:T(8,128)(2,1)S(1)}, bf16[16,1152]{1,0:T(8,128)(2,1)S(1)}, u32[]{:S(2)}, u32[]{:S(2)}) collective-permute-start(bf16[16,1152]{1,0:T(8,128)(2,1)S(1)} %get-tuple-element.69.refs_0_), channel_id=1, source_target_pairs={{0,3},{1,0},{2,1},{3,2},{4,7},{5,4},{6,5},{7,6},{8,11},{9,8},{10,9... | collective-permute-start | bytes 110600 | tf_op jit(solution)/shard_map/ppermute | solution.py:537
  66.6 1.2 %collective-permute-start.24 = (bf16[16,1152]{1,0:T(8,128)(2,1)S(1)}, bf16[16,1152]{1,0:T(8,128)(2,1)S(1)}, u32[]{:S(2)}, u32[]{:S(2)}) collective-permute-start(bf16[16,1152]{1,0:T(8,128)(2,1)S(1)} %get-tuple-element.69.refs_0_), channel_id=1, source_target_pairs={{0,1},{1,2},{2,3},{3,0},{4,5},{5,6},{6,7},{7,4},{8,9},{9,10},{10,1... | collective-permute-start | bytes 110600 | tf_op jit(solution)/shard_map/ppermute | solution.py:537
  67.8 3.9 %shard_map.111 = f32[4,8,4,2,64,64]{5,4,3,2,1,0:T(8,128)} custom-call(f32[8,16,128]{2,1,0:T(8,128)S(1)} %get-tuple-element.70.spec_ref, f32[8,16,128]{2,1,0:T(8,128)S(1)} %get-tuple-element.71.back_ref), custom_call_target="tpu_custom_call" | custom-call | tf_op jit(solution)/shard_map/pallas_call | solution.py:577
  73.8 1.5 %collective-permute-start.28 = (bf16[32,1152]{1,0:T(8,128)(2,1)S(1)}, bf16[32,1152]{1,0:T(8,128)(2,1)S(1)}, u32[]{:S(2)}, u32[]{:S(2)}) collective-permute-start(bf16[32,1152]{1,0:T(8,128)(2,1)S(1)} %shard_map.112.refs_1_), channel_id=1, source_target_pairs={{0,16},{4,20},{8,24},{12,28},{16,0},{20,4},{24,8},{28,12},{1,17},{... | collective-permute-start | bytes 221192 | tf_op jit(solution)/shard_map/ppermute | solution.py:500
  75.3 1.2 %collective-permute-start.27 = (bf16[32,1152]{1,0:T(8,128)(2,1)S(1)}, bf16[32,1152]{1,0:T(8,128)(2,1)S(1)}, u32[]{:S(2)}, u32[]{:S(2)}) collective-permute-start(bf16[32,1152]{1,0:T(8,128)(2,1)S(1)} %shard_map.112.refs_1_), channel_id=1, source_target_pairs={{0,8},{4,12},{8,0},{12,4},{16,24},{20,28},{24,16},{28,20},{1,9},{5... | collective-permute-start | bytes 221192 | tf_op jit(solution)/shard_map/ppermute | solution.py:500
  76.5 1.9 %collective-permute-done.29.refs_4_ = bf16[32,1152]{1,0:T(8,128)(2,1)S(1)} collective-permute-done((bf16[32,1152]{1,0:T(8,128)(2,1)S(1)}, bf16[32,1152]{1,0:T(8,128)(2,1)S(1)}, u32[]{:S(2)}, u32[]{:S(2)}) %collective-permute-start.29) | collective-permute-done | bytes 73760 | tf_op jit(solution)/shard_map/ppermute | solution.py:500
  80.9 1.3 %shard_map.113 = (bf16[16,16,8,64]{3,2,1,0:T(8,128)(2,1)}, f32[64,64]{1,0:T(8,128)}) custom-call(bf16[256,256]{1,0:T(8,128)(2,1)S(1)} %get-tuple-element.41.refs_0_, bf16[32,1152]{1,0:T(8,128)(2,1)S(1)} %shard_map.112.refs_1_, bf16[32,1152]{1,0:T(8,128)(2,1)S(1)} %collective-permute-done.27.refs_2_, bf16[32,1152]{1,0:T(8,128)(2,1)S(1)} %collective-permute-done.28.refs_3_, ...), custom_call_target="tpu_custom_call" | custom-call | tf_op jit(solution)/shard_map/pallas_call | solution.py:443
  (64 shorter events, 19.2 us)
Async XLA Ops:
  2.3 6.5 %collective-permute-start = (bf16[2,128,128]{2,1,0:T(8,128)(2,1)S(1)}, bf16[2,128,128]{2,1,0:T(8,128)(2,1)S(1)}, u32[]{:S(2)}, u32[]{:S(2)}) collective-permute-start(bf16[2,128,128]{2,1,0:T(8,128)(2,1)S(1)} %get-tuple-element.43), channel_id=1, source_target_pairs={{0,24},{4,28},{8,16},{12,20},{16,8},{20,12},{24,0},{28,4},{1,25},{... | collective-permute-start | bytes 196616 | tf_op jit(solution)/shard_map/ppermute | solution.py:500
  6.2 4.3 %collective-permute-start.1 = (bf16[2,128,128]{2,1,0:T(8,128)(2,1)S(1)}, bf16[2,128,128]{2,1,0:T(8,128)(2,1)S(1)}, u32[]{:S(2)}, u32[]{:S(2)}) collective-permute-start(bf16[2,128,128]{2,1,0:T(8,128)(2,1)S(1)} %get-tuple-element.49), channel_id=1, source_target_pairs={{0,8},{4,12},{8,0},{12,4},{16,24},{20,28},{24,16},{28,20},{1,9},{5... | collective-permute-start | bytes 196616 | tf_op jit(solution)/shard_map/ppermute | solution.py:500
  6.8 4.3 %collective-permute-start.2 = (bf16[2,128,128]{2,1,0:T(8,128)(2,1)S(1)}, bf16[2,128,128]{2,1,0:T(8,128)(2,1)S(1)}, u32[]{:S(2)}, u32[]{:S(2)}) collective-permute-start(bf16[2,128,128]{2,1,0:T(8,128)(2,1)S(1)} %get-tuple-element.50), channel_id=1, source_target_pairs={{0,16},{4,20},{8,24},{12,28},{16,0},{20,4},{24,8},{28,12},{1,17},{... | collective-permute-start | bytes 196616 | tf_op jit(solution)/shard_map/ppermute | solution.py:500
  6.9 4.7 %collective-permute-start.3 = (bf16[2,128,128]{2,1,0:T(8,128)(2,1)S(1)}, bf16[2,128,128]{2,1,0:T(8,128)(2,1)S(1)}, u32[]{:S(2)}, u32[]{:S(2)}) collective-permute-start(bf16[2,128,128]{2,1,0:T(8,128)(2,1)S(1)} %get-tuple-element.48.refs_2_), channel_id=1, source_target_pairs={{0,4},{4,0},{8,12},{12,8},{16,20},{20,16},{24,28},{28,24},{1,5},{5... | collective-permute-start | bytes 196616 | tf_op jit(solution)/shard_map/ppermute | solution.py:507
  11.0 1.4 %collective-permute-start.6 = (bf16[2,128,128]{2,1,0:T(8,128)(2,1)S(1)}, bf16[2,128,128]{2,1,0:T(8,128)(2,1)S(1)}, u32[]{:S(2)}, u32[]{:S(2)}) collective-permute-start(bf16[2,128,128]{2,1,0:T(8,128)(2,1)S(1)} %collective-permute-done.refs_5_), channel_id=1, source_target_pairs={{0,4},{4,0},{8,12},{12,8},{16,20},{20,16},{24,28},{28,24},{1,5},{5... | collective-permute-start | bytes 196616 | tf_op jit(solution)/shard_map/ppermute | solution.py:507
  27.5 4.1 %collective-permute-start.9 = (bf16[16,1024]{1,0:T(8,128)(2,1)S(1)}, bf16[16,1024]{1,0:T(8,128)(2,1)S(1)}, u32[]{:S(2)}, u32[]{:S(2)}) collective-permute-start(bf16[16,1024]{1,0:T(8,128)(2,1)S(1)} %get-tuple-element.52.refs_0_), channel_id=1, source_target_pairs={{0,3},{1,0},{2,1},{3,2},{4,7},{5,4},{6,5},{7,6},{8,11},{9,8},{10,9... | collective-permute-start | bytes 98312 | tf_op jit(solution)/shard_map/ppermute | solution.py:537
  28.8 5.8 %collective-permute-start.8 = (bf16[16,1024]{1,0:T(8,128)(2,1)S(1)}, bf16[16,1024]{1,0:T(8,128)(2,1)S(1)}, u32[]{:S(2)}, u32[]{:S(2)}) collective-permute-start(bf16[16,1024]{1,0:T(8,128)(2,1)S(1)} %get-tuple-element.52.refs_0_), channel_id=1, source_target_pairs={{0,2},{1,3},{2,0},{3,1},{4,6},{5,7},{6,4},{7,5},{8,10},{9,11},{10,... | collective-permute-start | bytes 98312 | tf_op jit(solution)/shard_map/ppermute | solution.py:537
  28.8 5.8 %collective-permute-start.7 = (bf16[16,1024]{1,0:T(8,128)(2,1)S(1)}, bf16[16,1024]{1,0:T(8,128)(2,1)S(1)}, u32[]{:S(2)}, u32[]{:S(2)}) collective-permute-start(bf16[16,1024]{1,0:T(8,128)(2,1)S(1)} %get-tuple-element.52.refs_0_), channel_id=1, source_target_pairs={{0,1},{1,2},{2,3},{3,0},{4,5},{5,6},{6,7},{7,4},{8,9},{9,10},{10,1... | collective-permute-start | bytes 98312 | tf_op jit(solution)/shard_map/ppermute | solution.py:537
  34.9 5.3 %collective-permute-start.12 = (bf16[32,1024]{1,0:T(8,128)(2,1)S(1)}, bf16[32,1024]{1,0:T(8,128)(2,1)S(1)}, u32[]{:S(2)}, u32[]{:S(2)}) collective-permute-start(bf16[32,1024]{1,0:T(8,128)(2,1)S(1)} %shard_map.107.refs_1_), channel_id=1, source_target_pairs={{0,24},{4,28},{8,16},{12,20},{16,8},{20,12},{24,0},{28,4},{1,25},{... | collective-permute-start | bytes 196616 | tf_op jit(solution)/shard_map/ppermute | solution.py:500
  35.9 5.0 %collective-permute-start.11 = (bf16[32,1024]{1,0:T(8,128)(2,1)S(1)}, bf16[32,1024]{1,0:T(8,128)(2,1)S(1)}, u32[]{:S(2)}, u32[]{:S(2)}) collective-permute-start(bf16[32,1024]{1,0:T(8,128)(2,1)S(1)} %shard_map.107.refs_1_), channel_id=1, source_target_pairs={{0,16},{4,20},{8,24},{12,28},{16,0},{20,4},{24,8},{28,12},{1,17},{... | collective-permute-start | bytes 196616 | tf_op jit(solution)/shard_map/ppermute | solution.py:500
  37.3 4.3 %collective-permute-start.10 = (bf16[32,1024]{1,0:T(8,128)(2,1)S(1)}, bf16[32,1024]{1,0:T(8,128)(2,1)S(1)}, u32[]{:S(2)}, u32[]{:S(2)}) collective-permute-start(bf16[32,1024]{1,0:T(8,128)(2,1)S(1)} %shard_map.107.refs_1_), channel_id=1, source_target_pairs={{0,8},{4,12},{8,0},{12,4},{16,24},{20,28},{24,16},{28,20},{1,9},{5... | collective-permute-start | bytes 196616 | tf_op jit(solution)/shard_map/ppermute | solution.py:500
  38.5 3.1 %collective-permute-start.13 = (bf16[32,1024]{1,0:T(8,128)(2,1)S(1)}, bf16[32,1024]{1,0:T(8,128)(2,1)S(1)}, u32[]{:S(2)}, u32[]{:S(2)}) collective-permute-start(bf16[32,1024]{1,0:T(8,128)(2,1)S(1)} %shard_map.107.refs_1_), channel_id=1, source_target_pairs={{0,4},{4,0},{8,12},{12,8},{16,20},{20,16},{24,28},{28,24},{1,5},{5... | collective-permute-start | bytes 196616 | tf_op jit(solution)/shard_map/ppermute | solution.py:507
  44.3 4.4 %collective-permute-start.17 = (bf16[2,144,128]{2,1,0:T(8,128)(2,1)S(1)}, bf16[2,144,128]{2,1,0:T(8,128)(2,1)S(1)}, u32[]{:S(2)}, u32[]{:S(2)}) collective-permute-start(bf16[2,144,128]{2,1,0:T(8,128)(2,1)S(1)} %get-tuple-element.64), channel_id=1, source_target_pairs={{0,8},{4,12},{8,0},{12,4},{16,24},{20,28},{24,16},{28,20},{1,9},{5... | collective-permute-start | bytes 221192 | tf_op jit(solution)/shard_map/ppermute | solution.py:500
  45.5 5.1 %collective-permute-start.18 = (bf16[2,144,128]{2,1,0:T(8,128)(2,1)S(1)}, bf16[2,144,128]{2,1,0:T(8,128)(2,1)S(1)}, u32[]{:S(2)}, u32[]{:S(2)}) collective-permute-start(bf16[2,144,128]{2,1,0:T(8,128)(2,1)S(1)} %get-tuple-element.65), channel_id=1, source_target_pairs={{0,16},{4,20},{8,24},{12,28},{16,0},{20,4},{24,8},{28,12},{1,17},{... | collective-permute-start | bytes 221192 | tf_op jit(solution)/shard_map/ppermute | solution.py:500
  46.3 5.3 %collective-permute-start.19 = (bf16[2,144,128]{2,1,0:T(8,128)(2,1)S(1)}, bf16[2,144,128]{2,1,0:T(8,128)(2,1)S(1)}, u32[]{:S(2)}, u32[]{:S(2)}) collective-permute-start(bf16[2,144,128]{2,1,0:T(8,128)(2,1)S(1)} %get-tuple-element.66), channel_id=1, source_target_pairs={{0,24},{4,28},{8,16},{12,20},{16,8},{20,12},{24,0},{28,4},{1,25},{... | collective-permute-start | bytes 221192 | tf_op jit(solution)/shard_map/ppermute | solution.py:500
  47.8 3.8 %collective-permute-start.20 = (bf16[2,144,128]{2,1,0:T(8,128)(2,1)S(1)}, bf16[2,144,128]{2,1,0:T(8,128)(2,1)S(1)}, u32[]{:S(2)}, u32[]{:S(2)}) collective-permute-start(bf16[2,144,128]{2,1,0:T(8,128)(2,1)S(1)} %get-tuple-element.63.refs_2_), channel_id=1, source_target_pairs={{0,4},{4,0},{8,12},{12,8},{16,20},{20,16},{24,28},{28,24},{1,5},{5... | collective-permute-start | bytes 221192 | tf_op jit(solution)/shard_map/ppermute | solution.py:507
  48.7 2.9 %collective-permute-start.21 = (bf16[2,144,128]{2,1,0:T(8,128)(2,1)S(1)}, bf16[2,144,128]{2,1,0:T(8,128)(2,1)S(1)}, u32[]{:S(2)}, u32[]{:S(2)}) collective-permute-start(bf16[2,144,128]{2,1,0:T(8,128)(2,1)S(1)} %collective-permute-done.17.refs_3_), channel_id=1, source_target_pairs={{0,4},{4,0},{8,12},{12,8},{16,20},{20,16},{24,28},{28,24},{1,5},{5... | collective-permute-start | bytes 221192 | tf_op jit(solution)/shard_map/ppermute | solution.py:507
  65.3 6.4 %collective-permute-start.26 = (bf16[16,1152]{1,0:T(8,128)(2,1)S(1)}, bf16[16,1152]{1,0:T(8,128)(2,1)S(1)}, u32[]{:S(2)}, u32[]{:S(2)}) collective-permute-start(bf16[16,1152]{1,0:T(8,128)(2,1)S(1)} %get-tuple-element.69.refs_0_), channel_id=1, source_target_pairs={{0,3},{1,0},{2,1},{3,2},{4,7},{5,4},{6,5},{7,6},{8,11},{9,8},{10,9... | collective-permute-start | bytes 110600 | tf_op jit(solution)/shard_map/ppermute | solution.py:537
  66.6 6.0 %collective-permute-start.25 = (bf16[16,1152]{1,0:T(8,128)(2,1)S(1)}, bf16[16,1152]{1,0:T(8,128)(2,1)S(1)}, u32[]{:S(2)}, u32[]{:S(2)}) collective-permute-start(bf16[16,1152]{1,0:T(8,128)(2,1)S(1)} %get-tuple-element.69.refs_0_), channel_id=1, source_target_pairs={{0,2},{1,3},{2,0},{3,1},{4,6},{5,7},{6,4},{7,5},{8,10},{9,11},{10,... | collective-permute-start | bytes 110600 | tf_op jit(solution)/shard_map/ppermute | solution.py:537
  66.6 6.0 %collective-permute-start.24 = (bf16[16,1152]{1,0:T(8,128)(2,1)S(1)}, bf16[16,1152]{1,0:T(8,128)(2,1)S(1)}, u32[]{:S(2)}, u32[]{:S(2)}) collective-permute-start(bf16[16,1152]{1,0:T(8,128)(2,1)S(1)} %get-tuple-element.69.refs_0_), channel_id=1, source_target_pairs={{0,1},{1,2},{2,3},{3,0},{4,5},{5,6},{6,7},{7,4},{8,9},{9,10},{10,1... | collective-permute-start | bytes 110600 | tf_op jit(solution)/shard_map/ppermute | solution.py:537
  72.9 5.4 %collective-permute-start.29 = (bf16[32,1152]{1,0:T(8,128)(2,1)S(1)}, bf16[32,1152]{1,0:T(8,128)(2,1)S(1)}, u32[]{:S(2)}, u32[]{:S(2)}) collective-permute-start(bf16[32,1152]{1,0:T(8,128)(2,1)S(1)} %shard_map.112.refs_1_), channel_id=1, source_target_pairs={{0,24},{4,28},{8,16},{12,20},{16,8},{20,12},{24,0},{28,4},{1,25},{... | collective-permute-start | bytes 221192 | tf_op jit(solution)/shard_map/ppermute | solution.py:500
  73.8 5.1 %collective-permute-start.28 = (bf16[32,1152]{1,0:T(8,128)(2,1)S(1)}, bf16[32,1152]{1,0:T(8,128)(2,1)S(1)}, u32[]{:S(2)}, u32[]{:S(2)}) collective-permute-start(bf16[32,1152]{1,0:T(8,128)(2,1)S(1)} %shard_map.112.refs_1_), channel_id=1, source_target_pairs={{0,16},{4,20},{8,24},{12,28},{16,0},{20,4},{24,8},{28,12},{1,17},{... | collective-permute-start | bytes 221192 | tf_op jit(solution)/shard_map/ppermute | solution.py:500
  75.3 4.4 %collective-permute-start.27 = (bf16[32,1152]{1,0:T(8,128)(2,1)S(1)}, bf16[32,1152]{1,0:T(8,128)(2,1)S(1)}, u32[]{:S(2)}, u32[]{:S(2)}) collective-permute-start(bf16[32,1152]{1,0:T(8,128)(2,1)S(1)} %shard_map.112.refs_1_), channel_id=1, source_target_pairs={{0,8},{4,12},{8,0},{12,4},{16,24},{20,28},{24,16},{28,20},{1,9},{5... | collective-permute-start | bytes 221192 | tf_op jit(solution)/shard_map/ppermute | solution.py:500
  76.5 3.1 %collective-permute-start.30 = (bf16[32,1152]{1,0:T(8,128)(2,1)S(1)}, bf16[32,1152]{1,0:T(8,128)(2,1)S(1)}, u32[]{:S(2)}, u32[]{:S(2)}) collective-permute-start(bf16[32,1152]{1,0:T(8,128)(2,1)S(1)} %shard_map.112.refs_1_), channel_id=1, source_target_pairs={{0,4},{4,0},{8,12},{12,8},{16,20},{20,16},{24,28},{28,24},{1,5},{5... | collective-permute-start | bytes 221192 | tf_op jit(solution)/shard_map/ppermute | solution.py:507
  (13 other events, 67.6 us)

commit v7 on v6

--- a/solution.py
+++ b/solution.py
@@ -383,7 +383,7 @@
         field = field_ref[p]
         pre = cells[:, p * LANES : (p + 1) * LANES] + conv_ref[p]
         cdf = normal_cdf(pre)
-        store_pair(act_ref, p, pre * cdf)
+        act_ref[p] = (pre * cdf).astype(BF)
         slope = cot_ref[p].astype(F32) * (cdf + pre * normal_pdf(pre))
         narrow = slope.astype(BF)
         slope_ref[p] = narrow
@@ -397,6 +397,11 @@
         chunk_ref[b, :rows, :] = chunk.astype(BF)
         chunk_ref[b, rows:, :] = parted(grad[b * block : (b + 1) * block])
     store_steps(chunk_ref, send_refs)
+
+
+def unpair_kernel(pairs_ref, out_ref):
+    for p in range(pairs_ref.shape[0]):
+        store_pair(out_ref, p, pairs_ref[p].astype(F32))
 
 
 def last_kernel(scale, table_ref, *refs):
@@ -512,9 +517,9 @@
         if extra:
             outs.append(sds((EXTRA, LANES), BF))
         kernel = bind(transform_kernel, factor, parts_x, parts_y)
-        pieces, ready = cross(send, None if extra else tables)
-        tables = tables if ready is None else ready
-        send, *rest = call(kernel, outs, *tables, *pieces)
+        pieces, ready = cross(send, tables)
+        tables = ready
+        send, *rest = call(kernel, outs, *tables[:2], *pieces)
         return lax.all_to_all(send, ("gx", "gy"), 0, 0, tiled=True), rest, tables
 
     def mix(recv, forward, rest):
@@ -561,8 +566,8 @@
     activation, slope, *send = call(
         bind(point_kernel, second),
         (
-            sds(features.shape, BF),
-            sds((half_y, cells, LANES), BF),
+            sds(pair_shape, BF),
+            sds(pair_shape, BF),
         )
         + (sds((2, cells + EXTRA, LANES), BF),) * SIDES,
         line_back,
@@ -572,7 +577,8 @@
         cot,
         scratch=[pltpu.VMEM((parts_x, cells + EXTRA, LANES), BF)],
     )
-    recv, rest, _ = to_modes(send, second, True, tables)
+    activation = call(unpair_kernel, sds(features.shape, BF), activation)
+    recv, rest, (_, _, activation) = to_modes(send, second, True, (*tables, activation))
     send, back = mix(recv, False, rest)
     grad_spectral = pl.pallas_call(
         outer_kernel,

time: 82.5 us -> 81.9 us (level)
  waiting for transfers between devices: 22.1 us -> 20.2 us
    ppermute x12, waiting for transfers between devices: 12.2 us -> 10.7 us  [cross(): lax.ppermute(piece, 'gx', [(i, i ^ 2 * t) for i in range(parts_x)])]
    pallas_call x10 -> x11, Pallas kernels: 7.9 us -> 8.29 us  [call(): pl.pallas_call(kernel, out_shape=outs, scratch_shapes=list(scratch), comp...]
  transfers between devices with their start and end apart: 34 -> 34, of which waited for: 23 -> 23; matrix products, arithmetic and copies ran while one was open for 0% -> 0% of each run, Pallas kernels for 7% -> 9%
where the time goes in v7:
time: 81.9 us; the launch traced here: 81.6 us
  blocking collectives  24.1 us (29%)
  starting transfers between devices  21.2 us (26%)
  waiting for transfers between devices  20.2 us (25%)
  Pallas kernels  14.1 us (17%)
  local copies, waits for them, and re-layouts  1.19 us (1%)
    all_to_all x2, blocking collectives, to_modes(): return (lax.all_to_all(send, ('gx', 'gy'), 0, 0, tiled=True), rest, tables)  24.1 us
    ppermute x12, starting transfers between devices, cross(): lax.ppermute(piece, 'gx', [(i, i ^ 2 * t) for i in range(parts_x)])  15.3 us
    ppermute x12, waiting for transfers between devices, cross(): lax.ppermute(piece, 'gx', [(i, i ^ 2 * t) for i in range(parts_x)])  10.7 us
    pallas_call x11, Pallas kernels, call(): pl.pallas_call(kernel, out_shape=outs, scratch_shapes=list(scratch), comp...  8.29 us
    ppermute x6, waiting for transfers between devices, to_lines(): pieces.append(lax.ppermute(send, 'gy', ring))  5.17 us
    ppermute x6, starting transfers between devices, to_lines(): pieces.append(lax.ppermute(send, 'gy', ring))  4.9 us
    ppermute x16, waiting for transfers between devices, cross(): pieces = pieces + [lax.ppermute(piece, 'gx', swap) for piece in pieces]  4.32 us
    pallas_call x1, Pallas kernels, fast(): pl.pallas_call(outer_kernel, in_specs=[inside] * 2, out_specs=outside, ou...  3.92 us
  transfers between devices with their start and end apart: 34, of which 23 were waited for; matrix products, arithmetic and copies ran while one was open for 0% of the time, Pallas kernels for 9%

profile of v7, /device:TPU:0, one launch (start us, length us, event | category | flops | bytes accessed | tf_op | source)
XLA Modules:
  0.0 81.6 jit_solution(10636159345016915839)
XLA Ops:
  0.7 1.2 %copy-done.1 = bf16[16,16,8,64]{3,2,1,0:T(8,128)(2,1)S(1)} copy-done((bf16[16,16,8,64]{3,2,1,0:T(8,128)(2,1)S(1)}, bf16[16,16,8,64]{3,2,1,0:T(8,128)(2,1)}, u32[]{:S(2)}) %copy-start.1) | copy-done | bytes 262168
  2.3 4.0 %collective-permute-start = (bf16[2,128,128]{2,1,0:T(8,128)(2,1)S(1)}, bf16[2,128,128]{2,1,0:T(8,128)(2,1)S(1)}, u32[]{:S(2)}, u32[]{:S(2)}) collective-permute-start(bf16[2,128,128]{2,1,0:T(8,128)(2,1)S(1)} %get-tuple-element.47), channel_id=1, source_target_pairs={{0,24},{4,28},{8,16},{12,20},{16,8},{20,12},{24,0},{28,4},{1,25},{... | collective-permute-start | bytes 196616 | tf_op jit(solution)/shard_map/ppermute | solution.py:505
  6.9 1.9 %shard_map.102 = (bf16[512,1024]{1,0:T(8,128)(2,1)S(1)}, bf16[512,512]{1,0:T(8,128)(2,1)S(1)}, bf16[64,64]{1,0:T(8,128)(2,1)S(1)}, bf16[256,256]{1,0:T(8,128)(2,...) custom-call(s32[32]{0:T(128)} %refs_0_.1, s32[32]{0:T(128)} %refs_1_.3, s32[4]{0:T(128)} %refs_2_.1, ...), custom_call_target="tpu_custom_call" | custom-call | tf_op jit(solution)/shard_map/pallas_call | solution.py:482
  8.8 1.7 %collective-permute-done.1.refs_3_ = bf16[2,128,128]{2,1,0:T(8,128)(2,1)S(1)} collective-permute-done((bf16[2,128,128]{2,1,0:T(8,128)(2,1)S(1)}, bf16[2,128,128]{2,1,0:T(8,128)(2,1)S(1)}, u32[]{:S(2)}, u32[]{:S(2)}) %collective-permute-start.1) | collective-permute-done | bytes 65568 | tf_op jit(solution)/shard_map/ppermute | solution.py:505
  13.1 13.1 %all_to_all.10.refs_0_ = bf16[32,16,128]{2,1,0:T(8,128)(2,1)S(1)} all-to-all(bf16[32,16,128]{2,1,0:T(8,128)(2,1)S(1)} %shard_map.104), channel_id=1, replica_groups=mesh['gx'=8,'gy'=4] {'gx','gy'}, dimensions={0} | all-to-all | bytes 262144 | tf_op jit(solution)/shard_map/all_to_all | solution.py:523
  26.2 1.3 %shard_map.105 = (bf16[16,1024]{1,0:T(8,128)(2,1)S(1)}, f32[8,16,128]{2,1,0:T(8,128)S(1)}) custom-call(bf16[32,16,128]{2,1,0:T(8,128)(2,1)S(1)} %all_to_all.10.refs_0_, bf16[4,8,4,2,64,64]{5,4,3,2,1,0:T(8,128)(2,1)S(1)} %copy-done), custom_call_target="tpu_custom_call" | custom-call | tf_op jit(solution)/shard_map/pallas_call | solution.py:448
  27.5 1.3 %collective-permute-start.9 = (bf16[16,1024]{1,0:T(8,128)(2,1)S(1)}, bf16[16,1024]{1,0:T(8,128)(2,1)S(1)}, u32[]{:S(2)}, u32[]{:S(2)}) collective-permute-start(bf16[16,1024]{1,0:T(8,128)(2,1)S(1)} %get-tuple-element.56.refs_0_), channel_id=1, source_target_pairs={{0,3},{1,0},{2,1},{3,2},{4,7},{5,4},{6,5},{7,6},{8,11},{9,8},{10,9... | collective-permute-start | bytes 98312 | tf_op jit(solution)/shard_map/ppermute | solution.py:542
  28.8 1.2 %collective-permute-start.7 = (bf16[16,1024]{1,0:T(8,128)(2,1)S(1)}, bf16[16,1024]{1,0:T(8,128)(2,1)S(1)}, u32[]{:S(2)}, u32[]{:S(2)}) collective-permute-start(bf16[16,1024]{1,0:T(8,128)(2,1)S(1)} %get-tuple-element.56.refs_0_), channel_id=1, source_target_pairs={{0,1},{1,2},{2,3},{3,0},{4,5},{5,6},{6,7},{7,4},{8,9},{9,10},{10,1... | collective-permute-start | bytes 98312 | tf_op jit(solution)/shard_map/ppermute | solution.py:542
  30.2 1.4 %collective-permute-done.9.refs_3_ = bf16[16,1024]{1,0:T(8,128)(2,1)S(1)} collective-permute-done((bf16[16,1024]{1,0:T(8,128)(2,1)S(1)}, bf16[16,1024]{1,0:T(8,128)(2,1)S(1)}, u32[]{:S(2)}, u32[]{:S(2)}) %collective-permute-start.9) | collective-permute-done | bytes 32800 | tf_op jit(solution)/shard_map/ppermute | solution.py:542
  31.6 2.9 %collective-permute-done.8.refs_2_ = bf16[16,1024]{1,0:T(8,128)(2,1)S(1)} collective-permute-done((bf16[16,1024]{1,0:T(8,128)(2,1)S(1)}, bf16[16,1024]{1,0:T(8,128)(2,1)S(1)}, u32[]{:S(2)}, u32[]{:S(2)}) %collective-permute-start.8) | collective-permute-done | bytes 32800 | tf_op jit(solution)/shard_map/ppermute | solution.py:542
  35.9 1.4 %collective-permute-start.11 = (bf16[32,1024]{1,0:T(8,128)(2,1)S(1)}, bf16[32,1024]{1,0:T(8,128)(2,1)S(1)}, u32[]{:S(2)}, u32[]{:S(2)}) collective-permute-start(bf16[32,1024]{1,0:T(8,128)(2,1)S(1)} %shard_map.107.refs_1_), channel_id=1, source_target_pairs={{0,16},{4,20},{8,24},{12,28},{16,0},{20,4},{24,8},{28,12},{1,17},{... | collective-permute-start | bytes 196616 | tf_op jit(solution)/shard_map/ppermute | solution.py:505
  37.3 1.2 %collective-permute-start.10 = (bf16[32,1024]{1,0:T(8,128)(2,1)S(1)}, bf16[32,1024]{1,0:T(8,128)(2,1)S(1)}, u32[]{:S(2)}, u32[]{:S(2)}) collective-permute-start(bf16[32,1024]{1,0:T(8,128)(2,1)S(1)} %shard_map.107.refs_1_), channel_id=1, source_target_pairs={{0,8},{4,12},{8,0},{12,4},{16,24},{20,28},{24,16},{28,20},{1,9},{5... | collective-permute-start | bytes 196616 | tf_op jit(solution)/shard_map/ppermute | solution.py:505
  38.5 1.7 %collective-permute-done.12.refs_4_ = bf16[32,1024]{1,0:T(8,128)(2,1)S(1)} collective-permute-done((bf16[32,1024]{1,0:T(8,128)(2,1)S(1)}, bf16[32,1024]{1,0:T(8,128)(2,1)S(1)}, u32[]{:S(2)}, u32[]{:S(2)}) %collective-permute-start.12) | collective-permute-done | bytes 65568 | tf_op jit(solution)/shard_map/ppermute | solution.py:505
  43.7 1.5 %collective-permute-start.17 = (bf16[2,144,128]{2,1,0:T(8,128)(2,1)S(1)}, bf16[2,144,128]{2,1,0:T(8,128)(2,1)S(1)}, u32[]{:S(2)}, u32[]{:S(2)}) collective-permute-start(bf16[2,144,128]{2,1,0:T(8,128)(2,1)S(1)} %get-tuple-element.66), channel_id=1, source_target_pairs={{0,24},{4,28},{8,16},{12,20},{16,8},{20,12},{24,0},{28,4},{1,25},{... | collective-permute-start | bytes 221192 | tf_op jit(solution)/shard_map/ppermute | solution.py:505
  45.9 1.4 %collective-permute-start.19 = (bf16[2,144,128]{2,1,0:T(8,128)(2,1)S(1)}, bf16[2,144,128]{2,1,0:T(8,128)(2,1)S(1)}, u32[]{:S(2)}, u32[]{:S(2)}) collective-permute-start(bf16[2,144,128]{2,1,0:T(8,128)(2,1)S(1)} %get-tuple-element.73), channel_id=1, source_target_pairs={{0,16},{4,20},{8,24},{12,28},{16,0},{20,4},{24,8},{28,12},{1,17},{... | collective-permute-start | bytes 221192 | tf_op jit(solution)/shard_map/ppermute | solution.py:505
  48.3 1.4 %collective-permute-done.17.refs_5_ = bf16[2,144,128]{2,1,0:T(8,128)(2,1)S(1)} collective-permute-done((bf16[2,144,128]{2,1,0:T(8,128)(2,1)S(1)}, bf16[2,144,128]{2,1,0:T(8,128)(2,1)S(1)}, u32[]{:S(2)}, u32[]{:S(2)}) %collective-permute-start.17) | collective-permute-done | bytes 73760 | tf_op jit(solution)/shard_map/ppermute | solution.py:505
  52.6 11.0 %all_to_all.11.refs_0_ = bf16[32,16,128]{2,1,0:T(8,128)(2,1)S(1)} all-to-all(bf16[32,16,128]{2,1,0:T(8,128)(2,1)S(1)} %get-tuple-element.75), channel_id=1, replica_groups=mesh['gx'=8,'gy'=4] {'gx','gy'}, dimensions={0} | all-to-all | bytes 262144 | tf_op jit(solution)/shard_map/all_to_all | solution.py:523
  64.7 1.3 %collective-permute-start.26 = (bf16[16,1152]{1,0:T(8,128)(2,1)S(1)}, bf16[16,1152]{1,0:T(8,128)(2,1)S(1)}, u32[]{:S(2)}, u32[]{:S(2)}) collective-permute-start(bf16[16,1152]{1,0:T(8,128)(2,1)S(1)} %get-tuple-element.77.refs_0_), channel_id=1, source_target_pairs={{0,3},{1,0},{2,1},{3,2},{4,7},{5,4},{6,5},{7,6},{8,11},{9,8},{10,9... | collective-permute-start | bytes 110600 | tf_op jit(solution)/shard_map/ppermute | solution.py:542
  66.0 1.2 %collective-permute-start.24 = (bf16[16,1152]{1,0:T(8,128)(2,1)S(1)}, bf16[16,1152]{1,0:T(8,128)(2,1)S(1)}, u32[]{:S(2)}, u32[]{:S(2)}) collective-permute-start(bf16[16,1152]{1,0:T(8,128)(2,1)S(1)} %get-tuple-element.77.refs_0_), channel_id=1, source_target_pairs={{0,1},{1,2},{2,3},{3,0},{4,5},{5,6},{6,7},{7,4},{8,9},{9,10},{10,1... | collective-permute-start | bytes 110600 | tf_op jit(solution)/shard_map/ppermute | solution.py:542
  67.2 3.9 %shard_map.112 = f32[4,8,4,2,64,64]{5,4,3,2,1,0:T(8,128)} custom-call(f32[8,16,128]{2,1,0:T(8,128)S(1)} %get-tuple-element.78.spec_ref, f32[8,16,128]{2,1,0:T(8,128)S(1)} %get-tuple-element.79.back_ref), custom_call_target="tpu_custom_call" | custom-call | tf_op jit(solution)/shard_map/pallas_call | solution.py:583
  73.2 1.5 %collective-permute-start.28 = (bf16[32,1152]{1,0:T(8,128)(2,1)S(1)}, bf16[32,1152]{1,0:T(8,128)(2,1)S(1)}, u32[]{:S(2)}, u32[]{:S(2)}) collective-permute-start(bf16[32,1152]{1,0:T(8,128)(2,1)S(1)} %shard_map.113.refs_1_), channel_id=1, source_target_pairs={{0,16},{4,20},{8,24},{12,28},{16,0},{20,4},{24,8},{28,12},{1,17},{... | collective-permute-start | bytes 221192 | tf_op jit(solution)/shard_map/ppermute | solution.py:505
  74.7 1.2 %collective-permute-start.27 = (bf16[32,1152]{1,0:T(8,128)(2,1)S(1)}, bf16[32,1152]{1,0:T(8,128)(2,1)S(1)}, u32[]{:S(2)}, u32[]{:S(2)}) collective-permute-start(bf16[32,1152]{1,0:T(8,128)(2,1)S(1)} %shard_map.113.refs_1_), channel_id=1, source_target_pairs={{0,8},{4,12},{8,0},{12,4},{16,24},{20,28},{24,16},{28,20},{1,9},{5... | collective-permute-start | bytes 221192 | tf_op jit(solution)/shard_map/ppermute | solution.py:505
  75.9 1.9 %collective-permute-done.29.refs_4_ = bf16[32,1152]{1,0:T(8,128)(2,1)S(1)} collective-permute-done((bf16[32,1152]{1,0:T(8,128)(2,1)S(1)}, bf16[32,1152]{1,0:T(8,128)(2,1)S(1)}, u32[]{:S(2)}, u32[]{:S(2)}) %collective-permute-start.29) | collective-permute-done | bytes 73760 | tf_op jit(solution)/shard_map/ppermute | solution.py:505
  80.3 1.3 %shard_map.114 = (bf16[16,16,8,64]{3,2,1,0:T(8,128)(2,1)}, f32[64,64]{1,0:T(8,128)}) custom-call(bf16[256,256]{1,0:T(8,128)(2,1)S(1)} %get-tuple-element.45.refs_0_, bf16[32,1152]{1,0:T(8,128)(2,1)S(1)} %shard_map.113.refs_1_, bf16[32,1152]{1,0:T(8,128)(2,1)S(1)} %collective-permute-done.27.refs_2_, bf16[32,1152]{1,0:T(8,128)(2,1)S(1)} %collective-permute-done.28.refs_3_, ...), custom_call_target="tpu_custom_call" | custom-call | tf_op jit(solution)/shard_map/pallas_call | solution.py:448
  (65 shorter events, 19.0 us)
Async XLA Ops:
  2.3 6.5 %collective-permute-start = (bf16[2,128,128]{2,1,0:T(8,128)(2,1)S(1)}, bf16[2,128,128]{2,1,0:T(8,128)(2,1)S(1)}, u32[]{:S(2)}, u32[]{:S(2)}) collective-permute-start(bf16[2,128,128]{2,1,0:T(8,128)(2,1)S(1)} %get-tuple-element.47), channel_id=1, source_target_pairs={{0,24},{4,28},{8,16},{12,20},{16,8},{20,12},{24,0},{28,4},{1,25},{... | collective-permute-start | bytes 196616 | tf_op jit(solution)/shard_map/ppermute | solution.py:505
  6.2 4.3 %collective-permute-start.1 = (bf16[2,128,128]{2,1,0:T(8,128)(2,1)S(1)}, bf16[2,128,128]{2,1,0:T(8,128)(2,1)S(1)}, u32[]{:S(2)}, u32[]{:S(2)}) collective-permute-start(bf16[2,128,128]{2,1,0:T(8,128)(2,1)S(1)} %get-tuple-element.53), channel_id=1, source_target_pairs={{0,8},{4,12},{8,0},{12,4},{16,24},{20,28},{24,16},{28,20},{1,9},{5... | collective-permute-start | bytes 196616 | tf_op jit(solution)/shard_map/ppermute | solution.py:505
  6.8 4.3 %collective-permute-start.2 = (bf16[2,128,128]{2,1,0:T(8,128)(2,1)S(1)}, bf16[2,128,128]{2,1,0:T(8,128)(2,1)S(1)}, u32[]{:S(2)}, u32[]{:S(2)}) collective-permute-start(bf16[2,128,128]{2,1,0:T(8,128)(2,1)S(1)} %get-tuple-element.54), channel_id=1, source_target_pairs={{0,16},{4,20},{8,24},{12,28},{16,0},{20,4},{24,8},{28,12},{1,17},{... | collective-permute-start | bytes 196616 | tf_op jit(solution)/shard_map/ppermute | solution.py:505
  6.9 4.7 %collective-permute-start.3 = (bf16[2,128,128]{2,1,0:T(8,128)(2,1)S(1)}, bf16[2,128,128]{2,1,0:T(8,128)(2,1)S(1)}, u32[]{:S(2)}, u32[]{:S(2)}) collective-permute-start(bf16[2,128,128]{2,1,0:T(8,128)(2,1)S(1)} %get-tuple-element.52.refs_2_), channel_id=1, source_target_pairs={{0,4},{4,0},{8,12},{12,8},{16,20},{20,16},{24,28},{28,24},{1,5},{5... | collective-permute-start | bytes 196616 | tf_op jit(solution)/shard_map/ppermute | solution.py:512
  11.0 1.4 %collective-permute-start.6 = (bf16[2,128,128]{2,1,0:T(8,128)(2,1)S(1)}, bf16[2,128,128]{2,1,0:T(8,128)(2,1)S(1)}, u32[]{:S(2)}, u32[]{:S(2)}) collective-permute-start(bf16[2,128,128]{2,1,0:T(8,128)(2,1)S(1)} %collective-permute-done.refs_5_), channel_id=1, source_target_pairs={{0,4},{4,0},{8,12},{12,8},{16,20},{20,16},{24,28},{28,24},{1,5},{5... | collective-permute-start | bytes 196616 | tf_op jit(solution)/shard_map/ppermute | solution.py:512
  27.5 4.1 %collective-permute-start.9 = (bf16[16,1024]{1,0:T(8,128)(2,1)S(1)}, bf16[16,1024]{1,0:T(8,128)(2,1)S(1)}, u32[]{:S(2)}, u32[]{:S(2)}) collective-permute-start(bf16[16,1024]{1,0:T(8,128)(2,1)S(1)} %get-tuple-element.56.refs_0_), channel_id=1, source_target_pairs={{0,3},{1,0},{2,1},{3,2},{4,7},{5,4},{6,5},{7,6},{8,11},{9,8},{10,9... | collective-permute-start | bytes 98312 | tf_op jit(solution)/shard_map/ppermute | solution.py:542
  28.8 5.8 %collective-permute-start.8 = (bf16[16,1024]{1,0:T(8,128)(2,1)S(1)}, bf16[16,1024]{1,0:T(8,128)(2,1)S(1)}, u32[]{:S(2)}, u32[]{:S(2)}) collective-permute-start(bf16[16,1024]{1,0:T(8,128)(2,1)S(1)} %get-tuple-element.56.refs_0_), channel_id=1, source_target_pairs={{0,2},{1,3},{2,0},{3,1},{4,6},{5,7},{6,4},{7,5},{8,10},{9,11},{10,... | collective-permute-start | bytes 98312 | tf_op jit(solution)/shard_map/ppermute | solution.py:542
  28.8 5.8 %collective-permute-start.7 = (bf16[16,1024]{1,0:T(8,128)(2,1)S(1)}, bf16[16,1024]{1,0:T(8,128)(2,1)S(1)}, u32[]{:S(2)}, u32[]{:S(2)}) collective-permute-start(bf16[16,1024]{1,0:T(8,128)(2,1)S(1)} %get-tuple-element.56.refs_0_), channel_id=1, source_target_pairs={{0,1},{1,2},{2,3},{3,0},{4,5},{5,6},{6,7},{7,4},{8,9},{9,10},{10,1... | collective-permute-start | bytes 98312 | tf_op jit(solution)/shard_map/ppermute | solution.py:542
  34.9 5.3 %collective-permute-start.12 = (bf16[32,1024]{1,0:T(8,128)(2,1)S(1)}, bf16[32,1024]{1,0:T(8,128)(2,1)S(1)}, u32[]{:S(2)}, u32[]{:S(2)}) collective-permute-start(bf16[32,1024]{1,0:T(8,128)(2,1)S(1)} %shard_map.107.refs_1_), channel_id=1, source_target_pairs={{0,24},{4,28},{8,16},{12,20},{16,8},{20,12},{24,0},{28,4},{1,25},{... | collective-permute-start | bytes 196616 | tf_op jit(solution)/shard_map/ppermute | solution.py:505
  35.9 5.0 %collective-permute-start.11 = (bf16[32,1024]{1,0:T(8,128)(2,1)S(1)}, bf16[32,1024]{1,0:T(8,128)(2,1)S(1)}, u32[]{:S(2)}, u32[]{:S(2)}) collective-permute-start(bf16[32,1024]{1,0:T(8,128)(2,1)S(1)} %shard_map.107.refs_1_), channel_id=1, source_target_pairs={{0,16},{4,20},{8,24},{12,28},{16,0},{20,4},{24,8},{28,12},{1,17},{... | collective-permute-start | bytes 196616 | tf_op jit(solution)/shard_map/ppermute | solution.py:505
  37.3 4.3 %collective-permute-start.10 = (bf16[32,1024]{1,0:T(8,128)(2,1)S(1)}, bf16[32,1024]{1,0:T(8,128)(2,1)S(1)}, u32[]{:S(2)}, u32[]{:S(2)}) collective-permute-start(bf16[32,1024]{1,0:T(8,128)(2,1)S(1)} %shard_map.107.refs_1_), channel_id=1, source_target_pairs={{0,8},{4,12},{8,0},{12,4},{16,24},{20,28},{24,16},{28,20},{1,9},{5... | collective-permute-start | bytes 196616 | tf_op jit(solution)/shard_map/ppermute | solution.py:505
  38.5 3.1 %collective-permute-start.13 = (bf16[32,1024]{1,0:T(8,128)(2,1)S(1)}, bf16[32,1024]{1,0:T(8,128)(2,1)S(1)}, u32[]{:S(2)}, u32[]{:S(2)}) collective-permute-start(bf16[32,1024]{1,0:T(8,128)(2,1)S(1)} %shard_map.107.refs_1_), channel_id=1, source_target_pairs={{0,4},{4,0},{8,12},{12,8},{16,20},{20,16},{24,28},{28,24},{1,5},{5... | collective-permute-start | bytes 196616 | tf_op jit(solution)/shard_map/ppermute | solution.py:512
  43.7 6.0 %collective-permute-start.17 = (bf16[2,144,128]{2,1,0:T(8,128)(2,1)S(1)}, bf16[2,144,128]{2,1,0:T(8,128)(2,1)S(1)}, u32[]{:S(2)}, u32[]{:S(2)}) collective-permute-start(bf16[2,144,128]{2,1,0:T(8,128)(2,1)S(1)} %get-tuple-element.66), channel_id=1, source_target_pairs={{0,24},{4,28},{8,16},{12,20},{16,8},{20,12},{24,0},{28,4},{1,25},{... | collective-permute-start | bytes 221192 | tf_op jit(solution)/shard_map/ppermute | solution.py:505
  45.2 4.6 %collective-permute-start.18 = (bf16[2,144,128]{2,1,0:T(8,128)(2,1)S(1)}, bf16[2,144,128]{2,1,0:T(8,128)(2,1)S(1)}, u32[]{:S(2)}, u32[]{:S(2)}) collective-permute-start(bf16[2,144,128]{2,1,0:T(8,128)(2,1)S(1)} %get-tuple-element.72), channel_id=1, source_target_pairs={{0,8},{4,12},{8,0},{12,4},{16,24},{20,28},{24,16},{28,20},{1,9},{5... | collective-permute-start | bytes 221192 | tf_op jit(solution)/shard_map/ppermute | solution.py:505
  45.9 4.7 %collective-permute-start.19 = (bf16[2,144,128]{2,1,0:T(8,128)(2,1)S(1)}, bf16[2,144,128]{2,1,0:T(8,128)(2,1)S(1)}, u32[]{:S(2)}, u32[]{:S(2)}) collective-permute-start(bf16[2,144,128]{2,1,0:T(8,128)(2,1)S(1)} %get-tuple-element.73), channel_id=1, source_target_pairs={{0,16},{4,20},{8,24},{12,28},{16,0},{20,4},{24,8},{28,12},{1,17},{... | collective-permute-start | bytes 221192 | tf_op jit(solution)/shard_map/ppermute | solution.py:505
  47.2 3.8 %collective-permute-start.20 = (bf16[2,144,128]{2,1,0:T(8,128)(2,1)S(1)}, bf16[2,144,128]{2,1,0:T(8,128)(2,1)S(1)}, u32[]{:S(2)}, u32[]{:S(2)}) collective-permute-start(bf16[2,144,128]{2,1,0:T(8,128)(2,1)S(1)} %get-tuple-element.71.refs_2_), channel_id=1, source_target_pairs={{0,4},{4,0},{8,12},{12,8},{16,20},{20,16},{24,28},{28,24},{1,5},{5... | collective-permute-start | bytes 221192 | tf_op jit(solution)/shard_map/ppermute | solution.py:512
  50.6 1.4 %collective-permute-start.23 = (bf16[2,144,128]{2,1,0:T(8,128)(2,1)S(1)}, bf16[2,144,128]{2,1,0:T(8,128)(2,1)S(1)}, u32[]{:S(2)}, u32[]{:S(2)}) collective-permute-start(bf16[2,144,128]{2,1,0:T(8,128)(2,1)S(1)} %collective-permute-done.17.refs_5_), channel_id=1, source_target_pairs={{0,4},{4,0},{8,12},{12,8},{16,20},{20,16},{24,28},{28,24},{1,5},{5... | collective-permute-start | bytes 221192 | tf_op jit(solution)/shard_map/ppermute | solution.py:512
  64.7 6.4 %collective-permute-start.26 = (bf16[16,1152]{1,0:T(8,128)(2,1)S(1)}, bf16[16,1152]{1,0:T(8,128)(2,1)S(1)}, u32[]{:S(2)}, u32[]{:S(2)}) collective-permute-start(bf16[16,1152]{1,0:T(8,128)(2,1)S(1)} %get-tuple-element.77.refs_0_), channel_id=1, source_target_pairs={{0,3},{1,0},{2,1},{3,2},{4,7},{5,4},{6,5},{7,6},{8,11},{9,8},{10,9... | collective-permute-start | bytes 110600 | tf_op jit(solution)/shard_map/ppermute | solution.py:542
  66.0 6.0 %collective-permute-start.25 = (bf16[16,1152]{1,0:T(8,128)(2,1)S(1)}, bf16[16,1152]{1,0:T(8,128)(2,1)S(1)}, u32[]{:S(2)}, u32[]{:S(2)}) collective-permute-start(bf16[16,1152]{1,0:T(8,128)(2,1)S(1)} %get-tuple-element.77.refs_0_), channel_id=1, source_target_pairs={{0,2},{1,3},{2,0},{3,1},{4,6},{5,7},{6,4},{7,5},{8,10},{9,11},{10,... | collective-permute-start | bytes 110600 | tf_op jit(solution)/shard_map/ppermute | solution.py:542
  66.0 6.0 %collective-permute-start.24 = (bf16[16,1152]{1,0:T(8,128)(2,1)S(1)}, bf16[16,1152]{1,0:T(8,128)(2,1)S(1)}, u32[]{:S(2)}, u32[]{:S(2)}) collective-permute-start(bf16[16,1152]{1,0:T(8,128)(2,1)S(1)} %get-tuple-element.77.refs_0_), channel_id=1, source_target_pairs={{0,1},{1,2},{2,3},{3,0},{4,5},{5,6},{6,7},{7,4},{8,9},{9,10},{10,1... | collective-permute-start | bytes 110600 | tf_op jit(solution)/shard_map/ppermute | solution.py:542
  72.3 5.4 %collective-permute-start.29 = (bf16[32,1152]{1,0:T(8,128)(2,1)S(1)}, bf16[32,1152]{1,0:T(8,128)(2,1)S(1)}, u32[]{:S(2)}, u32[]{:S(2)}) collective-permute-start(bf16[32,1152]{1,0:T(8,128)(2,1)S(1)} %shard_map.113.refs_1_), channel_id=1, source_target_pairs={{0,24},{4,28},{8,16},{12,20},{16,8},{20,12},{24,0},{28,4},{1,25},{... | collective-permute-start | bytes 221192 | tf_op jit(solution)/shard_map/ppermute | solution.py:505
  73.2 5.1 %collective-permute-start.28 = (bf16[32,1152]{1,0:T(8,128)(2,1)S(1)}, bf16[32,1152]{1,0:T(8,128)(2,1)S(1)}, u32[]{:S(2)}, u32[]{:S(2)}) collective-permute-start(bf16[32,1152]{1,0:T(8,128)(2,1)S(1)} %shard_map.113.refs_1_), channel_id=1, source_target_pairs={{0,16},{4,20},{8,24},{12,28},{16,0},{20,4},{24,8},{28,12},{1,17},{... | collective-permute-start | bytes 221192 | tf_op jit(solution)/shard_map/ppermute | solution.py:505
  74.7 4.4 %collective-permute-start.27 = (bf16[32,1152]{1,0:T(8,128)(2,1)S(1)}, bf16[32,1152]{1,0:T(8,128)(2,1)S(1)}, u32[]{:S(2)}, u32[]{:S(2)}) collective-permute-start(bf16[32,1152]{1,0:T(8,128)(2,1)S(1)} %shard_map.113.refs_1_), channel_id=1, source_target_pairs={{0,8},{4,12},{8,0},{12,4},{16,24},{20,28},{24,16},{28,20},{1,9},{5... | collective-permute-start | bytes 221192 | tf_op jit(solution)/shard_map/ppermute | solution.py:505
  75.9 3.1 %collective-permute-start.30 = (bf16[32,1152]{1,0:T(8,128)(2,1)S(1)}, bf16[32,1152]{1,0:T(8,128)(2,1)S(1)}, u32[]{:S(2)}, u32[]{:S(2)}) collective-permute-start(bf16[32,1152]{1,0:T(8,128)(2,1)S(1)} %shard_map.113.refs_1_), channel_id=1, source_target_pairs={{0,4},{4,0},{8,12},{12,8},{16,20},{20,16},{24,28},{28,24},{1,5},{5... | collective-permute-start | bytes 221192 | tf_op jit(solution)/shard_map/ppermute | solution.py:512
  (13 other events, 67.6 us)

commit v8 on v7

--- a/solution.py
+++ b/solution.py
@@ -399,14 +399,15 @@
     store_steps(chunk_ref, send_refs)
 
 
-def unpair_kernel(pairs_ref, out_ref):
+def unpair_kernel(pairs_ref, slope_ref, conv_ref, out_ref, turned_ref):
     for p in range(pairs_ref.shape[0]):
+        turned_ref[p] = dot(slope_ref[p], conv_ref[...])
         store_pair(out_ref, p, pairs_ref[p].astype(F32))
 
 
 def last_kernel(scale, table_ref, *refs):
-    conv_ref, slope_ref, out_ref, grad_ref = refs[-4:]
-    recv_refs = refs[:-4]
+    slope_ref, out_ref, grad_ref = refs[-3:]
+    recv_refs = refs[:-3]
     block = grad_ref.shape[0] // len(recv_refs)
     me = lax.axis_index("gx")
     for step, ref in zip(steps_of(len(recv_refs)), recv_refs):
@@ -414,7 +415,7 @@
         grad_ref[pl.ds(pl.multiple_of((me ^ step) * block, block), block), :] = total[:block] * scale
     cells = cells_of(table_ref, recv_refs, scale)
     for p in range(slope_ref.shape[0]):
-        store_pair(out_ref, p, cells[:, p * LANES : (p + 1) * LANES] + dot(slope_ref[p], conv_ref[...]))
+        store_pair(out_ref, p, cells[:, p * LANES : (p + 1) * LANES] + slope_ref[p])
 
 
 def outer_kernel(spec_ref, back_ref, out_ref, held_ref, sems):
@@ -577,8 +578,10 @@
         cot,
         scratch=[pltpu.VMEM((parts_x, cells + EXTRA, LANES), BF)],
     )
-    activation = call(unpair_kernel, sds(features.shape, BF), activation)
-    recv, rest, (_, _, activation) = to_modes(send, second, True, (*tables, activation))
+    laid = call(
+        unpair_kernel, (sds(features.shape, BF), sds(pair_shape, F32)), activation, slope, conv_turn
+    )
+    recv, rest, (_, _, (activation, turned)) = to_modes(send, second, True, (*tables, tuple(laid)))
     send, back = mix(recv, False, rest)
     grad_spectral = pl.pallas_call(
         outer_kernel,
@@ -594,8 +597,7 @@
         (sds(features.shape, BF), sds((chans, chans), F32)),
         line_back,
         *pieces,
-        conv_turn,
-        slope,
+        turned,
     )
     return activation, grad_features, grad_spectral, grad_conv
 

time: 81.9 us -> 81.8 us (level)
  no operation moved by 1% of the time
where the time goes in v8:
time: 81.8 us; the launch traced here: 81.5 us
  blocking collectives  24.1 us (29%)
  starting transfers between devices  21.2 us (26%)
  waiting for transfers between devices  20.2 us (25%)
  Pallas kernels  14 us (17%)
  local copies, waits for them, and re-layouts  1.19 us (1%)
    all_to_all x2, blocking collectives, to_modes(): return (lax.all_to_all(send, ('gx', 'gy'), 0, 0, tiled=True), rest, tables)  24.1 us
    ppermute x12, starting transfers between devices, cross(): lax.ppermute(piece, 'gx', [(i, i ^ 2 * t) for i in range(parts_x)])  15.3 us
    ppermute x12, waiting for transfers between devices, cross(): lax.ppermute(piece, 'gx', [(i, i ^ 2 * t) for i in range(parts_x)])  10.7 us
    pallas_call x11, Pallas kernels, call(): pl.pallas_call(kernel, out_shape=outs, scratch_shapes=list(scratch), comp...  8.21 us
    ppermute x6, waiting for transfers between devices, to_lines(): pieces.append(lax.ppermute(send, 'gy', ring))  5.17 us
    ppermute x6, starting transfers between devices, to_lines(): pieces.append(lax.ppermute(send, 'gy', ring))  4.9 us
    ppermute x16, waiting for transfers between devices, cross(): pieces = pieces + [lax.ppermute(piece, 'gx', swap) for piece in pieces]  4.32 us
    pallas_call x1, Pallas kernels, fast(): pl.pallas_call(outer_kernel, in_specs=[inside] * 2, out_specs=outside, ou...  3.91 us
  transfers between devices with their start and end apart: 34, of which 23 were waited for; matrix products, arithmetic and copies ran while one was open for 0% of the time, Pallas kernels for 9%

profile of v8, /device:TPU:0, one launch (start us, length us, event | category | flops | bytes accessed | tf_op | source)
XLA Modules:
  0.0 81.5 jit_solution(6396566243190132899)
XLA Ops:
  0.7 1.2 %copy-done.1 = bf16[16,16,8,64]{3,2,1,0:T(8,128)(2,1)S(1)} copy-done((bf16[16,16,8,64]{3,2,1,0:T(8,128)(2,1)S(1)}, bf16[16,16,8,64]{3,2,1,0:T(8,128)(2,1)}, u32[]{:S(2)}) %copy-start.1) | copy-done | bytes 262168
  2.3 4.0 %collective-permute-start = (bf16[2,128,128]{2,1,0:T(8,128)(2,1)S(1)}, bf16[2,128,128]{2,1,0:T(8,128)(2,1)S(1)}, u32[]{:S(2)}, u32[]{:S(2)}) collective-permute-start(bf16[2,128,128]{2,1,0:T(8,128)(2,1)S(1)} %get-tuple-element.50), channel_id=1, source_target_pairs={{0,24},{4,28},{8,16},{12,20},{16,8},{20,12},{24,0},{28,4},{1,25},{... | collective-permute-start | bytes 196616 | tf_op jit(solution)/shard_map/ppermute | solution.py:506
  6.9 1.9 %shard_map.102 = (bf16[512,1024]{1,0:T(8,128)(2,1)S(1)}, bf16[512,512]{1,0:T(8,128)(2,1)S(1)}, bf16[64,64]{1,0:T(8,128)(2,1)S(1)}, bf16[256,256]{1,0:T(8,128)(2,...) custom-call(s32[32]{0:T(128)} %refs_0_.1, s32[32]{0:T(128)} %refs_1_.3, s32[4]{0:T(128)} %refs_2_.1, ...), custom_call_target="tpu_custom_call" | custom-call | tf_op jit(solution)/shard_map/pallas_call | solution.py:483
  8.8 1.7 %collective-permute-done.1.refs_3_ = bf16[2,128,128]{2,1,0:T(8,128)(2,1)S(1)} collective-permute-done((bf16[2,128,128]{2,1,0:T(8,128)(2,1)S(1)}, bf16[2,128,128]{2,1,0:T(8,128)(2,1)S(1)}, u32[]{:S(2)}, u32[]{:S(2)}) %collective-permute-start.1) | collective-permute-done | bytes 65568 | tf_op jit(solution)/shard_map/ppermute | solution.py:506
  13.1 13.1 %all_to_all.10.refs_0_ = bf16[32,16,128]{2,1,0:T(8,128)(2,1)S(1)} all-to-all(bf16[32,16,128]{2,1,0:T(8,128)(2,1)S(1)} %shard_map.104), channel_id=1, replica_groups=mesh['gx'=8,'gy'=4] {'gx','gy'}, dimensions={0} | all-to-all | bytes 262144 | tf_op jit(solution)/shard_map/all_to_all | solution.py:524
  26.2 1.3 %shard_map.105 = (bf16[16,1024]{1,0:T(8,128)(2,1)S(1)}, f32[8,16,128]{2,1,0:T(8,128)S(1)}) custom-call(bf16[32,16,128]{2,1,0:T(8,128)(2,1)S(1)} %all_to_all.10.refs_0_, bf16[4,8,4,2,64,64]{5,4,3,2,1,0:T(8,128)(2,1)S(1)} %copy-done), custom_call_target="tpu_custom_call" | custom-call | tf_op jit(solution)/shard_map/pallas_call | solution.py:449
  27.5 1.3 %collective-permute-start.9 = (bf16[16,1024]{1,0:T(8,128)(2,1)S(1)}, bf16[16,1024]{1,0:T(8,128)(2,1)S(1)}, u32[]{:S(2)}, u32[]{:S(2)}) collective-permute-start(bf16[16,1024]{1,0:T(8,128)(2,1)S(1)} %get-tuple-element.59.refs_0_), channel_id=1, source_target_pairs={{0,3},{1,0},{2,1},{3,2},{4,7},{5,4},{6,5},{7,6},{8,11},{9,8},{10,9... | collective-permute-start | bytes 98312 | tf_op jit(solution)/shard_map/ppermute | solution.py:543
  28.8 1.2 %collective-permute-start.7 = (bf16[16,1024]{1,0:T(8,128)(2,1)S(1)}, bf16[16,1024]{1,0:T(8,128)(2,1)S(1)}, u32[]{:S(2)}, u32[]{:S(2)}) collective-permute-start(bf16[16,1024]{1,0:T(8,128)(2,1)S(1)} %get-tuple-element.59.refs_0_), channel_id=1, source_target_pairs={{0,1},{1,2},{2,3},{3,0},{4,5},{5,6},{6,7},{7,4},{8,9},{9,10},{10,1... | collective-permute-start | bytes 98312 | tf_op jit(solution)/shard_map/ppermute | solution.py:543
  30.2 1.4 %collective-permute-done.9.refs_3_ = bf16[16,1024]{1,0:T(8,128)(2,1)S(1)} collective-permute-done((bf16[16,1024]{1,0:T(8,128)(2,1)S(1)}, bf16[16,1024]{1,0:T(8,128)(2,1)S(1)}, u32[]{:S(2)}, u32[]{:S(2)}) %collective-permute-start.9) | collective-permute-done | bytes 32800 | tf_op jit(solution)/shard_map/ppermute | solution.py:543
  31.6 2.9 %collective-permute-done.8.refs_2_ = bf16[16,1024]{1,0:T(8,128)(2,1)S(1)} collective-permute-done((bf16[16,1024]{1,0:T(8,128)(2,1)S(1)}, bf16[16,1024]{1,0:T(8,128)(2,1)S(1)}, u32[]{:S(2)}, u32[]{:S(2)}) %collective-permute-start.8) | collective-permute-done | bytes 32800 | tf_op jit(solution)/shard_map/ppermute | solution.py:543
  35.9 1.4 %collective-permute-start.11 = (bf16[32,1024]{1,0:T(8,128)(2,1)S(1)}, bf16[32,1024]{1,0:T(8,128)(2,1)S(1)}, u32[]{:S(2)}, u32[]{:S(2)}) collective-permute-start(bf16[32,1024]{1,0:T(8,128)(2,1)S(1)} %shard_map.107.refs_1_), channel_id=1, source_target_pairs={{0,16},{4,20},{8,24},{12,28},{16,0},{20,4},{24,8},{28,12},{1,17},{... | collective-permute-start | bytes 196616 | tf_op jit(solution)/shard_map/ppermute | solution.py:506
  37.3 1.2 %collective-permute-start.10 = (bf16[32,1024]{1,0:T(8,128)(2,1)S(1)}, bf16[32,1024]{1,0:T(8,128)(2,1)S(1)}, u32[]{:S(2)}, u32[]{:S(2)}) collective-permute-start(bf16[32,1024]{1,0:T(8,128)(2,1)S(1)} %shard_map.107.refs_1_), channel_id=1, source_target_pairs={{0,8},{4,12},{8,0},{12,4},{16,24},{20,28},{24,16},{28,20},{1,9},{5... | collective-permute-start | bytes 196616 | tf_op jit(solution)/shard_map/ppermute | solution.py:506
  38.5 1.7 %collective-permute-done.12.refs_4_ = bf16[32,1024]{1,0:T(8,128)(2,1)S(1)} collective-permute-done((bf16[32,1024]{1,0:T(8,128)(2,1)S(1)}, bf16[32,1024]{1,0:T(8,128)(2,1)S(1)}, u32[]{:S(2)}, u32[]{:S(2)}) %collective-permute-start.12) | collective-permute-done | bytes 65568 | tf_op jit(solution)/shard_map/ppermute | solution.py:506
  43.7 1.5 %collective-permute-start.17 = (bf16[2,144,128]{2,1,0:T(8,128)(2,1)S(1)}, bf16[2,144,128]{2,1,0:T(8,128)(2,1)S(1)}, u32[]{:S(2)}, u32[]{:S(2)}) collective-permute-start(bf16[2,144,128]{2,1,0:T(8,128)(2,1)S(1)} %get-tuple-element.69), channel_id=1, source_target_pairs={{0,24},{4,28},{8,16},{12,20},{16,8},{20,12},{24,0},{28,4},{1,25},{... | collective-permute-start | bytes 221192 | tf_op jit(solution)/shard_map/ppermute | solution.py:506
  45.9 1.4 %collective-permute-start.19 = (bf16[2,144,128]{2,1,0:T(8,128)(2,1)S(1)}, bf16[2,144,128]{2,1,0:T(8,128)(2,1)S(1)}, u32[]{:S(2)}, u32[]{:S(2)}) collective-permute-start(bf16[2,144,128]{2,1,0:T(8,128)(2,1)S(1)} %get-tuple-element.80), channel_id=1, source_target_pairs={{0,16},{4,20},{8,24},{12,28},{16,0},{20,4},{24,8},{28,12},{1,17},{... | collective-permute-start | bytes 221192 | tf_op jit(solution)/shard_map/ppermute | solution.py:506
  48.3 1.4 %collective-permute-done.17.refs_5_ = bf16[2,144,128]{2,1,0:T(8,128)(2,1)S(1)} collective-permute-done((bf16[2,144,128]{2,1,0:T(8,128)(2,1)S(1)}, bf16[2,144,128]{2,1,0:T(8,128)(2,1)S(1)}, u32[]{:S(2)}, u32[]{:S(2)}) %collective-permute-start.17) | collective-permute-done | bytes 73760 | tf_op jit(solution)/shard_map/ppermute | solution.py:506
  52.6 11.0 %all_to_all.11.refs_0_ = bf16[32,16,128]{2,1,0:T(8,128)(2,1)S(1)} all-to-all(bf16[32,16,128]{2,1,0:T(8,128)(2,1)S(1)} %get-tuple-element.82), channel_id=1, replica_groups=mesh['gx'=8,'gy'=4] {'gx','gy'}, dimensions={0} | all-to-all | bytes 262144 | tf_op jit(solution)/shard_map/all_to_all | solution.py:524
  64.7 1.3 %collective-permute-start.26 = (bf16[16,1152]{1,0:T(8,128)(2,1)S(1)}, bf16[16,1152]{1,0:T(8,128)(2,1)S(1)}, u32[]{:S(2)}, u32[]{:S(2)}) collective-permute-start(bf16[16,1152]{1,0:T(8,128)(2,1)S(1)} %get-tuple-element.84.refs_0_), channel_id=1, source_target_pairs={{0,3},{1,0},{2,1},{3,2},{4,7},{5,4},{6,5},{7,6},{8,11},{9,8},{10,9... | collective-permute-start | bytes 110600 | tf_op jit(solution)/shard_map/ppermute | solution.py:543
  66.0 1.2 %collective-permute-start.24 = (bf16[16,1152]{1,0:T(8,128)(2,1)S(1)}, bf16[16,1152]{1,0:T(8,128)(2,1)S(1)}, u32[]{:S(2)}, u32[]{:S(2)}) collective-permute-start(bf16[16,1152]{1,0:T(8,128)(2,1)S(1)} %get-tuple-element.84.refs_0_), channel_id=1, source_target_pairs={{0,1},{1,2},{2,3},{3,0},{4,5},{5,6},{6,7},{7,4},{8,9},{9,10},{10,1... | collective-permute-start | bytes 110600 | tf_op jit(solution)/shard_map/ppermute | solution.py:543
  67.2 3.9 %shard_map.112 = f32[4,8,4,2,64,64]{5,4,3,2,1,0:T(8,128)} custom-call(f32[8,16,128]{2,1,0:T(8,128)S(1)} %get-tuple-element.85.spec_ref, f32[8,16,128]{2,1,0:T(8,128)S(1)} %get-tuple-element.86.back_ref), custom_call_target="tpu_custom_call" | custom-call | tf_op jit(solution)/shard_map/pallas_call | solution.py:586
  73.2 1.5 %collective-permute-start.28 = (bf16[32,1152]{1,0:T(8,128)(2,1)S(1)}, bf16[32,1152]{1,0:T(8,128)(2,1)S(1)}, u32[]{:S(2)}, u32[]{:S(2)}) collective-permute-start(bf16[32,1152]{1,0:T(8,128)(2,1)S(1)} %shard_map.113.refs_1_), channel_id=1, source_target_pairs={{0,16},{4,20},{8,24},{12,28},{16,0},{20,4},{24,8},{28,12},{1,17},{... | collective-permute-start | bytes 221192 | tf_op jit(solution)/shard_map/ppermute | solution.py:506
  74.7 1.2 %collective-permute-start.27 = (bf16[32,1152]{1,0:T(8,128)(2,1)S(1)}, bf16[32,1152]{1,0:T(8,128)(2,1)S(1)}, u32[]{:S(2)}, u32[]{:S(2)}) collective-permute-start(bf16[32,1152]{1,0:T(8,128)(2,1)S(1)} %shard_map.113.refs_1_), channel_id=1, source_target_pairs={{0,8},{4,12},{8,0},{12,4},{16,24},{20,28},{24,16},{28,20},{1,9},{5... | collective-permute-start | bytes 221192 | tf_op jit(solution)/shard_map/ppermute | solution.py:506
  75.9 1.9 %collective-permute-done.29.refs_4_ = bf16[32,1152]{1,0:T(8,128)(2,1)S(1)} collective-permute-done((bf16[32,1152]{1,0:T(8,128)(2,1)S(1)}, bf16[32,1152]{1,0:T(8,128)(2,1)S(1)}, u32[]{:S(2)}, u32[]{:S(2)}) %collective-permute-start.29) | collective-permute-done | bytes 73760 | tf_op jit(solution)/shard_map/ppermute | solution.py:506
  80.3 1.2 %shard_map.114 = (bf16[16,16,8,64]{3,2,1,0:T(8,128)(2,1)}, f32[64,64]{1,0:T(8,128)}) custom-call(bf16[256,256]{1,0:T(8,128)(2,1)S(1)} %get-tuple-element.48.refs_0_, bf16[32,1152]{1,0:T(8,128)(2,1)S(1)} %shard_map.113.refs_1_, bf16[32,1152]{1,0:T(8,128)(2,1)S(1)} %collective-permute-done.27.refs_2_, bf16[32,1152]{1,0:T(8,128)(2,1)S(1)} %collective-permute-done.28.refs_3_, ...), custom_call_target="tpu_custom_call" | custom-call | tf_op jit(solution)/shard_map/pallas_call | solution.py:449
  (65 shorter events, 19.0 us)
Async XLA Ops:
  2.3 6.5 %collective-permute-start = (bf16[2,128,128]{2,1,0:T(8,128)(2,1)S(1)}, bf16[2,128,128]{2,1,0:T(8,128)(2,1)S(1)}, u32[]{:S(2)}, u32[]{:S(2)}) collective-permute-start(bf16[2,128,128]{2,1,0:T(8,128)(2,1)S(1)} %get-tuple-element.50), channel_id=1, source_target_pairs={{0,24},{4,28},{8,16},{12,20},{16,8},{20,12},{24,0},{28,4},{1,25},{... | collective-permute-start | bytes 196616 | tf_op jit(solution)/shard_map/ppermute | solution.py:506
  6.2 4.3 %collective-permute-start.1 = (bf16[2,128,128]{2,1,0:T(8,128)(2,1)S(1)}, bf16[2,128,128]{2,1,0:T(8,128)(2,1)S(1)}, u32[]{:S(2)}, u32[]{:S(2)}) collective-permute-start(bf16[2,128,128]{2,1,0:T(8,128)(2,1)S(1)} %get-tuple-element.56), channel_id=1, source_target_pairs={{0,8},{4,12},{8,0},{12,4},{16,24},{20,28},{24,16},{28,20},{1,9},{5... | collective-permute-start | bytes 196616 | tf_op jit(solution)/shard_map/ppermute | solution.py:506
  6.8 4.3 %collective-permute-start.2 = (bf16[2,128,128]{2,1,0:T(8,128)(2,1)S(1)}, bf16[2,128,128]{2,1,0:T(8,128)(2,1)S(1)}, u32[]{:S(2)}, u32[]{:S(2)}) collective-permute-start(bf16[2,128,128]{2,1,0:T(8,128)(2,1)S(1)} %get-tuple-element.57), channel_id=1, source_target_pairs={{0,16},{4,20},{8,24},{12,28},{16,0},{20,4},{24,8},{28,12},{1,17},{... | collective-permute-start | bytes 196616 | tf_op jit(solution)/shard_map/ppermute | solution.py:506
  6.9 4.7 %collective-permute-start.3 = (bf16[2,128,128]{2,1,0:T(8,128)(2,1)S(1)}, bf16[2,128,128]{2,1,0:T(8,128)(2,1)S(1)}, u32[]{:S(2)}, u32[]{:S(2)}) collective-permute-start(bf16[2,128,128]{2,1,0:T(8,128)(2,1)S(1)} %get-tuple-element.55.refs_2_), channel_id=1, source_target_pairs={{0,4},{4,0},{8,12},{12,8},{16,20},{20,16},{24,28},{28,24},{1,5},{5... | collective-permute-start | bytes 196616 | tf_op jit(solution)/shard_map/ppermute | solution.py:513
  11.0 1.4 %collective-permute-start.6 = (bf16[2,128,128]{2,1,0:T(8,128)(2,1)S(1)}, bf16[2,128,128]{2,1,0:T(8,128)(2,1)S(1)}, u32[]{:S(2)}, u32[]{:S(2)}) collective-permute-start(bf16[2,128,128]{2,1,0:T(8,128)(2,1)S(1)} %collective-permute-done.refs_5_), channel_id=1, source_target_pairs={{0,4},{4,0},{8,12},{12,8},{16,20},{20,16},{24,28},{28,24},{1,5},{5... | collective-permute-start | bytes 196616 | tf_op jit(solution)/shard_map/ppermute | solution.py:513
  27.5 4.1 %collective-permute-start.9 = (bf16[16,1024]{1,0:T(8,128)(2,1)S(1)}, bf16[16,1024]{1,0:T(8,128)(2,1)S(1)}, u32[]{:S(2)}, u32[]{:S(2)}) collective-permute-start(bf16[16,1024]{1,0:T(8,128)(2,1)S(1)} %get-tuple-element.59.refs_0_), channel_id=1, source_target_pairs={{0,3},{1,0},{2,1},{3,2},{4,7},{5,4},{6,5},{7,6},{8,11},{9,8},{10,9... | collective-permute-start | bytes 98312 | tf_op jit(solution)/shard_map/ppermute | solution.py:543
  28.8 5.8 %collective-permute-start.8 = (bf16[16,1024]{1,0:T(8,128)(2,1)S(1)}, bf16[16,1024]{1,0:T(8,128)(2,1)S(1)}, u32[]{:S(2)}, u32[]{:S(2)}) collective-permute-start(bf16[16,1024]{1,0:T(8,128)(2,1)S(1)} %get-tuple-element.59.refs_0_), channel_id=1, source_target_pairs={{0,2},{1,3},{2,0},{3,1},{4,6},{5,7},{6,4},{7,5},{8,10},{9,11},{10,... | collective-permute-start | bytes 98312 | tf_op jit(solution)/shard_map/ppermute | solution.py:543
  28.8 5.8 %collective-permute-start.7 = (bf16[16,1024]{1,0:T(8,128)(2,1)S(1)}, bf16[16,1024]{1,0:T(8,128)(2,1)S(1)}, u32[]{:S(2)}, u32[]{:S(2)}) collective-permute-start(bf16[16,1024]{1,0:T(8,128)(2,1)S(1)} %get-tuple-element.59.refs_0_), channel_id=1, source_target_pairs={{0,1},{1,2},{2,3},{3,0},{4,5},{5,6},{6,7},{7,4},{8,9},{9,10},{10,1... | collective-permute-start | bytes 98312 | tf_op jit(solution)/shard_map/ppermute | solution.py:543
  34.9 5.3 %collective-permute-start.12 = (bf16[32,1024]{1,0:T(8,128)(2,1)S(1)}, bf16[32,1024]{1,0:T(8,128)(2,1)S(1)}, u32[]{:S(2)}, u32[]{:S(2)}) collective-permute-start(bf16[32,1024]{1,0:T(8,128)(2,1)S(1)} %shard_map.107.refs_1_), channel_id=1, source_target_pairs={{0,24},{4,28},{8,16},{12,20},{16,8},{20,12},{24,0},{28,4},{1,25},{... | collective-permute-start | bytes 196616 | tf_op jit(solution)/shard_map/ppermute | solution.py:506
  35.9 5.0 %collective-permute-start.11 = (bf16[32,1024]{1,0:T(8,128)(2,1)S(1)}, bf16[32,1024]{1,0:T(8,128)(2,1)S(1)}, u32[]{:S(2)}, u32[]{:S(2)}) collective-permute-start(bf16[32,1024]{1,0:T(8,128)(2,1)S(1)} %shard_map.107.refs_1_), channel_id=1, source_target_pairs={{0,16},{4,20},{8,24},{12,28},{16,0},{20,4},{24,8},{28,12},{1,17},{... | collective-permute-start | bytes 196616 | tf_op jit(solution)/shard_map/ppermute | solution.py:506
  37.3 4.3 %collective-permute-start.10 = (bf16[32,1024]{1,0:T(8,128)(2,1)S(1)}, bf16[32,1024]{1,0:T(8,128)(2,1)S(1)}, u32[]{:S(2)}, u32[]{:S(2)}) collective-permute-start(bf16[32,1024]{1,0:T(8,128)(2,1)S(1)} %shard_map.107.refs_1_), channel_id=1, source_target_pairs={{0,8},{4,12},{8,0},{12,4},{16,24},{20,28},{24,16},{28,20},{1,9},{5... | collective-permute-start | bytes 196616 | tf_op jit(solution)/shard_map/ppermute | solution.py:506
  38.5 3.1 %collective-permute-start.13 = (bf16[32,1024]{1,0:T(8,128)(2,1)S(1)}, bf16[32,1024]{1,0:T(8,128)(2,1)S(1)}, u32[]{:S(2)}, u32[]{:S(2)}) collective-permute-start(bf16[32,1024]{1,0:T(8,128)(2,1)S(1)} %shard_map.107.refs_1_), channel_id=1, source_target_pairs={{0,4},{4,0},{8,12},{12,8},{16,20},{20,16},{24,28},{28,24},{1,5},{5... | collective-permute-start | bytes 196616 | tf_op jit(solution)/shard_map/ppermute | solution.py:513
  43.7 6.0 %collective-permute-start.17 = (bf16[2,144,128]{2,1,0:T(8,128)(2,1)S(1)}, bf16[2,144,128]{2,1,0:T(8,128)(2,1)S(1)}, u32[]{:S(2)}, u32[]{:S(2)}) collective-permute-start(bf16[2,144,128]{2,1,0:T(8,128)(2,1)S(1)} %get-tuple-element.69), channel_id=1, source_target_pairs={{0,24},{4,28},{8,16},{12,20},{16,8},{20,12},{24,0},{28,4},{1,25},{... | collective-permute-start | bytes 221192 | tf_op jit(solution)/shard_map/ppermute | solution.py:506
  45.2 4.6 %collective-permute-start.18 = (bf16[2,144,128]{2,1,0:T(8,128)(2,1)S(1)}, bf16[2,144,128]{2,1,0:T(8,128)(2,1)S(1)}, u32[]{:S(2)}, u32[]{:S(2)}) collective-permute-start(bf16[2,144,128]{2,1,0:T(8,128)(2,1)S(1)} %get-tuple-element.79), channel_id=1, source_target_pairs={{0,8},{4,12},{8,0},{12,4},{16,24},{20,28},{24,16},{28,20},{1,9},{5... | collective-permute-start | bytes 221192 | tf_op jit(solution)/shard_map/ppermute | solution.py:506
  45.9 4.7 %collective-permute-start.19 = (bf16[2,144,128]{2,1,0:T(8,128)(2,1)S(1)}, bf16[2,144,128]{2,1,0:T(8,128)(2,1)S(1)}, u32[]{:S(2)}, u32[]{:S(2)}) collective-permute-start(bf16[2,144,128]{2,1,0:T(8,128)(2,1)S(1)} %get-tuple-element.80), channel_id=1, source_target_pairs={{0,16},{4,20},{8,24},{12,28},{16,0},{20,4},{24,8},{28,12},{1,17},{... | collective-permute-start | bytes 221192 | tf_op jit(solution)/shard_map/ppermute | solution.py:506
  47.2 3.8 %collective-permute-start.20 = (bf16[2,144,128]{2,1,0:T(8,128)(2,1)S(1)}, bf16[2,144,128]{2,1,0:T(8,128)(2,1)S(1)}, u32[]{:S(2)}, u32[]{:S(2)}) collective-permute-start(bf16[2,144,128]{2,1,0:T(8,128)(2,1)S(1)} %get-tuple-element.78.refs_2_), channel_id=1, source_target_pairs={{0,4},{4,0},{8,12},{12,8},{16,20},{20,16},{24,28},{28,24},{1,5},{5... | collective-permute-start | bytes 221192 | tf_op jit(solution)/shard_map/ppermute | solution.py:513
  50.6 1.4 %collective-permute-start.23 = (bf16[2,144,128]{2,1,0:T(8,128)(2,1)S(1)}, bf16[2,144,128]{2,1,0:T(8,128)(2,1)S(1)}, u32[]{:S(2)}, u32[]{:S(2)}) collective-permute-start(bf16[2,144,128]{2,1,0:T(8,128)(2,1)S(1)} %collective-permute-done.17.refs_5_), channel_id=1, source_target_pairs={{0,4},{4,0},{8,12},{12,8},{16,20},{20,16},{24,28},{28,24},{1,5},{5... | collective-permute-start | bytes 221192 | tf_op jit(solution)/shard_map/ppermute | solution.py:513
  64.7 6.4 %collective-permute-start.26 = (bf16[16,1152]{1,0:T(8,128)(2,1)S(1)}, bf16[16,1152]{1,0:T(8,128)(2,1)S(1)}, u32[]{:S(2)}, u32[]{:S(2)}) collective-permute-start(bf16[16,1152]{1,0:T(8,128)(2,1)S(1)} %get-tuple-element.84.refs_0_), channel_id=1, source_target_pairs={{0,3},{1,0},{2,1},{3,2},{4,7},{5,4},{6,5},{7,6},{8,11},{9,8},{10,9... | collective-permute-start | bytes 110600 | tf_op jit(solution)/shard_map/ppermute | solution.py:543
  66.0 6.0 %collective-permute-start.25 = (bf16[16,1152]{1,0:T(8,128)(2,1)S(1)}, bf16[16,1152]{1,0:T(8,128)(2,1)S(1)}, u32[]{:S(2)}, u32[]{:S(2)}) collective-permute-start(bf16[16,1152]{1,0:T(8,128)(2,1)S(1)} %get-tuple-element.84.refs_0_), channel_id=1, source_target_pairs={{0,2},{1,3},{2,0},{3,1},{4,6},{5,7},{6,4},{7,5},{8,10},{9,11},{10,... | collective-permute-start | bytes 110600 | tf_op jit(solution)/shard_map/ppermute | solution.py:543
  66.0 6.0 %collective-permute-start.24 = (bf16[16,1152]{1,0:T(8,128)(2,1)S(1)}, bf16[16,1152]{1,0:T(8,128)(2,1)S(1)}, u32[]{:S(2)}, u32[]{:S(2)}) collective-permute-start(bf16[16,1152]{1,0:T(8,128)(2,1)S(1)} %get-tuple-element.84.refs_0_), channel_id=1, source_target_pairs={{0,1},{1,2},{2,3},{3,0},{4,5},{5,6},{6,7},{7,4},{8,9},{9,10},{10,1... | collective-permute-start | bytes 110600 | tf_op jit(solution)/shard_map/ppermute | solution.py:543
  72.3 5.4 %collective-permute-start.29 = (bf16[32,1152]{1,0:T(8,128)(2,1)S(1)}, bf16[32,1152]{1,0:T(8,128)(2,1)S(1)}, u32[]{:S(2)}, u32[]{:S(2)}) collective-permute-start(bf16[32,1152]{1,0:T(8,128)(2,1)S(1)} %shard_map.113.refs_1_), channel_id=1, source_target_pairs={{0,24},{4,28},{8,16},{12,20},{16,8},{20,12},{24,0},{28,4},{1,25},{... | collective-permute-start | bytes 221192 | tf_op jit(solution)/shard_map/ppermute | solution.py:506
  73.2 5.1 %collective-permute-start.28 = (bf16[32,1152]{1,0:T(8,128)(2,1)S(1)}, bf16[32,1152]{1,0:T(8,128)(2,1)S(1)}, u32[]{:S(2)}, u32[]{:S(2)}) collective-permute-start(bf16[32,1152]{1,0:T(8,128)(2,1)S(1)} %shard_map.113.refs_1_), channel_id=1, source_target_pairs={{0,16},{4,20},{8,24},{12,28},{16,0},{20,4},{24,8},{28,12},{1,17},{... | collective-permute-start | bytes 221192 | tf_op jit(solution)/shard_map/ppermute | solution.py:506
  74.7 4.4 %collective-permute-start.27 = (bf16[32,1152]{1,0:T(8,128)(2,1)S(1)}, bf16[32,1152]{1,0:T(8,128)(2,1)S(1)}, u32[]{:S(2)}, u32[]{:S(2)}) collective-permute-start(bf16[32,1152]{1,0:T(8,128)(2,1)S(1)} %shard_map.113.refs_1_), channel_id=1, source_target_pairs={{0,8},{4,12},{8,0},{12,4},{16,24},{20,28},{24,16},{28,20},{1,9},{5... | collective-permute-start | bytes 221192 | tf_op jit(solution)/shard_map/ppermute | solution.py:506
  75.9 3.1 %collective-permute-start.30 = (bf16[32,1152]{1,0:T(8,128)(2,1)S(1)}, bf16[32,1152]{1,0:T(8,128)(2,1)S(1)}, u32[]{:S(2)}, u32[]{:S(2)}) collective-permute-start(bf16[32,1152]{1,0:T(8,128)(2,1)S(1)} %shard_map.113.refs_1_), channel_id=1, source_target_pairs={{0,4},{4,0},{8,12},{12,8},{16,20},{20,16},{24,28},{28,24},{1,5},{5... | collective-permute-start | bytes 221192 | tf_op jit(solution)/shard_map/ppermute | solution.py:513
  (13 other events, 67.6 us)
